TPU v7x, 32 devices: a whole 2x2x4 slice. The times are simulated.
32 devices in a mesh: dp: 4 (over z), fsdp: 8 (over y, x, core).
Axes of the slice: x: 2, y: 2, z: 4, core: 2. Of those that a mesh axis runs over, the one named last changes fastest.
Arguments:
- tokens: bfloat16 [32, 512, 1024], P(('dp', 'fsdp')), may hold values from -6 to 6
- memory: bfloat16 [32, 588, 1024], P(('dp', 'fsdp')), may hold values from -6 to 6
- page_lengths: int32 [32], P(('dp', 'fsdp')), may hold values from 256 to 512, as said below
- end_flags: int32 [32], P(('dp', 'fsdp')), may hold values from 0 to 1, as said below
- out_grad: bfloat16 [32, 512, 1024], P(('dp', 'fsdp')), may hold values from -6 to 6
- self_gain: bfloat16 [1024], P(('dp', 'fsdp')), may hold values from 0.25 to 1.75
- self_shift: bfloat16 [1024], P(('dp', 'fsdp')), may hold values from -1.25 to 1.25
- self_query: bfloat16 [1024, 1024], P(('dp', 'fsdp')), may hold values from -0.1875 to 0.1875
- self_query_bias: bfloat16 [1024], P(('dp', 'fsdp')), may hold values from -1.25 to 1.25
- self_key: bfloat16 [1024, 1024], P(('dp', 'fsdp')), may hold values from -0.1875 to 0.1875
- self_value: bfloat16 [1024, 1024], P(('dp', 'fsdp')), may hold values from -0.1875 to 0.1875
- self_value_bias: bfloat16 [1024], P(('dp', 'fsdp')), may hold values from -1.25 to 1.25
- self_out: bfloat16 [1024, 1024], P(('dp', 'fsdp')), may hold values from -1.5 to 1.5
- self_out_bias: bfloat16 [1024], P(('dp', 'fsdp')), may hold values from -1.25 to 1.25
- cross_gain: bfloat16 [1024], P(('dp', 'fsdp')), may hold values from 0.25 to 1.75
- cross_shift: bfloat16 [1024], P(('dp', 'fsdp')), may hold values from -1.25 to 1.25
- cross_query: bfloat16 [1024, 1024], P(('dp', 'fsdp')), may hold values from -0.1875 to 0.1875
- cross_query_bias: bfloat16 [1024], P(('dp', 'fsdp')), may hold values from -1.25 to 1.25
- cross_key: bfloat16 [1024, 1024], P(('dp', 'fsdp')), may hold values from -0.1875 to 0.1875
- cross_value: bfloat16 [1024, 1024], P(('dp', 'fsdp')), may hold values from -0.1875 to 0.1875
- cross_value_bias: bfloat16 [1024], P(('dp', 'fsdp')), may hold values from -1.25 to 1.25
- cross_out: bfloat16 [1024, 1024], P(('dp', 'fsdp')), may hold values from -1.5 to 1.5
- cross_out_bias: bfloat16 [1024], P(('dp', 'fsdp')), may hold values from -1.25 to 1.25
- feed_gain: bfloat16 [1024], P(('dp', 'fsdp')), may hold values from 0.25 to 1.75
- feed_shift: bfloat16 [1024], P(('dp', 'fsdp')), may hold values from -1.25 to 1.25
- feed_in: bfloat16 [1024, 4096], P(('dp', 'fsdp')), may hold values from -0.1875 to 0.1875
- feed_in_bias: bfloat16 [4096], P(('dp', 'fsdp')), may hold values from -1.25 to 1.25
- feed_out: bfloat16 [4096, 1024], P(('dp', 'fsdp')), may hold values from -0.09375 to 0.09375
- feed_out_bias: bfloat16 [1024], P(('dp', 'fsdp')), may hold values from -1.25 to 1.25
Outputs:
- layer_out: bfloat16 [32, 512, 1024], P(('dp', 'fsdp'))
- tokens_grad: float32 [32, 512, 1024], P(('dp', 'fsdp'))
- memory_grad: float32 [32, 588, 1024], P(('dp', 'fsdp'))
- grad_self_gain: float32 [1024], P(('dp', 'fsdp'))
- grad_self_shift: float32 [1024], P(('dp', 'fsdp'))
- grad_self_query: float32 [1024, 1024], P(('dp', 'fsdp'))
- grad_self_query_bias: float32 [1024], P(('dp', 'fsdp'))
- grad_self_key: float32 [1024, 1024], P(('dp', 'fsdp'))
- grad_self_value: float32 [1024, 1024], P(('dp', 'fsdp'))
- grad_self_value_bias: float32 [1024], P(('dp', 'fsdp'))
- grad_self_out: float32 [1024, 1024], P(('dp', 'fsdp'))
- grad_self_out_bias: float32 [1024], P(('dp', 'fsdp'))
- grad_cross_gain: float32 [1024], P(('dp', 'fsdp'))
- grad_cross_shift: float32 [1024], P(('dp', 'fsdp'))
- grad_cross_query: float32 [1024, 1024], P(('dp', 'fsdp'))
- grad_cross_query_bias: float32 [1024], P(('dp', 'fsdp'))
- grad_cross_key: float32 [1024, 1024], P(('dp', 'fsdp'))
- grad_cross_value: float32 [1024, 1024], P(('dp', 'fsdp'))
- grad_cross_value_bias: float32 [1024], P(('dp', 'fsdp'))
- grad_cross_out: float32 [1024, 1024], P(('dp', 'fsdp'))
- grad_cross_out_bias: float32 [1024], P(('dp', 'fsdp'))
- grad_feed_gain: float32 [1024], P(('dp', 'fsdp'))
- grad_feed_shift: float32 [1024], P(('dp', 'fsdp'))
- grad_feed_in: float32 [1024, 4096], P(('dp', 'fsdp'))
- grad_feed_in_bias: float32 [4096], P(('dp', 'fsdp'))
- grad_feed_out: float32 [4096, 1024], P(('dp', 'fsdp'))
- grad_feed_out_bias: float32 [1024], P(('dp', 'fsdp'))
Inputs may be any that keep to these rules, and one draw needn't show every extreme that they name: `page_lengths`: lengths lie from 256 to 512; some page that is not an end page has exactly 512. `end_flags`: an end page's entry of page_lengths is not used; some page is an end page.
All inputs are finite; a program needn't handle non-finite values.
Results may differ from a plain program's by a relative error of at most 0.02.
Values may be sent and summed in bfloat16 or wider, within the bound.
A program may use at most 256 MiB of HBM per device.

v0:
```python
import jax
import jax.numpy as jnp
from jax import lax
from jax.sharding import PartitionSpec as P

HEADS = 16


EPSILON = 1e-05
MASKED = -1000000000.0
ROOT_HALF = 0.7071067811865476
INV_ROOT_TWO_PI = 0.3989422804014327


def product(left, right):
    return jnp.dot(left, right, preferred_element_type=jnp.float32)


def product_tn(left, right):
    return lax.dot_general(
        left, right, (((0,), (0,)), ((), ())), preferred_element_type=jnp.float32
    )


def product_nt(left, right):
    return lax.dot_general(
        left, right, (((1,), (1,)), ((), ())), preferred_element_type=jnp.float32
    )


def normalize(rows_in, norm_gain, norm_shift):
    centered = rows_in - jnp.mean(rows_in, axis=-1, keepdims=True)
    inv_std = lax.rsqrt(jnp.mean(centered * centered, axis=-1, keepdims=True) + EPSILON)
    unit_rows = centered * inv_std
    return (unit_rows * norm_gain + norm_shift, unit_rows, inv_std)


def normalize_back(grad_norm, unit_rows, inv_std, norm_gain):
    scaled = grad_norm * norm_gain
    inner_part = (
        scaled
        - jnp.mean(scaled, axis=-1, keepdims=True)
        - unit_rows * jnp.mean(scaled * unit_rows, axis=-1, keepdims=True)
    )
    return (
        inner_part * inv_std,
        jnp.sum(grad_norm * unit_rows, axis=0),
        jnp.sum(grad_norm, axis=0),
    )


def gelu_slope(pre_act):
    return 0.5 * (
        1.0 + jax.scipy.special.erf(pre_act * ROOT_HALF)
    ) + pre_act * INV_ROOT_TWO_PI * jnp.exp(-0.5 * pre_act * pre_act)


def page_mask(length_now, row_count):
    query_pos = lax.broadcasted_iota(jnp.int32, (row_count, row_count), 0)
    key_pos = lax.broadcasted_iota(jnp.int32, (row_count, row_count), 1)
    return (key_pos <= query_pos) & (key_pos < length_now)


def split_heads(rows_in):
    return rows_in.reshape(rows_in.shape[0], HEADS, rows_in.shape[1] // HEADS)


def merge_heads(heads_in):
    return heads_in.reshape(heads_in.shape[0], heads_in.shape[1] * heads_in.shape[2])


def scores_of(query_rows, key_rows, mask_now):
    head_size = query_rows.shape[1] // HEADS
    raw_scores = jnp.einsum(
        "qhe,khe->hqk",
        split_heads(query_rows),
        split_heads(key_rows),
        preferred_element_type=jnp.float32,
    )
    scaled = raw_scores * head_size ** (-0.5)
    if mask_now is None:
        return scaled
    return jnp.where(mask_now[None], scaled, MASKED)


def attend_forward(query_rows, key_rows, value_rows, mask_now):
    scaled = scores_of(query_rows, key_rows, mask_now)
    row_top = jnp.max(scaled, axis=-1, keepdims=True)
    expo_rows = jnp.exp(scaled - row_top)
    row_total = jnp.sum(expo_rows, axis=-1, keepdims=True)
    weights_low = (expo_rows / row_total).astype(jnp.bfloat16)
    mixed = jnp.einsum(
        "hqk,khe->qhe", weights_low, split_heads(value_rows), preferred_element_type=jnp.float32
    )
    return (merge_heads(mixed), row_top + jnp.log(row_total))


def attend_backward(query_rows, key_rows, value_rows, mixed_grad, log_total, mask_now):
    head_size = query_rows.shape[1] // HEADS
    probs = jnp.exp(scores_of(query_rows, key_rows, mask_now) - log_total)
    grad_heads = split_heads(mixed_grad)
    query_heads = split_heads(query_rows)
    key_heads = split_heads(key_rows)
    prob_grad = jnp.einsum(
        "qhe,khe->hqk", grad_heads, split_heads(value_rows), preferred_element_type=jnp.float32
    )
    value_grad = jnp.einsum(
        "hqk,qhe->khe", probs.astype(jnp.bfloat16), grad_heads, preferred_element_type=jnp.float32
    )
    row_dot = jnp.sum(probs * prob_grad, axis=-1, keepdims=True)
    score_grad = (probs * (prob_grad - row_dot) * head_size ** (-0.5)).astype(jnp.bfloat16)
    query_grad = jnp.einsum(
        "hqk,khe->qhe", score_grad, key_heads, preferred_element_type=jnp.float32
    )
    key_grad = jnp.einsum(
        "hqk,qhe->khe", score_grad, query_heads, preferred_element_type=jnp.float32
    )
    return (merge_heads(query_grad), merge_heads(key_grad), merge_heads(value_grad))


def self_forward(query_pages, key_pages, value_pages, lengths_now):

    def one_page(page_item):
        mask_now = page_mask(page_item[3], page_item[0].shape[0])
        return attend_forward(page_item[0], page_item[1], page_item[2], mask_now)

    return lax.map(one_page, (query_pages, key_pages, value_pages, lengths_now))


def self_backward(query_pages, key_pages, value_pages, grad_pages, total_pages, lengths_now):

    def one_page(page_item):
        mask_now = page_mask(page_item[5], page_item[0].shape[0])
        return attend_backward(
            page_item[0], page_item[1], page_item[2], page_item[3], page_item[4], mask_now
        )

    return lax.map(
        one_page, (query_pages, key_pages, value_pages, grad_pages, total_pages, lengths_now)
    )


def cross_forward(query_pages, key_pages, value_pages):

    def one_page(page_item):
        return attend_forward(page_item[0], page_item[1], page_item[2], None)

    return lax.map(one_page, (query_pages, key_pages, value_pages))


def cross_backward(query_pages, key_pages, value_pages, grad_pages, total_pages):

    def one_page(page_item):
        return attend_backward(
            page_item[0], page_item[1], page_item[2], page_item[3], page_item[4], None
        )

    return lax.map(one_page, (query_pages, key_pages, value_pages, grad_pages, total_pages))


def collect(
    self_gain,
    self_shift,
    self_query,
    self_query_bias,
    self_key,
    self_value,
    self_value_bias,
    self_out,
    self_out_bias,
    cross_gain,
    cross_shift,
    cross_query,
    cross_query_bias,
    cross_key,
    cross_value,
    cross_value_bias,
    cross_out,
    cross_out_bias,
    feed_gain,
    feed_shift,
    feed_in,
    feed_in_bias,
    feed_out,
    feed_out_bias,
):
    return (
        lax.all_gather(self_gain, ("dp", "fsdp"), axis=0, tiled=True),
        lax.all_gather(self_shift, ("dp", "fsdp"), axis=0, tiled=True),
        lax.all_gather(self_query, ("dp", "fsdp"), axis=0, tiled=True),
        lax.all_gather(self_query_bias, ("dp", "fsdp"), axis=0, tiled=True),
        lax.all_gather(self_key, ("dp", "fsdp"), axis=0, tiled=True),
        lax.all_gather(self_value, ("dp", "fsdp"), axis=0, tiled=True),
        lax.all_gather(self_value_bias, ("dp", "fsdp"), axis=0, tiled=True),
        lax.all_gather(self_out, ("dp", "fsdp"), axis=0, tiled=True),
        lax.all_gather(self_out_bias, ("dp", "fsdp"), axis=0, tiled=True),
        lax.all_gather(cross_gain, ("dp", "fsdp"), axis=0, tiled=True),
        lax.all_gather(cross_shift, ("dp", "fsdp"), axis=0, tiled=True),
        lax.all_gather(cross_query, ("dp", "fsdp"), axis=0, tiled=True),
        lax.all_gather(cross_query_bias, ("dp", "fsdp"), axis=0, tiled=True),
        lax.all_gather(cross_key, ("dp", "fsdp"), axis=0, tiled=True),
        lax.all_gather(cross_value, ("dp", "fsdp"), axis=0, tiled=True),
        lax.all_gather(cross_value_bias, ("dp", "fsdp"), axis=0, tiled=True),
        lax.all_gather(cross_out, ("dp", "fsdp"), axis=0, tiled=True),
        lax.all_gather(cross_out_bias, ("dp", "fsdp"), axis=0, tiled=True),
        lax.all_gather(feed_gain, ("dp", "fsdp"), axis=0, tiled=True),
        lax.all_gather(feed_shift, ("dp", "fsdp"), axis=0, tiled=True),
        lax.all_gather(feed_in, ("dp", "fsdp"), axis=0, tiled=True),
        lax.all_gather(feed_in_bias, ("dp", "fsdp"), axis=0, tiled=True),
        lax.all_gather(feed_out, ("dp", "fsdp"), axis=0, tiled=True),
        lax.all_gather(feed_out_bias, ("dp", "fsdp"), axis=0, tiled=True),
    )


def spread(
    grad_gain_one,
    grad_shift_one,
    grad_query_mat,
    grad_query_vec,
    grad_key_mat,
    grad_value_mat,
    grad_value_vec,
    grad_out_mat,
    grad_out_vec,
    grad_gain_two,
    grad_shift_two,
    grad_cquery_mat,
    grad_cquery_vec,
    grad_ckey_mat,
    grad_cvalue_mat,
    grad_cvalue_vec,
    grad_cout_mat,
    grad_cout_vec,
    grad_gain_three,
    grad_shift_three,
    grad_hidden_mat,
    grad_hidden_vec,
    grad_final_mat,
    grad_final_vec,
):
    return (
        lax.psum_scatter(grad_gain_one, ("dp", "fsdp"), scatter_dimension=0, tiled=True),
        lax.psum_scatter(grad_shift_one, ("dp", "fsdp"), scatter_dimension=0, tiled=True),
        lax.psum_scatter(grad_query_mat, ("dp", "fsdp"), scatter_dimension=0, tiled=True),
        lax.psum_scatter(grad_query_vec, ("dp", "fsdp"), scatter_dimension=0, tiled=True),
        lax.psum_scatter(grad_key_mat, ("dp", "fsdp"), scatter_dimension=0, tiled=True),
        lax.psum_scatter(grad_value_mat, ("dp", "fsdp"), scatter_dimension=0, tiled=True),
        lax.psum_scatter(grad_value_vec, ("dp", "fsdp"), scatter_dimension=0, tiled=True),
        lax.psum_scatter(grad_out_mat, ("dp", "fsdp"), scatter_dimension=0, tiled=True),
        lax.psum_scatter(grad_out_vec, ("dp", "fsdp"), scatter_dimension=0, tiled=True),
        lax.psum_scatter(grad_gain_two, ("dp", "fsdp"), scatter_dimension=0, tiled=True),
        lax.psum_scatter(grad_shift_two, ("dp", "fsdp"), scatter_dimension=0, tiled=True),
        lax.psum_scatter(grad_cquery_mat, ("dp", "fsdp"), scatter_dimension=0, tiled=True),
        lax.psum_scatter(grad_cquery_vec, ("dp", "fsdp"), scatter_dimension=0, tiled=True),
        lax.psum_scatter(grad_ckey_mat, ("dp", "fsdp"), scatter_dimension=0, tiled=True),
        lax.psum_scatter(grad_cvalue_mat, ("dp", "fsdp"), scatter_dimension=0, tiled=True),
        lax.psum_scatter(grad_cvalue_vec, ("dp", "fsdp"), scatter_dimension=0, tiled=True),
        lax.psum_scatter(grad_cout_mat, ("dp", "fsdp"), scatter_dimension=0, tiled=True),
        lax.psum_scatter(grad_cout_vec, ("dp", "fsdp"), scatter_dimension=0, tiled=True),
        lax.psum_scatter(grad_gain_three, ("dp", "fsdp"), scatter_dimension=0, tiled=True),
        lax.psum_scatter(grad_shift_three, ("dp", "fsdp"), scatter_dimension=0, tiled=True),
        lax.psum_scatter(grad_hidden_mat, ("dp", "fsdp"), scatter_dimension=0, tiled=True),
        lax.psum_scatter(grad_hidden_vec, ("dp", "fsdp"), scatter_dimension=0, tiled=True),
        lax.psum_scatter(grad_final_mat, ("dp", "fsdp"), scatter_dimension=0, tiled=True),
        lax.psum_scatter(grad_final_vec, ("dp", "fsdp"), scatter_dimension=0, tiled=True),
    )


def on_device(
    tokens,
    memory,
    page_lengths,
    end_flags,
    out_grad,
    self_gain,
    self_shift,
    self_query,
    self_query_bias,
    self_key,
    self_value,
    self_value_bias,
    self_out,
    self_out_bias,
    cross_gain,
    cross_shift,
    cross_query,
    cross_query_bias,
    cross_key,
    cross_value,
    cross_value_bias,
    cross_out,
    cross_out_bias,
    feed_gain,
    feed_shift,
    feed_in,
    feed_in_bias,
    feed_out,
    feed_out_bias,
):
    page_count, page_len, width = tokens.shape
    mem_len = memory.shape[1]
    row_count = page_count * page_len
    lengths_now = jnp.where(end_flags == 1, 1, page_lengths)
    inputs = tokens.reshape(row_count, width).astype(jnp.float32)
    mem_rows = memory.reshape(page_count * mem_len, width)
    full_set = collect(
        self_gain,
        self_shift,
        self_query,
        self_query_bias,
        self_key,
        self_value,
        self_value_bias,
        self_out,
        self_out_bias,
        cross_gain,
        cross_shift,
        cross_query,
        cross_query_bias,
        cross_key,
        cross_value,
        cross_value_bias,
        cross_out,
        cross_out_bias,
        feed_gain,
        feed_shift,
        feed_in,
        feed_in_bias,
        feed_out,
        feed_out_bias,
    )
    (
        gain_one,
        shift_one,
        query_mat,
        query_vec,
        key_mat,
        value_mat,
        value_vec,
        out_mat,
        out_vec,
        gain_two,
        shift_two,
        cquery_mat,
        cquery_vec,
        ckey_mat,
        cvalue_mat,
        cvalue_vec,
        cout_mat,
        cout_vec,
        gain_three,
        shift_three,
        hidden_mat,
        hidden_vec,
        final_mat,
        final_vec,
    ) = full_set
    first_norm, first_unit, first_std = normalize(
        inputs, gain_one.astype(jnp.float32), shift_one.astype(jnp.float32)
    )
    first_low = first_norm.astype(jnp.bfloat16)
    query_low = (product(first_low, query_mat) + query_vec.astype(jnp.float32)).astype(jnp.bfloat16)
    key_low = product(first_low, key_mat).astype(jnp.bfloat16)
    value_low = (product(first_low, value_mat) + value_vec.astype(jnp.float32)).astype(jnp.bfloat16)
    query_pages = query_low.reshape(page_count, page_len, width)
    key_pages = key_low.reshape(page_count, page_len, width)
    value_pages = value_low.reshape(page_count, page_len, width)
    self_mixed, self_total = self_forward(query_pages, key_pages, value_pages, lengths_now)
    self_low = self_mixed.reshape(row_count, width).astype(jnp.bfloat16)
    after_self = inputs + product(self_low, out_mat) + out_vec.astype(jnp.float32)
    second_norm, second_unit, second_std = normalize(
        after_self, gain_two.astype(jnp.float32), shift_two.astype(jnp.float32)
    )
    second_low = second_norm.astype(jnp.bfloat16)
    cquery_low = (product(second_low, cquery_mat) + cquery_vec.astype(jnp.float32)).astype(
        jnp.bfloat16
    )
    ckey_low = product(mem_rows, ckey_mat).astype(jnp.bfloat16)
    cvalue_low = (product(mem_rows, cvalue_mat) + cvalue_vec.astype(jnp.float32)).astype(
        jnp.bfloat16
    )
    cquery_pages = cquery_low.reshape(page_count, page_len, width)
    ckey_pages = ckey_low.reshape(page_count, mem_len, width)
    cvalue_pages = cvalue_low.reshape(page_count, mem_len, width)
    cross_mixed, cross_total = cross_forward(cquery_pages, ckey_pages, cvalue_pages)
    cross_low = cross_mixed.reshape(row_count, width).astype(jnp.bfloat16)
    after_cross = after_self + product(cross_low, cout_mat) + cout_vec.astype(jnp.float32)
    third_norm, third_unit, third_std = normalize(
        after_cross, gain_three.astype(jnp.float32), shift_three.astype(jnp.float32)
    )
    third_low = third_norm.astype(jnp.bfloat16)
    hidden_pre = product(third_low, hidden_mat) + hidden_vec.astype(jnp.float32)
    hidden_low = jax.nn.gelu(hidden_pre, approximate=False).astype(jnp.bfloat16)
    result = after_cross + product(hidden_low, final_mat) + final_vec.astype(jnp.float32)
    layer_out = result.astype(jnp.bfloat16).reshape(page_count, page_len, width)
    back_set = collect(
        self_gain,
        self_shift,
        self_query,
        self_query_bias,
        self_key,
        self_value,
        self_value_bias,
        self_out,
        self_out_bias,
        cross_gain,
        cross_shift,
        cross_query,
        cross_query_bias,
        cross_key,
        cross_value,
        cross_value_bias,
        cross_out,
        cross_out_bias,
        feed_gain,
        feed_shift,
        feed_in,
        feed_in_bias,
        feed_out,
        feed_out_bias,
    )
    (
        gain_one,
        shift_one,
        query_mat,
        query_vec,
        key_mat,
        value_mat,
        value_vec,
        out_mat,
        out_vec,
        gain_two,
        shift_two,
        cquery_mat,
        cquery_vec,
        ckey_mat,
        cvalue_mat,
        cvalue_vec,
        cout_mat,
        cout_vec,
        gain_three,
        shift_three,
        hidden_mat,
        hidden_vec,
        final_mat,
        final_vec,
    ) = back_set
    grad_rows = out_grad.reshape(row_count, width).astype(jnp.float32)
    final_grad = out_grad.reshape(row_count, width)
    grad_final_mat = product_tn(hidden_low, final_grad)
    grad_final_vec = jnp.sum(final_grad.astype(jnp.float32), axis=0)
    hidden_grad = (product_nt(final_grad, final_mat) * gelu_slope(hidden_pre)).astype(jnp.bfloat16)
    grad_hidden_mat = product_tn(third_low, hidden_grad)
    grad_hidden_vec = jnp.sum(hidden_grad.astype(jnp.float32), axis=0)
    third_back, grad_gain_three, grad_shift_three = normalize_back(
        product_nt(hidden_grad, hidden_mat), third_unit, third_std, gain_three.astype(jnp.float32)
    )
    cross_grad_total = grad_rows + third_back
    cout_grad = cross_grad_total.astype(jnp.bfloat16)
    grad_cout_mat = product_tn(cross_low, cout_grad)
    grad_cout_vec = jnp.sum(cout_grad.astype(jnp.float32), axis=0)
    cmix_grad = (
        product_nt(cout_grad, cout_mat).astype(jnp.bfloat16).reshape(page_count, page_len, width)
    )
    cquery_grad, ckey_grad, cvalue_grad = cross_backward(
        cquery_pages, ckey_pages, cvalue_pages, cmix_grad, cross_total
    )
    cquery_grad = cquery_grad.reshape(row_count, width).astype(jnp.bfloat16)
    ckey_grad = ckey_grad.reshape(page_count * mem_len, width).astype(jnp.bfloat16)
    cvalue_grad = cvalue_grad.reshape(page_count * mem_len, width).astype(jnp.bfloat16)
    grad_cquery_mat = product_tn(second_low, cquery_grad)
    grad_cquery_vec = jnp.sum(cquery_grad.astype(jnp.float32), axis=0)
    grad_ckey_mat = product_tn(mem_rows, ckey_grad)
    grad_cvalue_mat = product_tn(mem_rows, cvalue_grad)
    grad_cvalue_vec = jnp.sum(cvalue_grad.astype(jnp.float32), axis=0)
    memory_grad = (product_nt(ckey_grad, ckey_mat) + product_nt(cvalue_grad, cvalue_mat)).reshape(
        page_count, mem_len, width
    )
    second_back, grad_gain_two, grad_shift_two = normalize_back(
        product_nt(cquery_grad, cquery_mat), second_unit, second_std, gain_two.astype(jnp.float32)
    )
    self_grad_total = cross_grad_total + second_back
    sout_grad = self_grad_total.astype(jnp.bfloat16)
    grad_out_mat = product_tn(self_low, sout_grad)
    grad_out_vec = jnp.sum(sout_grad.astype(jnp.float32), axis=0)
    smix_grad = (
        product_nt(sout_grad, out_mat).astype(jnp.bfloat16).reshape(page_count, page_len, width)
    )
    query_grad, key_grad, value_grad = self_backward(
        query_pages, key_pages, value_pages, smix_grad, self_total, lengths_now
    )
    query_grad = query_grad.reshape(row_count, width).astype(jnp.bfloat16)
    key_grad = key_grad.reshape(row_count, width).astype(jnp.bfloat16)
    value_grad = value_grad.reshape(row_count, width).astype(jnp.bfloat16)
    grad_query_mat = product_tn(first_low, query_grad)
    grad_query_vec = jnp.sum(query_grad.astype(jnp.float32), axis=0)
    grad_key_mat = product_tn(first_low, key_grad)
    grad_value_mat = product_tn(first_low, value_grad)
    grad_value_vec = jnp.sum(value_grad.astype(jnp.float32), axis=0)
    first_in = (
        product_nt(query_grad, query_mat)
        + product_nt(key_grad, key_mat)
        + product_nt(value_grad, value_mat)
    )
    first_back, grad_gain_one, grad_shift_one = normalize_back(
        first_in, first_unit, first_std, gain_one.astype(jnp.float32)
    )
    tokens_grad = (self_grad_total + first_back).reshape(page_count, page_len, width)
    owned = spread(
        grad_gain_one,
        grad_shift_one,
        grad_query_mat,
        grad_query_vec,
        grad_key_mat,
        grad_value_mat,
        grad_value_vec,
        grad_out_mat,
        grad_out_vec,
        grad_gain_two,
        grad_shift_two,
        grad_cquery_mat,
        grad_cquery_vec,
        grad_ckey_mat,
        grad_cvalue_mat,
        grad_cvalue_vec,
        grad_cout_mat,
        grad_cout_vec,
        grad_gain_three,
        grad_shift_three,
        grad_hidden_mat,
        grad_hidden_vec,
        grad_final_mat,
        grad_final_vec,
    )
    return (layer_out, tokens_grad, memory_grad) + tuple(owned)


def solution(mesh):
    placed = (
        P(("dp", "fsdp"), None, None),
        P(("dp", "fsdp"), None, None),
        P(("dp", "fsdp")),
        P(("dp", "fsdp")),
        P(("dp", "fsdp"), None, None),
        P(("dp", "fsdp")),
        P(("dp", "fsdp")),
        P(("dp", "fsdp"), None),
        P(("dp", "fsdp")),
        P(("dp", "fsdp"), None),
        P(("dp", "fsdp"), None),
        P(("dp", "fsdp")),
        P(("dp", "fsdp"), None),
        P(("dp", "fsdp")),
        P(("dp", "fsdp")),
        P(("dp", "fsdp")),
        P(("dp", "fsdp"), None),
        P(("dp", "fsdp")),
        P(("dp", "fsdp"), None),
        P(("dp", "fsdp"), None),
        P(("dp", "fsdp")),
        P(("dp", "fsdp"), None),
        P(("dp", "fsdp")),
        P(("dp", "fsdp")),
        P(("dp", "fsdp")),
        P(("dp", "fsdp"), None),
        P(("dp", "fsdp")),
        P(("dp", "fsdp"), None),
        P(("dp", "fsdp")),
    )
    return jax.shard_map(
        on_device,
        mesh=mesh,
        in_specs=placed,
        out_specs=(
            P(("dp", "fsdp"), None, None),
            P(("dp", "fsdp"), None, None),
            P(("dp", "fsdp"), None, None),
            P(("dp", "fsdp")),
            P(("dp", "fsdp")),
            P(("dp", "fsdp"), None),
            P(("dp", "fsdp")),
            P(("dp", "fsdp"), None),
            P(("dp", "fsdp"), None),
            P(("dp", "fsdp")),
            P(("dp", "fsdp"), None),
            P(("dp", "fsdp")),
            P(("dp", "fsdp")),
            P(("dp", "fsdp")),
            P(("dp", "fsdp"), None),
            P(("dp", "fsdp")),
            P(("dp", "fsdp"), None),
            P(("dp", "fsdp"), None),
            P(("dp", "fsdp")),
            P(("dp", "fsdp"), None),
            P(("dp", "fsdp")),
            P(("dp", "fsdp")),
            P(("dp", "fsdp")),
            P(("dp", "fsdp"), None),
            P(("dp", "fsdp")),
            P(("dp", "fsdp"), None),
            P(("dp", "fsdp")),
        ),
        check_vma=False,
    )
```

profile of v0, /device:TPU:0, one launch (start us, length us, event | category | flops | bytes accessed | tf_op | source)
XLA Modules:
  0.0 2430.6 jit_solution(14723082137461177575)
XLA Ops:
  20.5 42.9 %all-reduce.28 = (bf16[1024]{0:T(1024)(128)(2,1)S(1)}, bf16[1024]{0:T(1024)(128)(2,1)S(1)}, bf16[1024]{0:T(1024)(128)(2,1)S(1)}, bf16[1024]{0:T(1024)(128)(2,1)S...) all-reduce(bf16[1024]{0:T(1024)(128)(2,1)S(1)} %dynamic-update-slic, ...), channel_id=1, replica_groups=mesh['dp'=4,'fsdp'=8] {'dp','fsdp'}, use_global_device_ids=true, to_apply=%add.2 | all-reduce | flops 13312 | bytes 53248
  63.5 39.8 %all-gather = bf16[32,1,128]{2,1,0:T(2,128)(2,1)S(1)} all-gather(bf16[1,1,128]{2,1,0:T(2,128)(2,1)S(1)} %bitcast.197), channel_id=1, replica_groups=mesh['dp'=4,'fsdp'=8] {'dp','fsdp'}, dimensions={0}, use_global_device_ids=true | all-gather | bytes 8448 | tf_op jit(solution)/shard_map/all_gather | solution.py:209
  110.0 18.9 all-gather.12.cloned.1.call-done
  135.0 52.0 %all-gather.16.cloned.1.call-done = bf16[1024,1024]{1,0:T(8,128)(2,1)} async-done(((bf16[32,1024]{1,0:T(8,128)(2,1)}), bf16[1024,1024]{1,0:T(8,128)(2,1)}) %all-gather.16.cloned.1.call-update) | async-done | bytes 2097168 | tf_op jit(solution)/shard_map/all_gather | solution.py:192
  192.4 8.4 fusion.130
  200.8 8.4 fusion.7
  209.2 8.5 fusion.76
  217.7 27.3 %all-gather.20.cloned.1.call-done = bf16[1024,1024]{1,0:T(8,128)(2,1)} async-done(((bf16[32,1024]{1,0:T(8,128)(2,1)}), bf16[1024,1024]{1,0:T(8,128)(2,1)}) %all-gather.20.cloned.1.call-update) | async-done | bytes 2097168 | tf_op jit(solution)/shard_map/all_gather | solution.py:202
  248.0 54.9 %all-gather.24.cloned.1.call-done = bf16[1024,1024]{1,0:T(8,128)(2,1)} async-done(((bf16[32,1024]{1,0:T(8,128)(2,1)}), bf16[1024,1024]{1,0:T(8,128)(2,1)}) %all-gather.24.cloned.1.call-update) | async-done | bytes 2097168 | tf_op jit(solution)/shard_map/all_gather | solution.py:201
  311.0 49.9 %all-gather.18.cloned.1.call-done = bf16[1024,1024]{1,0:T(8,128)(2,1)} async-done(((bf16[32,1024]{1,0:T(8,128)(2,1)}), bf16[1024,1024]{1,0:T(8,128)(2,1)}) %all-gather.18.cloned.1.call-update) | async-done | bytes 2097168 | tf_op jit(solution)/shard_map/all_gather | solution.py:195
  364.8 54.2 %all-gather.22.cloned.1.call-done = bf16[1024,1024]{1,0:T(8,128)(2,1)} async-done(((bf16[32,1024]{1,0:T(8,128)(2,1)}), bf16[1024,1024]{1,0:T(8,128)(2,1)}) %all-gather.22.cloned.1.call-update) | async-done | bytes 2097168 | tf_op jit(solution)/shard_map/all_gather | solution.py:199
  425.2 10.9 multiply_reduce_fusion.2
  436.2 9.8 fusion.3
  446.0 10.1 fusion.77
  456.1 21.1 all-gather.26.cloned.1.call-done
  482.2 74.2 %all-gather.28.cloned.1.call-done = bf16[1024,4096]{1,0:T(8,128)(2,1)} async-done(((bf16[32,4096]{1,0:T(8,128)(2,1)}), bf16[1024,4096]{1,0:T(8,128)(2,1)}) %all-gather.28.cloned.1.call-update) | async-done | bytes 8388624 | tf_op jit(solution)/shard_map/all_gather | solution.py:208
  556.4 27.4 %fusion.24 = (bf16[512,4096]{1,0:T(8,128)(2,1)}, f32[512,4096]{1,0:T(8,128)}) fusion(f32[4096]{0:T(1024)S(1)} %bitcast.195, bf16[1024,4096]{1,0:T(8,128)(2,1)} %all-gather.28.cloned.1.call-done, f32[512,1024]{1,0:T(8,128)} %copy-done.11, f32[1024]{0:T(1024)S(1)} %convert_element_type.279, f32[1024]{0:T(1024)S(1)} %convert_element_type.278, ...), kind=kOutput, calls=%fused_computation.30 | convolution fusion | flops 4436000768 | bytes 23097344 | tf_op jit(solution)/shard_map/dot_general | solution.py:16
  583.7 51.4 %all-gather.30.cloned.1.call-done = bf16[4096,1024]{1,0:T(8,128)(2,1)} async-done(((bf16[128,1024]{1,0:T(8,128)(2,1)}), bf16[4096,1024]{1,0:T(8,128)(2,1)}) %all-gather.30.cloned.1.call-update) | async-done | bytes 8388624 | tf_op jit(solution)/shard_map/all_gather | solution.py:210
  635.2 12.9 convert_reduce_fusion
  648.0 8.0 multiply_reduce_fusion.3
  662.2 11.1 fusion.137
  673.3 9.6 convert_reduce_fusion.3
  682.9 27.6 %convert_reduce_fusion.5 = (f32[16,64]{1,0:T(8,128)S(1)}, bf16[16,64,512]{2,1,0:T(8,128)(2,1)}) fusion(bf16[588,16,64]{0,2,1:T(8,128)(2,1)} %bitcast.178, f32[16,512,588]{1,2,0:T(8,128)} %fusion.137, f32[16,512]{1,0:T(8,128)S(1)} %log_add_fusion.1, f32[16,512,588]{1,2,0:T(8,128)} %get-tuple-element.253), kind=kOutput, calls=%fused_computation.92 | convolution fusion | flops 661495360 | bytes 40824832 | tf_op jit(solution)/shard_map/while/body/eval_jaxpr/hqk,khe->qhe/dot_general | solution.py:112
  710.6 5.2 multiply_reduce_fusion.4
  723.0 9.8 fusion.138
  732.7 9.5 convert_reduce_fusion.7
  742.2 24.0 fusion.81
  766.2 24.1 convert_reduce_fusion.8
  812.0 5.3 copy.115
  824.9 27.6 %fusion.73 = bf16[16,64,588]{2,1,0:T(8,128)(2,1)} fusion(bf16[512,16,64]{0,2,1:T(8,128)(2,1)S(1)} %bitcast.188, f32[16,512,588]{1,2,0:T(8,128)} %fusion.137, f32[16,512]{1,0:T(8,128)S(1)} %log_add_fusion.1, f32[16,512,588]{1,2,0:T(8,128)} %get-tuple-element.253), kind=kOutput, calls=%fused_computation.116 | convolution fusion | flops 660525632 | bytes 40820736 | tf_op jit(solution)/shard_map/while/body/eval_jaxpr/hqk,qhe->khe/dot_general | solution.py:115
  852.5 5.2 convolution_bitcast_fusion.1
  857.6 5.4 copy.113
  869.8 5.1 fusion.121
  875.0 5.1 fusion.125
  880.2 5.0 fusion.123
  885.3 13.3 fusion.119
  898.9 12.8 fusion.96
  925.5 5.5 fusion.90
  949.3 128.6 %reduce-scatter.25.cloned.1.call-done = f32[32,1024]{1,0:T(8,128)} async-done(((f32[1024,1024]{1,0:T(8,128)}), f32[32,1024]{1,0:T(8,128)}) %reduce-scatter.25.cloned.1.call-update) | async-done | bytes 131088 | tf_op jit(solution)/shard_map/reduce_scatter | solution.py:258
  1077.9 139.7 %reduce-scatter.33.cloned.1.call-done = f32[32,1024]{1,0:T(8,128)} async-done(((f32[1024,1024]{1,0:T(8,128)}), f32[32,1024]{1,0:T(8,128)}) %reduce-scatter.33.cloned.1.call-update) | async-done | bytes 131088
  1217.6 139.6 %reduce-scatter.23.cloned.1.call-done = f32[32,1024]{1,0:T(8,128)} async-done(((f32[1024,1024]{1,0:T(8,128)}), f32[32,1024]{1,0:T(8,128)}) %reduce-scatter.23.cloned.1.call-update) | async-done | bytes 131088 | tf_op jit(solution)/shard_map/reduce_scatter | solution.py:253
  1357.2 139.6 %reduce-scatter.31.cloned.1.call-done = f32[32,1024]{1,0:T(8,128)} async-done(((f32[1024,1024]{1,0:T(8,128)}), f32[32,1024]{1,0:T(8,128)}) %reduce-scatter.31.cloned.1.call-update) | async-done | bytes 131088
  1496.9 139.5 %reduce-scatter.21.cloned.1.call-done = f32[32,1024]{1,0:T(8,128)} async-done(((f32[1024,1024]{1,0:T(8,128)}), f32[32,1024]{1,0:T(8,128)}) %reduce-scatter.21.cloned.1.call-update) | async-done | bytes 131088 | tf_op jit(solution)/shard_map/reduce_scatter | solution.py:249
  1636.3 139.5 %reduce-scatter.19.cloned.1.call-done = f32[32,1024]{1,0:T(8,128)} async-done(((f32[1024,1024]{1,0:T(8,128)}), f32[32,1024]{1,0:T(8,128)}) %reduce-scatter.19.cloned.1.call-update) | async-done | bytes 131088 | tf_op jit(solution)/shard_map/reduce_scatter | solution.py:247
  1775.8 139.3 %reduce-scatter.15.cloned.1.call-done = f32[32,1024]{1,0:T(8,128)} async-done(((f32[1024,1024]{1,0:T(8,128)}), f32[32,1024]{1,0:T(8,128)}) %reduce-scatter.15.cloned.1.call-update) | async-done | bytes 131088 | tf_op jit(solution)/shard_map/reduce_scatter | solution.py:244
  1915.1 139.7 %reduce-scatter.17.cloned.1.call-done = f32[32,1024]{1,0:T(8,128)} async-done(((f32[1024,1024]{1,0:T(8,128)}), f32[32,1024]{1,0:T(8,128)}) %reduce-scatter.17.cloned.1.call-update) | async-done | bytes 131088 | tf_op jit(solution)/shard_map/reduce_scatter | solution.py:246
  2054.8 181.4 %reduce-scatter.27.cloned.1.call-done = f32[32,4096]{1,0:T(8,128)} async-done(((f32[1024,4096]{1,0:T(8,128)}), f32[32,4096]{1,0:T(8,128)}) %reduce-scatter.27.cloned.1.call-update) | async-done | bytes 524304 | tf_op jit(solution)/shard_map/reduce_scatter | solution.py:262
  2236.2 187.4 %reduce-scatter.29.cloned.1.call-done = f32[128,1024]{1,0:T(8,128)} async-done(((f32[4096,1024]{1,0:T(8,128)}), f32[128,1024]{1,0:T(8,128)}) %reduce-scatter.29.cloned.1.call-update) | async-done | bytes 524304 | tf_op jit(solution)/shard_map/reduce_scatter | solution.py:264
  (271 shorter events, 137.7 us)
Async XLA Ops:
  7.2 237.8 %copy-start = (bf16[1,588,1024]{2,1,0:T(8,128)(2,1)S(1)}, bf16[1,588,1024]{2,1,0:T(8,128)(2,1)}, u32[]{:S(2)}) copy-start(bf16[1,588,1024]{2,1,0:T(8,128)(2,1)} %param.30) | copy-start | bytes 3612676
  7.2 10.2 copy-start.42
  7.2 10.4 copy-start.43
  7.3 10.7 copy-start.44
  7.3 10.9 copy-start.45
  7.3 11.1 copy-start.46
  7.3 11.3 copy-start.47
  7.3 11.6 copy-start.48
  7.3 11.8 copy-start.49
  7.3 12.0 copy-start.50
  7.3 12.2 copy-start.51
  7.3 12.5 copy-start.52
  7.3 12.7 copy-start.53
  7.4 12.9 copy-start.54
  7.4 56.2 %copy-start.36 = (bf16[128]{0:T(256)(128)(2,1)S(1)}, bf16[128]{0:T(256)(128)(2,1)}, u32[]{:S(2)}) copy-start(bf16[128]{0:T(256)(128)(2,1)} %param.55) | copy-start | bytes 772
  7.4 96.8 %all-gather.14.cloned.1.call-start = ((), (), s32[]{:S(2)}) async-start(), calls=%async_computation.11 | async-start | bytes 2162688 | tf_op jit(solution)/shard_map/all_gather | solution.py:190
  8.1 120.8 %all-gather.12.cloned.1.call-start = ((), (), s32[]{:S(2)}) async-start(), calls=%async_computation.10 | async-start | bytes 2162688 | tf_op jit(solution)/shard_map/all_gather | solution.py:193
  8.9 178.2 %all-gather.16.cloned.1.call-start = ((), (), s32[]{:S(2)}) async-start(), calls=%async_computation.12 | async-start | bytes 2162688 | tf_op jit(solution)/shard_map/all_gather | solution.py:192
  9.6 235.4 %all-gather.20.cloned.1.call-start = ((), (), s32[]{:S(2)}) async-start(), calls=%async_computation.14 | async-start | bytes 2162688 | tf_op jit(solution)/shard_map/all_gather | solution.py:202
  10.2 292.8 %all-gather.24.cloned.1.call-start = ((), (), s32[]{:S(2)}) async-start(), calls=%async_computation.16 | async-start | bytes 2162688 | tf_op jit(solution)/shard_map/all_gather | solution.py:201
  10.8 350.2 %all-gather.18.cloned.1.call-start = ((), (), s32[]{:S(2)}) async-start(), calls=%async_computation.13 | async-start | bytes 2162688 | tf_op jit(solution)/shard_map/all_gather | solution.py:195
  11.3 407.7 %all-gather.22.cloned.1.call-start = ((), (), s32[]{:S(2)}) async-start(), calls=%async_computation.15 | async-start | bytes 2162688 | tf_op jit(solution)/shard_map/all_gather | solution.py:199
  12.1 465.1 %all-gather.26.cloned.1.call-start = ((), (), s32[]{:S(2)}) async-start(), calls=%async_computation.17 | async-start | bytes 2162688 | tf_op jit(solution)/shard_map/all_gather | solution.py:204
  12.8 543.5 %all-gather.28.cloned.1.call-start = ((), (), s32[]{:S(2)}) async-start(), calls=%async_computation.18 | async-start | bytes 8650752 | tf_op jit(solution)/shard_map/all_gather | solution.py:208
  13.6 621.6 %all-gather.30.cloned.1.call-start = ((), (), s32[]{:S(2)}) async-start(), calls=%async_computation.19 | async-start | bytes 8650752 | tf_op jit(solution)/shard_map/all_gather | solution.py:210
  14.2 917.5 %all-reduce.31.cloned.1.call-start = ((), (), s32[]{:S(2)}) async-start(), calls=%async_computation.30 | async-start | bytes 139264
  17.0 170.0 %copy-start.25 = (f32[512]{0:T(512)}, f32[512]{0:T(512)S(1)}, u32[]{:S(2)}) copy-start(f32[512]{0:T(512)S(1)} %broadcast_multiply_fusion.8) | copy-start | bytes 6148
  17.4 169.6 %copy-start.29 = (f32[512]{0:T(512)}, f32[512]{0:T(512)S(1)}, u32[]{:S(2)}) copy-start(f32[512]{0:T(512)S(1)} %add_rsqrt_fusion.2) | copy-start | bytes 6148
  63.4 123.6 %copy-start.27 = (f32[1024]{0:T(1024)}, f32[1024]{0:T(1024)S(1)}, u32[]{:S(2)}) copy-start(f32[1024]{0:T(1024)S(1)} %convert_element_type.252) | copy-start | bytes 12292
  63.4 123.6 %copy-start.31 = (f32[1024]{0:T(1024)}, f32[1024]{0:T(1024)S(1)}, u32[]{:S(2)}) copy-start(f32[1024]{0:T(1024)S(1)} %convert_element_type.253) | copy-start | bytes 12292
  63.5 355.6 %copy-start.33 = (f32[1024]{0:T(1024)}, f32[1024]{0:T(1024)S(1)}, u32[]{:S(2)}) copy-start(f32[1024]{0:T(1024)S(1)} %convert_element_type.268) | copy-start | bytes 12292
  110.0 82.4 %copy-start.14 = (bf16[512,1024]{0,1:T(8,128)(2,1)}, bf16[512,1024]{0,1:T(8,128)(2,1)S(1)}, u32[]{:S(2)}) copy-start(bf16[512,1024]{0,1:T(8,128)(2,1)S(1)} %copy.95) | copy-start | bytes 3145732
  364.4 112.7 %copy-start.3 = (f32[512,1024]{1,0:T(8,128)}, f32[512,1024]{1,0:T(8,128)S(1)}, u32[]{:S(2)}) copy-start(f32[512,1024]{1,0:T(8,128)S(1)} %get-tuple-element.251) | copy-start | bytes 6291460
  556.4 78.8 %copy-start.22 = (bf16[1,512,1024]{2,1,0:T(8,128)(2,1)S(1)}, bf16[1,512,1024]{2,1,0:T(8,128)(2,1)}, u32[]{:S(2)}) copy-start(bf16[1,512,1024]{2,1,0:T(8,128)(2,1)} %param.33) | copy-start | bytes 3145732
  635.2 12.9 copy-start.12
  635.2 12.9 copy-start.37
  662.2 11.1 copy-start.10
  802.4 275.4 %reduce-scatter.25.cloned.1.call-start = ((), (), s32[]{:S(2)}) async-start(), calls=%async_computation.25 | async-start | bytes 4325376 | tf_op jit(solution)/shard_map/reduce_scatter | solution.py:258
  807.0 410.6 %reduce-scatter.33.cloned.1.call-start = ((), (), s32[]{:S(2)}) async-start(), calls=%async_computation.29 | async-start | bytes 4325376
  817.4 539.9 %reduce-scatter.23.cloned.1.call-start = ((), (), s32[]{:S(2)}) async-start(), calls=%async_computation.24 | async-start | bytes 4325376 | tf_op jit(solution)/shard_map/reduce_scatter | solution.py:253
  823.7 673.2 %reduce-scatter.31.cloned.1.call-start = ((), (), s32[]{:S(2)}) async-start(), calls=%async_computation.28 | async-start | bytes 4325376
  863.1 773.2 %reduce-scatter.21.cloned.1.call-start = ((), (), s32[]{:S(2)}) async-start(), calls=%async_computation.23 | async-start | bytes 4325376 | tf_op jit(solution)/shard_map/reduce_scatter | solution.py:249
  869.2 906.6 %reduce-scatter.19.cloned.1.call-start = ((), (), s32[]{:S(2)}) async-start(), calls=%async_computation.22 | async-start | bytes 4325376 | tf_op jit(solution)/shard_map/reduce_scatter | solution.py:247
  875.0 1040.2 %reduce-scatter.15.cloned.1.call-start = ((), (), s32[]{:S(2)}) async-start(), calls=%async_computation.20 | async-start | bytes 4325376 | tf_op jit(solution)/shard_map/reduce_scatter | solution.py:244
  880.1 1174.7 %reduce-scatter.17.cloned.1.call-start = ((), (), s32[]{:S(2)}) async-start(), calls=%async_computation.21 | async-start | bytes 4325376 | tf_op jit(solution)/shard_map/reduce_scatter | solution.py:246
  885.3 1350.9 %reduce-scatter.27.cloned.1.call-start = ((), (), s32[]{:S(2)}) async-start(), calls=%async_computation.26 | async-start | bytes 17301504 | tf_op jit(solution)/shard_map/reduce_scatter | solution.py:262
  898.7 1524.9 %reduce-scatter.29.cloned.1.call-start = ((), (), s32[]{:S(2)}) async-start(), calls=%async_computation.27 | async-start | bytes 17301504 | tf_op jit(solution)/shard_map/reduce_scatter | solution.py:264
  912.4 11.6 slice-start
  (32 other events, 110.4 us)
Sparse Core Ops, SparseCore 0:
  11.1 59.4 all-gather.13
  73.5 55.3 all-gather.11
  131.8 55.2 all-gather.15
  189.7 55.2 all-gather.19
  247.7 55.2 all-gather.23
  305.7 55.2 all-gather.17
  363.8 55.2 all-gather.21
  421.9 55.2 all-gather.25
  480.0 76.2 all-gather.27
  559.1 76.0 all-gather.29
  802.6 129.0 all-reduce.30
  934.4 143.4 reduce-scatter.24
  1080.7 136.8 reduce-scatter.32
  1220.3 136.8 reduce-scatter.22
  1359.9 136.8 reduce-scatter.30
  1499.6 136.7 reduce-scatter.20
  1639.0 136.7 reduce-scatter.18
  1778.5 136.5 reduce-scatter.14
  1918.0 136.7 reduce-scatter.16
  2057.5 178.6 reduce-scatter.26
  2239.1 184.4 reduce-scatter.28
where the time goes:
time: 2440 us; the launch traced here: 2430 us
  waiting for transfers between devices  1890 us (77%)
  matrix products  352 us (14%)
  blocking collectives  82.7 us (3%)
  local copies, waits for them, and re-layouts  66.6 us (3%)
  other arithmetic  26.5 us (1%)
    unnamed x24, waiting for transfers between devices  286 us
    reduce_scatter x1, waiting for transfers between devices, spread(): lax.psum_scatter(grad_final_mat, ('dp', 'fsdp'), scatter_dimension=0, til...  187 us
    reduce_scatter x1, waiting for transfers between devices, spread(): lax.psum_scatter(grad_hidden_mat, ('dp', 'fsdp'), scatter_dimension=0, ti...  181 us
    reduce_scatter x1, waiting for transfers between devices, spread(): lax.psum_scatter(grad_key_mat, ('dp', 'fsdp'), scatter_dimension=0, tiled...  140 us
    reduce_scatter x1, waiting for transfers between devices, spread(): lax.psum_scatter(grad_cquery_mat, ('dp', 'fsdp'), scatter_dimension=0, ti...  140 us
    reduce_scatter x1, waiting for transfers between devices, spread(): lax.psum_scatter(grad_value_mat, ('dp', 'fsdp'), scatter_dimension=0, til...  139 us
    reduce_scatter x1, waiting for transfers between devices, spread(): lax.psum_scatter(grad_out_mat, ('dp', 'fsdp'), scatter_dimension=0, tiled...  139 us
    reduce_scatter x1, waiting for transfers between devices, spread(): lax.psum_scatter(grad_query_mat, ('dp', 'fsdp'), scatter_dimension=0, til...  139 us
  transfers between devices with their start and end apart: 21, of which 20 were waited for; matrix products, arithmetic and copies ran while one was open for 11% of the time, Pallas kernels for 0%

commit v1 on v0

--- a/solution.py
+++ b/solution.py
@@ -1,6 +1,10 @@
+import functools
+
 import jax
 import jax.numpy as jnp
 from jax import lax
+from jax.experimental import pallas as pl
+from jax.experimental.pallas import tpu as pltpu
 from jax.sharding import PartitionSpec as P
 
 HEADS = 16
@@ -158,115 +162,388 @@
     return lax.map(one_page, (query_pages, key_pages, value_pages, grad_pages, total_pages))
 
 
-def collect(
-    self_gain,
-    self_shift,
-    self_query,
-    self_query_bias,
-    self_key,
-    self_value,
-    self_value_bias,
-    self_out,
-    self_out_bias,
-    cross_gain,
-    cross_shift,
-    cross_query,
-    cross_query_bias,
-    cross_key,
-    cross_value,
-    cross_value_bias,
-    cross_out,
-    cross_out_bias,
-    feed_gain,
-    feed_shift,
-    feed_in,
-    feed_in_bias,
-    feed_out,
-    feed_out_bias,
-):
-    return (
-        lax.all_gather(self_gain, ("dp", "fsdp"), axis=0, tiled=True),
-        lax.all_gather(self_shift, ("dp", "fsdp"), axis=0, tiled=True),
-        lax.all_gather(self_query, ("dp", "fsdp"), axis=0, tiled=True),
-        lax.all_gather(self_query_bias, ("dp", "fsdp"), axis=0, tiled=True),
-        lax.all_gather(self_key, ("dp", "fsdp"), axis=0, tiled=True),
-        lax.all_gather(self_value, ("dp", "fsdp"), axis=0, tiled=True),
-        lax.all_gather(self_value_bias, ("dp", "fsdp"), axis=0, tiled=True),
-        lax.all_gather(self_out, ("dp", "fsdp"), axis=0, tiled=True),
-        lax.all_gather(self_out_bias, ("dp", "fsdp"), axis=0, tiled=True),
-        lax.all_gather(cross_gain, ("dp", "fsdp"), axis=0, tiled=True),
-        lax.all_gather(cross_shift, ("dp", "fsdp"), axis=0, tiled=True),
-        lax.all_gather(cross_query, ("dp", "fsdp"), axis=0, tiled=True),
-        lax.all_gather(cross_query_bias, ("dp", "fsdp"), axis=0, tiled=True),
-        lax.all_gather(cross_key, ("dp", "fsdp"), axis=0, tiled=True),
-        lax.all_gather(cross_value, ("dp", "fsdp"), axis=0, tiled=True),
-        lax.all_gather(cross_value_bias, ("dp", "fsdp"), axis=0, tiled=True),
-        lax.all_gather(cross_out, ("dp", "fsdp"), axis=0, tiled=True),
-        lax.all_gather(cross_out_bias, ("dp", "fsdp"), axis=0, tiled=True),
-        lax.all_gather(feed_gain, ("dp", "fsdp"), axis=0, tiled=True),
-        lax.all_gather(feed_shift, ("dp", "fsdp"), axis=0, tiled=True),
-        lax.all_gather(feed_in, ("dp", "fsdp"), axis=0, tiled=True),
-        lax.all_gather(feed_in_bias, ("dp", "fsdp"), axis=0, tiled=True),
-        lax.all_gather(feed_out, ("dp", "fsdp"), axis=0, tiled=True),
-        lax.all_gather(feed_out_bias, ("dp", "fsdp"), axis=0, tiled=True),
-    )
-
-
-def spread(
-    grad_gain_one,
-    grad_shift_one,
-    grad_query_mat,
-    grad_query_vec,
-    grad_key_mat,
-    grad_value_mat,
-    grad_value_vec,
-    grad_out_mat,
-    grad_out_vec,
-    grad_gain_two,
-    grad_shift_two,
-    grad_cquery_mat,
-    grad_cquery_vec,
-    grad_ckey_mat,
-    grad_cvalue_mat,
-    grad_cvalue_vec,
-    grad_cout_mat,
-    grad_cout_vec,
-    grad_gain_three,
-    grad_shift_three,
-    grad_hidden_mat,
-    grad_hidden_vec,
-    grad_final_mat,
-    grad_final_vec,
-):
-    return (
-        lax.psum_scatter(grad_gain_one, ("dp", "fsdp"), scatter_dimension=0, tiled=True),
-        lax.psum_scatter(grad_shift_one, ("dp", "fsdp"), scatter_dimension=0, tiled=True),
-        lax.psum_scatter(grad_query_mat, ("dp", "fsdp"), scatter_dimension=0, tiled=True),
-        lax.psum_scatter(grad_query_vec, ("dp", "fsdp"), scatter_dimension=0, tiled=True),
-        lax.psum_scatter(grad_key_mat, ("dp", "fsdp"), scatter_dimension=0, tiled=True),
-        lax.psum_scatter(grad_value_mat, ("dp", "fsdp"), scatter_dimension=0, tiled=True),
-        lax.psum_scatter(grad_value_vec, ("dp", "fsdp"), scatter_dimension=0, tiled=True),
-        lax.psum_scatter(grad_out_mat, ("dp", "fsdp"), scatter_dimension=0, tiled=True),
-        lax.psum_scatter(grad_out_vec, ("dp", "fsdp"), scatter_dimension=0, tiled=True),
-        lax.psum_scatter(grad_gain_two, ("dp", "fsdp"), scatter_dimension=0, tiled=True),
-        lax.psum_scatter(grad_shift_two, ("dp", "fsdp"), scatter_dimension=0, tiled=True),
-        lax.psum_scatter(grad_cquery_mat, ("dp", "fsdp"), scatter_dimension=0, tiled=True),
-        lax.psum_scatter(grad_cquery_vec, ("dp", "fsdp"), scatter_dimension=0, tiled=True),
-        lax.psum_scatter(grad_ckey_mat, ("dp", "fsdp"), scatter_dimension=0, tiled=True),
-        lax.psum_scatter(grad_cvalue_mat, ("dp", "fsdp"), scatter_dimension=0, tiled=True),
-        lax.psum_scatter(grad_cvalue_vec, ("dp", "fsdp"), scatter_dimension=0, tiled=True),
-        lax.psum_scatter(grad_cout_mat, ("dp", "fsdp"), scatter_dimension=0, tiled=True),
-        lax.psum_scatter(grad_cout_vec, ("dp", "fsdp"), scatter_dimension=0, tiled=True),
-        lax.psum_scatter(grad_gain_three, ("dp", "fsdp"), scatter_dimension=0, tiled=True),
-        lax.psum_scatter(grad_shift_three, ("dp", "fsdp"), scatter_dimension=0, tiled=True),
-        lax.psum_scatter(grad_hidden_mat, ("dp", "fsdp"), scatter_dimension=0, tiled=True),
-        lax.psum_scatter(grad_hidden_vec, ("dp", "fsdp"), scatter_dimension=0, tiled=True),
-        lax.psum_scatter(grad_final_mat, ("dp", "fsdp"), scatter_dimension=0, tiled=True),
-        lax.psum_scatter(grad_final_vec, ("dp", "fsdp"), scatter_dimension=0, tiled=True),
-    )
+MESH_ID = pl.DeviceIdType.MESH
+BOTH = ("dp", "fsdp")
+CORE_RATE = 500e3
+LINK_RATE = 96e3
+HOP = 2.5
+VEC_ROWS = 8
+VEC_LANES = 128
+
+
+def bit_table(mesh):
+    bits = []
+    for axis, name in enumerate(BOTH):
+        step = mesh.shape[name] // 2
+        while step >= 1:
+            bits.append((axis, step))
+            step //= 2
+    return bits
+
+
+def can_route(mesh, rows):
+    sizes = [mesh.shape[name] for name in BOTH]
+    return all(s & (s - 1) == 0 for s in sizes) and rows % 16 == 0
+
+
+def route_orders(bits):
+    outer = [i for i, (axis, _) in enumerate(bits) if axis == 0]
+    inner = [i for i, (axis, _) in enumerate(bits) if axis == 1]
+    return (outer + inner, outer + inner[:-1][::-1] + inner[-1:])
+
+
+def loads_of(bits, at, size):
+    axis, step = bits[at]
+    if axis == 1 and step == 1:
+        return {"core": size / CORE_RATE}
+    if axis == 1:
+        return {f"inner{step}": 2 * size / LINK_RATE}
+    loads = {"outer1": 2 * size / LINK_RATE}
+    if step > 1:
+        loads["outer2"] = 2 * size * step / LINK_RATE
+    return loads
+
+
+def plan_sends(bits, orders, sizes, growing, add_rate):
+    count = len(bits)
+    ready = [(0.0, unit, 0) for unit in range(len(orders))]
+    free = {}
+    plan = []
+    while ready:
+        choices = []
+        for when, unit, stage in ready:
+            scale = 2**stage if growing else 2 ** (count - 1 - stage)
+            loads = loads_of(bits, orders[unit][stage], sizes[unit] * scale)
+            start = max([when] + [free.get(link, 0.0) for link in loads])
+            choices.append((round(start, 3), unit, -stage, when, scale))
+        start, unit, stage, when, scale = min(choices)
+        stage = -stage
+        ready.remove((when, unit, stage))
+        loads = loads_of(bits, orders[unit][stage], sizes[unit] * scale)
+        for link, took in loads.items():
+            free[link] = start + took
+        plan.append((start, unit, stage))
+        if stage + 1 < count:
+            after = start + max(loads.values()) + HOP
+            if add_rate:
+                after += sizes[unit] * scale / add_rate
+            ready.append((after, unit, stage + 1))
+    return [(unit, stage) for _, unit, stage in sorted(plan)]
+
+
+def my_bits(bits):
+    place = (lax.axis_index("dp"), lax.axis_index("fsdp"))
+    return [(place[axis] // step) % 2 for axis, step in bits]
+
+
+def partner(bits, mine, at):
+    place = [lax.axis_index("dp"), lax.axis_index("fsdp")]
+    axis, step = bits[at]
+    place[axis] = place[axis] + step * (1 - 2 * mine[at])
+    return tuple(place)
+
+
+def greet(bits, mine):
+    barrier = pltpu.get_barrier_semaphore()
+    for at in range(len(bits)):
+        pl.semaphore_signal(
+            barrier, inc=1, device_id=partner(bits, mine, at), device_id_type=MESH_ID
+        )
+    pl.semaphore_wait(barrier, len(bits))
+
+
+def unit_shape(blocks, unit):
+    array, rows, cols = unit
+    block = blocks[array]
+    return (len(range(*rows.indices(block[0]))), len(range(*cols.indices(block[1]))))
+
+
+def gather_kernel(bits, units, orders, plan, n_arrays, *refs):
+    count = len(bits)
+    sources = refs[:n_arrays]
+    targets = refs[n_arrays : 2 * n_arrays]
+    send_sem, recv_sem, own_sem = refs[2 * n_arrays :]
+    mine = my_bits(bits)
+    own = [
+        pltpu.make_async_copy(sources[i], targets[i].at[tuple(mine)], own_sem.at[i])
+        for i in range(n_arrays)
+    ]
+    for copy in own:
+        copy.start()
+    greet(bits, mine)
+
+    def message(unit, stage):
+        array, rows, cols = units[unit]
+        order = orders[unit]
+        where = tuple(slice(None) if b in order[:stage] else mine[b] for b in range(count))
+        place = targets[array].at[where + (rows, cols)]
+        source = sources[array].at[rows, cols] if stage == 0 else place
+        return pltpu.make_async_remote_copy(
+            src_ref=source,
+            dst_ref=place,
+            send_sem=send_sem.at[unit, stage],
+            recv_sem=recv_sem.at[unit, stage],
+            device_id=partner(bits, mine, order[stage]),
+            device_id_type=MESH_ID,
+        )
+
+    settled = set()
+    for unit, stage in plan:
+        array = units[unit][0]
+        if stage > 0:
+            if array not in settled:
+                settled.add(array)
+                own[array].wait()
+            message(unit, stage - 1).wait_recv()
+        message(unit, stage).start()
+    for array in range(n_arrays):
+        if array not in settled:
+            own[array].wait()
+    for unit in range(len(units)):
+        message(unit, count - 1).wait_recv()
+    for unit in range(len(units)):
+        for stage in range(count):
+            message(unit, stage).wait_send()
+
+
+def gather_all(mesh, shards, units, collective_id):
+    bits = bit_table(mesh)
+    routes = route_orders(bits)
+    orders = [routes[u % 2] for u in range(len(units))]
+    shapes = [unit_shape([s.shape for s in shards], unit) for unit in units]
+    sizes = [
+        shape[0] * shape[1] * shards[unit[0]].dtype.itemsize for shape, unit in zip(shapes, units)
+    ]
+    plan = plan_sends(bits, orders, sizes, True, None)
+    n = len(shards)
+    sems = (len(units), len(bits))
+    return pl.pallas_call(
+        functools.partial(gather_kernel, bits, units, orders, plan, n),
+        out_shape=[
+            jax.ShapeDtypeStruct((2,) * len(bits) + s.shape, s.dtype) for s in shards
+        ],
+        in_specs=[pl.BlockSpec(memory_space=pltpu.HBM)] * n,
+        out_specs=[pl.BlockSpec(memory_space=pltpu.HBM)] * n,
+        scratch_shapes=[
+            pltpu.SemaphoreType.DMA(sems),
+            pltpu.SemaphoreType.DMA(sems),
+            pltpu.SemaphoreType.DMA((n,)),
+        ],
+        compiler_params=pltpu.CompilerParams(
+            collective_id=collective_id, has_side_effects=True
+        ),
+        name="gather_weights",
+    )(*shards)
+
+
+def scatter_kernel(bits, units, orders, plan, n_arrays, n_units, *refs):
+    count = len(bits)
+    sources = refs[:n_arrays]
+    results = refs[n_arrays : 2 * n_arrays]
+    held = refs[2 * n_arrays : 2 * n_arrays + n_units]
+    boxes = refs[2 * n_arrays + n_units : 2 * n_arrays + n_units + n_units * count]
+    totals = refs[2 * n_arrays + n_units + n_units * count : -4]
+    send_sem, recv_sem, load_sem, store_sem = refs[-4:]
+    mine = my_bits(bits)
+
+    def load(unit):
+        array, rows, cols = units[unit]
+        first = orders[unit][0]
+        where = tuple(mine[b] if b == first else slice(None) for b in range(count))
+        return pltpu.make_async_copy(
+            sources[array].at[where + (rows, cols)], held[unit], load_sem.at[unit]
+        )
+
+    for unit in range(n_units):
+        load(unit).start()
+    greet(bits, mine)
+
+    def message(unit, stage):
+        array, rows, cols = units[unit]
+        order = orders[unit]
+        now = order[stage]
+        where = []
+        for b in range(count):
+            if b == now:
+                where.append(1 - mine[b])
+            elif b in order[:stage]:
+                where.append(mine[b])
+            else:
+                where.append(slice(None))
+        if stage == 0:
+            source = sources[array].at[tuple(where) + (rows, cols)]
+        else:
+            source = held[unit].at[tuple(w for b, w in enumerate(where) if b != order[0])]
+        return pltpu.make_async_remote_copy(
+            src_ref=source,
+            dst_ref=boxes[unit * count + stage],
+            send_sem=send_sem.at[unit, stage],
+            recv_sem=recv_sem.at[unit, stage],
+            device_id=partner(bits, mine, now),
+            device_id_type=MESH_ID,
+        )
+
+    def add(unit, stage):
+        order = orders[unit]
+        message(unit, stage).wait_recv()
+        if stage == 0:
+            load(unit).wait()
+        box = boxes[unit * count + stage]
+        open_bits = [b for b in range(count) if b not in order[: stage + 1]]
+        blocks = 2 ** len(open_bits)
+
+        def one(block, carry):
+            where = []
+            spot = []
+            for b in range(count):
+                if b == order[0]:
+                    continue
+                if b in open_bits:
+                    digit = (block // 2 ** (len(open_bits) - 1 - open_bits.index(b))) % 2
+                    where.append(digit)
+                    spot.append(digit)
+                else:
+                    where.append(mine[b])
+            where, spot = tuple(where), tuple(spot)
+            total = held[unit][where].astype(jnp.float32) + box[spot].astype(jnp.float32)
+            if stage == count - 1:
+                totals[unit][...] = total
+            else:
+                held[unit][where] = total.astype(held[unit].dtype)
+            return carry
+
+        if blocks == 1:
+            one(0, 0)
+        else:
+            lax.fori_loop(0, blocks, one, 0)
+
+    def store(unit):
+        array, rows, cols = units[unit]
+        return pltpu.make_async_copy(
+            totals[unit], results[array].at[rows, cols], store_sem.at[unit]
+        )
+
+    for unit, stage in plan:
+        if stage > 0:
+            add(unit, stage - 1)
+        message(unit, stage).start()
+    for unit in range(n_units):
+        add(unit, count - 1)
+        store(unit).start()
+    for unit in range(n_units):
+        store(unit).wait()
+        for stage in range(count):
+            message(unit, stage).wait_send()
+
+
+def scatter_all(mesh, terms, units, collective_id):
+    bits = bit_table(mesh)
+    routes = route_orders(bits)
+    count = len(bits)
+    orders = [routes[u % 2][::-1] for u in range(len(units))]
+    shapes = [unit_shape([t.shape[count:] for t in terms], unit) for unit in units]
+    kinds = [terms[array].dtype for array, _, _ in units]
+    sizes = [s[0] * s[1] * kind.itemsize for s, kind in zip(shapes, kinds)]
+    plan = plan_sends(bits, orders, sizes, False, 1000e3)
+    n = len(terms)
+    n_units = len(units)
+    sems = (n_units, count)
+    scratch = [
+        pltpu.VMEM((2,) * (count - 1) + shapes[u], kinds[u]) for u in range(n_units)
+    ]
+    for u in range(n_units):
+        for stage in range(count):
+            scratch.append(pltpu.VMEM((2,) * (count - 1 - stage) + shapes[u], kinds[u]))
+    scratch += [pltpu.VMEM(shapes[u], jnp.float32) for u in range(n_units)]
+    scratch += [
+        pltpu.SemaphoreType.DMA(sems),
+        pltpu.SemaphoreType.DMA(sems),
+        pltpu.SemaphoreType.DMA((n_units,)),
+        pltpu.SemaphoreType.DMA((n_units,)),
+    ]
+    return pl.pallas_call(
+        functools.partial(scatter_kernel, bits, units, orders, plan, n, n_units),
+        out_shape=[jax.ShapeDtypeStruct(t.shape[count:], jnp.float32) for t in terms],
+        in_specs=[pl.BlockSpec(memory_space=pltpu.HBM)] * n,
+        out_specs=[pl.BlockSpec(memory_space=pltpu.HBM)] * n,
+        scratch_shapes=scratch,
+        compiler_params=pltpu.CompilerParams(
+            collective_id=collective_id,
+            has_side_effects=True,
+            vmem_limit_bytes=60 * 1024 * 1024,
+        ),
+        name="scatter_grads",
+    )(*terms)
+
+
+MATS = (2, 4, 5, 7, 11, 13, 14, 16, 20, 22)
+VECS = (0, 1, 3, 6, 8, 9, 10, 12, 15, 17, 18, 19, 23, 21)
+
+
+def split_units(blocks):
+    units = [(0, slice(None), slice(None))]
+    for i, (rows, cols) in enumerate(blocks):
+        base_rows, base_cols = min(rows, blocks[0][0]), min(cols, blocks[0][1])
+        for top in range(0, rows, base_rows):
+            for left in range(0, cols, base_cols):
+                units.append(
+                    (i + 1, slice(top, top + base_rows), slice(left, left + base_cols))
+                )
+    return units
+
+
+def collect(mesh, *shards):
+    mats = [shards[i] for i in MATS]
+    if not can_route(mesh, mats[0].shape[0]):
+        return tuple(lax.all_gather(s, BOTH, axis=0, tiled=True) for s in shards)
+    per = shards[0].shape[0]
+    packed = jnp.concatenate([shards[i].astype(jnp.float32) for i in VECS])
+    spare = VEC_ROWS * VEC_LANES - packed.shape[0]
+    packed = jnp.pad(packed, (0, spare)).reshape(VEC_ROWS, VEC_LANES)
+    units = split_units([m.shape for m in mats])
+    got = gather_all(mesh, [packed] + mats, units, 0)
+    devices = mesh.shape["dp"] * mesh.shape["fsdp"]
+    table = got[0].reshape(devices, VEC_ROWS * VEC_LANES)
+    full = [None] * len(shards)
+    start = 0
+    for i in VECS:
+        size = shards[i].shape[0]
+        full[i] = table[:, start : start + size].reshape(devices * size)
+        start += size
+    for i, value in zip(MATS, got[1:]):
+        full[i] = value.reshape(devices * shards[i].shape[0], shards[i].shape[1])
+    return tuple(full)
+
+
+def spread(mesh, *grads):
+    devices = mesh.shape["dp"] * mesh.shape["fsdp"]
+    mats = [grads[i] for i in MATS]
+    if not can_route(mesh, mats[0].shape[0] // devices):
+        return tuple(
+            lax.psum_scatter(g.astype(jnp.float32), BOTH, scatter_dimension=0, tiled=True)
+            for g in grads
+        )
+    spots = (2,) * len(bit_table(mesh))
+    table = jnp.concatenate([grads[i].reshape(devices, -1) for i in VECS], axis=1)
+    spare = VEC_ROWS * VEC_LANES - table.shape[1]
+    table = jnp.pad(table, ((0, 0), (0, spare))).reshape(spots + (VEC_ROWS, VEC_LANES))
+    terms = [m.reshape(spots + (m.shape[0] // devices, m.shape[1])) for m in mats]
+    units = split_units([t.shape[-2:] for t in terms])
+    got = scatter_all(mesh, [table] + terms, units, 1)
+    flat = got[0].reshape(-1)
+    owned = [None] * len(grads)
+    start = 0
+    for i in VECS:
+        size = grads[i].shape[0] // devices
+        owned[i] = flat[start : start + size]
+        start += size
+    for i, value in zip(MATS, got[1:]):
+        owned[i] = value
+    return tuple(owned)
 
 
 def on_device(
+    mesh,
     tokens,
     memory,
     page_lengths,
@@ -304,6 +581,7 @@
     inputs = tokens.reshape(row_count, width).astype(jnp.float32)
     mem_rows = memory.reshape(page_count * mem_len, width)
     full_set = collect(
+        mesh,
         self_gain,
         self_shift,
         self_query,
@@ -393,71 +671,19 @@
     hidden_low = jax.nn.gelu(hidden_pre, approximate=False).astype(jnp.bfloat16)
     result = after_cross + product(hidden_low, final_mat) + final_vec.astype(jnp.float32)
     layer_out = result.astype(jnp.bfloat16).reshape(page_count, page_len, width)
-    back_set = collect(
-        self_gain,
-        self_shift,
-        self_query,
-        self_query_bias,
-        self_key,
-        self_value,
-        self_value_bias,
-        self_out,
-        self_out_bias,
-        cross_gain,
-        cross_shift,
-        cross_query,
-        cross_query_bias,
-        cross_key,
-        cross_value,
-        cross_value_bias,
-        cross_out,
-        cross_out_bias,
-        feed_gain,
-        feed_shift,
-        feed_in,
-        feed_in_bias,
-        feed_out,
-        feed_out_bias,
-    )
-    (
-        gain_one,
-        shift_one,
-        query_mat,
-        query_vec,
-        key_mat,
-        value_mat,
-        value_vec,
-        out_mat,
-        out_vec,
-        gain_two,
-        shift_two,
-        cquery_mat,
-        cquery_vec,
-        ckey_mat,
-        cvalue_mat,
-        cvalue_vec,
-        cout_mat,
-        cout_vec,
-        gain_three,
-        shift_three,
-        hidden_mat,
-        hidden_vec,
-        final_mat,
-        final_vec,
-    ) = back_set
     grad_rows = out_grad.reshape(row_count, width).astype(jnp.float32)
     final_grad = out_grad.reshape(row_count, width)
-    grad_final_mat = product_tn(hidden_low, final_grad)
+    grad_final_mat = product_tn(hidden_low, final_grad).astype(jnp.bfloat16)
     grad_final_vec = jnp.sum(final_grad.astype(jnp.float32), axis=0)
     hidden_grad = (product_nt(final_grad, final_mat) * gelu_slope(hidden_pre)).astype(jnp.bfloat16)
-    grad_hidden_mat = product_tn(third_low, hidden_grad)
+    grad_hidden_mat = product_tn(third_low, hidden_grad).astype(jnp.bfloat16)
     grad_hidden_vec = jnp.sum(hidden_grad.astype(jnp.float32), axis=0)
     third_back, grad_gain_three, grad_shift_three = normalize_back(
         product_nt(hidden_grad, hidden_mat), third_unit, third_std, gain_three.astype(jnp.float32)
     )
     cross_grad_total = grad_rows + third_back
     cout_grad = cross_grad_total.astype(jnp.bfloat16)
-    grad_cout_mat = product_tn(cross_low, cout_grad)
+    grad_cout_mat = product_tn(cross_low, cout_grad).astype(jnp.bfloat16)
     grad_cout_vec = jnp.sum(cout_grad.astype(jnp.float32), axis=0)
     cmix_grad = (
         product_nt(cout_grad, cout_mat).astype(jnp.bfloat16).reshape(page_count, page_len, width)
@@ -468,10 +694,10 @@
     cquery_grad = cquery_grad.reshape(row_count, width).astype(jnp.bfloat16)
     ckey_grad = ckey_grad.reshape(page_count * mem_len, width).astype(jnp.bfloat16)
     cvalue_grad = cvalue_grad.reshape(page_count * mem_len, width).astype(jnp.bfloat16)
-    grad_cquery_mat = product_tn(second_low, cquery_grad)
+    grad_cquery_mat = product_tn(second_low, cquery_grad).astype(jnp.bfloat16)
     grad_cquery_vec = jnp.sum(cquery_grad.astype(jnp.float32), axis=0)
-    grad_ckey_mat = product_tn(mem_rows, ckey_grad)
-    grad_cvalue_mat = product_tn(mem_rows, cvalue_grad)
+    grad_ckey_mat = product_tn(mem_rows, ckey_grad).astype(jnp.bfloat16)
+    grad_cvalue_mat = product_tn(mem_rows, cvalue_grad).astype(jnp.bfloat16)
     grad_cvalue_vec = jnp.sum(cvalue_grad.astype(jnp.float32), axis=0)
     memory_grad = (product_nt(ckey_grad, ckey_mat) + product_nt(cvalue_grad, cvalue_mat)).reshape(
         page_count, mem_len, width
@@ -481,7 +707,7 @@
     )
     self_grad_total = cross_grad_total + second_back
     sout_grad = self_grad_total.astype(jnp.bfloat16)
-    grad_out_mat = product_tn(self_low, sout_grad)
+    grad_out_mat = product_tn(self_low, sout_grad).astype(jnp.bfloat16)
     grad_out_vec = jnp.sum(sout_grad.astype(jnp.float32), axis=0)
     smix_grad = (
         product_nt(sout_grad, out_mat).astype(jnp.bfloat16).reshape(page_count, page_len, width)
@@ -492,10 +718,10 @@
     query_grad = query_grad.reshape(row_count, width).astype(jnp.bfloat16)
     key_grad = key_grad.reshape(row_count, width).astype(jnp.bfloat16)
     value_grad = value_grad.reshape(row_count, width).astype(jnp.bfloat16)
-    grad_query_mat = product_tn(first_low, query_grad)
+    grad_query_mat = product_tn(first_low, query_grad).astype(jnp.bfloat16)
     grad_query_vec = jnp.sum(query_grad.astype(jnp.float32), axis=0)
-    grad_key_mat = product_tn(first_low, key_grad)
-    grad_value_mat = product_tn(first_low, value_grad)
+    grad_key_mat = product_tn(first_low, key_grad).astype(jnp.bfloat16)
+    grad_value_mat = product_tn(first_low, value_grad).astype(jnp.bfloat16)
     grad_value_vec = jnp.sum(value_grad.astype(jnp.float32), axis=0)
     first_in = (
         product_nt(query_grad, query_mat)
@@ -507,6 +733,7 @@
     )
     tokens_grad = (self_grad_total + first_back).reshape(page_count, page_len, width)
     owned = spread(
+        mesh,
         grad_gain_one,
         grad_shift_one,
         grad_query_mat,
@@ -568,7 +795,7 @@
         P(("dp", "fsdp")),
     )
     return jax.shard_map(
-        on_device,
+        functools.partial(on_device, mesh),
         mesh=mesh,
         in_specs=placed,
         out_specs=(

time: 2440 us -> 734 us (0.30)
  waiting for transfers between devices: 1890 us -> 0 us
  Pallas kernels: 0 us -> 322 us
  blocking collectives: 82.7 us -> 0 us
  matrix products: 352 us -> 323 us
    reduce_scatter x8 -> x0, waiting for transfers between devices: 1190 us -> none  [the longest x1 187 us: spread(): lax.psum_scatter(grad_final_mat, ('dp', 'fsdp'), scatter_dimension=0, til...]
    all_gather x10 -> x0, waiting for transfers between devices: 404 us -> none  [the longest x1 74.2 us: collect(): lax.all_gather(feed_in, ('dp', 'fsdp'), axis=0, tiled=True)]
    pallas_call x0 -> x2, Pallas kernels: none -> 322 us  [the longest x1 162 us: gather_all(): pl.pallas_call(functools.partial(gather_kernel, bits, units, orders, plan...]
    unnamed x24 -> x0, waiting for transfers between devices: 286 us -> none
    unnamed x1 -> x0, blocking collectives: 42.9 us -> none
    all_gather x1 -> x0, blocking collectives: 39.8 us -> none  [collect(): lax.all_gather(feed_in_bias, ('dp', 'fsdp'), axis=0, tiled=True)]
  transfers between devices with their start and end apart: 21 -> 0, of which waited for: 20 -> 0; matrix products, arithmetic and copies ran while one was open for 11% -> 0% of each run, Pallas kernels for 0% -> 0%
where the time goes in v1:
time: 734 us; the launch traced here: 730 us
  matrix products  323 us (44%)
  Pallas kernels  322 us (44%)
  local copies, waits for them, and re-layouts  54.5 us (7%)
  other arithmetic  27.7 us (4%)
    pallas_call x1, Pallas kernels, gather_all(): pl.pallas_call(functools.partial(gather_kernel, bits, units, orders, plan...  162 us
    pallas_call x1, Pallas kernels, scatter_all(): pl.pallas_call(functools.partial(scatter_kernel, bits, units, orders, pla...  160 us
    dot_general x10, matrix products, product(): return jnp.dot(left, right, preferred_element_type=jnp.float32)  61.8 us
    dot_general x2, matrix products, attend_backward(): jnp.einsum('hqk,qhe->khe', score_grad, query_heads, preferred_element_typ...  51.8 us
    dot_general x2, matrix products, attend_backward(): jnp.einsum('hqk,khe->qhe', score_grad, key_heads, preferred_element_type=...  51 us
    dot_general x10, matrix products, product_tn(): lax.dot_general(left, right, (((0,), (0,)), ((), ())), preferred_element_...  45.5 us
    dot_general x10, matrix products, product_nt(): lax.dot_general(left, right, (((1,), (1,)), ((), ())), preferred_element_...  40.4 us
    unnamed x132, local copies, waits for them, and re-layouts  24.2 us

profile of v1, /device:TPU:0, one launch (start us, length us, event | category | flops | bytes accessed | tf_op | source)
XLA Modules:
  0.0 729.8 jit_solution(7844807381531467560)
XLA Ops:
  2.1 9.4 %concatenate.7 = bf16[544]{0:T(1024)(128)(2,1)S(1)} concatenate(bf16[32]{0:T(256)(128)(2,1)} %param.34, bf16[32]{0:T(256)(128)(2,1)} %param.35, bf16[32]{0:T(256)(128)(2,1)} %param.37, bf16[32]{0:T(256)(128)(2,1)} %param.40, bf16[32]{0:T(256)(128)(2,1)} %param.42, bf16[32]{0:T(256)(128)(2,1)} %param.43, bf16[32]{0:T(256)(128)(2,1)} %param.44, bf16[32]{0:T(256)(128)(2,1)} %param.46, ...), dimensions={0} | concatenate | bytes 2176 | tf_op jit(solution)/shard_map/concatenate | solution.py:500
  16.2 161.7 %gather_weights.1 = (f32[2,2,2,2,2,8,128]{6,5,4,3,2,1,0:T(8,128)}, bf16[2,2,2,2,2,32,1024]{6,5,4,3,2,1,0:T(8,128)(2,1)}, bf16[2,2,2,2,2,32,1024]{6,5,4,3,2,1,0:T...) custom-call(f32[8,128]{1,0:T(8,128)} %bitcast_convert_fusion.refs_0_, ...), custom_call_target="tpu_custom_call" | custom-call | tf_op jit(solution)/shard_map/gather_weights/pallas_call | solution.py:320
  180.6 3.9 add_convert_fusion.6
  186.1 4.3 add_convert_fusion.5
  190.4 2.3 copy.78
  192.7 3.9 convolution_convert_fusion.13
  198.1 4.4 fusion.88
  202.5 2.4 copy.81
  205.0 4.0 fusion.87
  209.0 2.5 copy.83
  211.5 8.5 %fusion.123 = (f32[16,512]{1,0:T(8,128)S(1)}, f32[16,512,512]{1,2,0:T(8,128)}) fusion(bf16[512,16,64]{0,2,1:T(8,128)(2,1)} %bitcast.218, bf16[512,16,64]{0,2,1:T(8,128)(2,1)S(1)} %bitcast.216, pred[512,512]{0,1:T(8,128)(4,1)} %fusion.97), kind=kOutput, calls=%fused_computation.180 | convolution fusion | flops 549445632 | bytes 19169280 | tf_op jit(solution)/shard_map/while/body/eval_jaxpr/qhe,khe->hqk/dot_general | solution.py:78
  219.9 8.3 %fusion.7 = f32[16,512]{1,0:T(8,128)S(1)} fusion(f32[16,512,512]{1,2,0:T(8,128)} %get-tuple-element.265, f32[16,512]{1,0:T(8,128)S(1)} %get-tuple-element.264), kind=kLoop, calls=%fused_computation.17 | loop fusion | flops 8380416 | bytes 16842752 | tf_op jit(solution)/shard_map/while/body/eval_jaxpr/reduce_sum | solution.py:94
  228.8 7.9 %fusion.73 = bf16[16,64,512]{2,1,0:T(8,128)(2,1)S(1)} fusion(bf16[512,16,64]{0,2,1:T(8,128)(2,1)S(1)} %bitcast.214, f32[16,512,512]{1,2,0:T(8,128)} %get-tuple-element.265, f32[16,512]{1,0:T(8,128)S(1)} %fusion.7, f32[16,512]{1,0:T(8,128)S(1)} %get-tuple-element.264), kind=kOutput, calls=%fused_computation.123 | convolution fusion | flops 549978112 | bytes 18939904 | tf_op jit(solution)/shard_map/while/body/eval_jaxpr/hqk,khe->qhe/dot_general | solution.py:96
  240.5 2.3 add_convert_fusion.3
  242.8 2.3 copy.82
  245.1 11.0 %multiply_reduce_fusion.2 = (f32[16,512]{1,0:T(8,128)S(1)}, f32[16,512,588]{1,2,0:T(8,128)}) fusion(bf16[512,16,64]{0,2,1:T(8,128)(2,1)} %bitcast.220, bf16[588,16,64]{0,2,1:T(8,128)(2,1)} %bitcast.210), kind=kOutput, calls=%fused_computation.16 | convolution fusion | flops 626188288 | bytes 21553152 | tf_op jit(solution)/shard_map/while/body/eval_jaxpr/qhe,khe->hqk/dot_general | solution.py:78
  256.0 9.8 %fusion.3 = f32[16,512]{1,0:T(8,128)S(1)} fusion(f32[16,512,588]{1,2,0:T(8,128)} %get-tuple-element.269, f32[16,512]{1,0:T(8,128)S(1)} %get-tuple-element.268), kind=kLoop, calls=%fused_computation.8 | loop fusion | flops 14442496 | bytes 19333120 | tf_op jit(solution)/shard_map/while/body/eval_jaxpr/reduce_sum | solution.py:94
  265.8 9.2 %fusion.74 = bf16[16,64,512]{2,1,0:T(8,128)(2,1)S(1)} fusion(bf16[588,16,64]{0,2,1:T(8,128)(2,1)} %bitcast.212, f32[16,512,588]{1,2,0:T(8,128)} %get-tuple-element.269, f32[16,512]{1,0:T(8,128)S(1)} %fusion.3, f32[16,512]{1,0:T(8,128)S(1)} %get-tuple-element.268), kind=kOutput, calls=%fused_computation.124 | convolution fusion | flops 636354560 | bytes 21585920 | tf_op jit(solution)/shard_map/while/body/eval_jaxpr/hqk,khe->qhe/dot_general | solution.py:96
  276.9 27.3 %fusion.24 = (bf16[512,4096]{1,0:T(8,128)(2,1)S(1)}, f32[512,4096]{1,0:T(8,128)}) fusion(f32[4096]{0:T(1024)S(1)} %slice_bitcast_fusion, bf16[1024,4096]{1,0:T(8,128)(2,1)} %bitcast.245, f32[512,1024]{1,0:T(8,128)S(1)} %get-tuple-element.271, f32[1024]{0:T(1024)S(1)} %add.233, f32[1024]{0:T(1024)S(1)} %mul.248, f32[512]{0:T(512)S(1)} %add_rsqrt_fusion, ...), kind=kOutput, calls=%fused_computation.30 | convolution fusion | flops 4436000768 | bytes 23097344 | tf_op jit(solution)/shard_map/dot_general | solution.py:20
  304.2 13.5 %convert_reduce_fusion = (f32[4096]{0:T(1024)S(1)}, bf16[512,4096]{1,0:T(8,128)(2,1)}) fusion(f32[512,4096]{1,0:T(8,128)} %get-tuple-element.286, f32[4096]{0:T(1024)S(1)} %slice_bitcast_fusion, bf16[4096,1024]{1,0:T(8,128)(2,1)} %bitcast.249, bf16[1,512,1024]{2,1,0:T(8,128)(2,1)S(1)} %copy-done.21), kind=kOutput, calls=%fused_computation.37 | convolution fusion | flops 4322226176 | bytes 22052864 | tf_op jit(solution)/shard_map/dot_general | solution.py:30
  317.7 8.9 %fusion.89 = bf16[1,512,1024]{2,1,0:T(8,128)(2,1)} fusion(f32[512,1024]{1,0:T(8,128)S(1)} %get-tuple-element.271, bf16[512,4096]{1,0:T(8,128)(2,1)S(1)} %get-tuple-element.285, bf16[4096,1024]{1,0:T(8,128)(2,1)} %bitcast.250, f32[1024]{0:T(1024)S(1)} %copy-done.44), kind=kOutput, calls=%fused_computation.134 | convolution fusion | flops 4296540160 | bytes 15732736 | tf_op jit(solution)/shard_map/dot_general | solution.py:20
  326.6 7.0 multiply_reduce_fusion.3
  336.0 2.3 convolution_convert_fusion.12
  340.3 4.7 convolution_convert_fusion.2
  345.0 9.6 %convert_reduce_fusion.3 = (f32[16,64]{1,0:T(8,128)S(1)}, bf16[16,64,588]{2,1,0:T(8,128)(2,1)}) fusion(bf16[512,16,64]{0,2,1:T(8,128)(2,1)S(1)} %bitcast.206, f32[16,512]{1,0:T(8,128)S(1)} %log_add_fusion.1, f32[16,512,588]{1,2,0:T(8,128)} %get-tuple-element.269), kind=kOutput, calls=%fused_computation.67 | convolution fusion | flops 632818688 | bytes 21557248 | tf_op jit(solution)/shard_map/while/body/eval_jaxpr/hqk,qhe->khe/dot_general | solution.py:111
  354.7 11.0 %convolution_convert_fusion.1 = bf16[1024,4096]{1,0:T(8,128)(2,1)} fusion(bf16[512,4096]{1,0:T(8,128)(2,1)} %get-tuple-element.284, f32[512,1024]{1,0:T(8,128)} %copy-done.6, f32[1024]{0:T(1024)S(1)} %add.233, f32[1024]{0:T(1024)S(1)} %mul.248, f32[512]{0:T(512)S(1)} %add_rsqrt_fusion, f32[512]{0:T(512)S(1)} %broadcast_multiply_fusion.6), kind=kOutput, calls=%fused_computation.57 | convolution fusion | flops 4301783040 | bytes 14692352 | tf_op jit(solution)/shard_map/dot_general | solution.py:24
  365.6 3.2 convolution_convert_fusion.8
  368.8 6.9 convolution_convert_fusion
  375.7 8.6 %fusion.130 = f32[16,512,588]{1,2,0:T(8,128)} fusion(bf16[512,16,64]{0,2,1:T(8,128)(2,1)S(1)} %bitcast.207, bf16[588,16,64]{0,2,1:T(8,128)(2,1)S(1)} %bitcast.213), kind=kOutput, calls=%fused_computation.183 | convolution fusion | flops 616562688 | bytes 21520384 | tf_op jit(solution)/shard_map/while/body/eval_jaxpr/qhe,khe->hqk/dot_general | solution.py:108
  384.2 27.5 %convert_reduce_fusion.5 = (f32[16,64]{1,0:T(8,128)S(1)}, bf16[16,64,512]{2,1,0:T(8,128)(2,1)}) fusion(bf16[588,16,64]{0,2,1:T(8,128)(2,1)} %bitcast.211, f32[16,512,588]{1,2,0:T(8,128)} %fusion.130, f32[16,512]{1,0:T(8,128)S(1)} %log_add_fusion.1, f32[16,512,588]{1,2,0:T(8,128)} %get-tuple-element.269), kind=kOutput, calls=%fused_computation.89 | convolution fusion | flops 661495360 | bytes 40824832 | tf_op jit(solution)/shard_map/while/body/eval_jaxpr/hqk,khe->qhe/dot_general | solution.py:116
  411.7 27.7 %fusion.70 = bf16[16,64,588]{2,1,0:T(8,128)(2,1)} fusion(bf16[512,16,64]{0,2,1:T(8,128)(2,1)} %bitcast.221, f32[16,512,588]{1,2,0:T(8,128)} %fusion.130, f32[16,512]{1,0:T(8,128)S(1)} %log_add_fusion.1, f32[16,512,588]{1,2,0:T(8,128)} %get-tuple-element.269), kind=kOutput, calls=%fused_computation.121 | convolution fusion | flops 660525632 | bytes 40820736 | tf_op jit(solution)/shard_map/while/body/eval_jaxpr/hqk,qhe->khe/dot_general | solution.py:119
  439.6 4.0 multiply_reduce_fusion.4
  444.9 2.9 convolution_convert_fusion.3
  450.0 3.8 fusion.134
  455.6 3.9 copy.89
  459.5 3.1 convolution_convert_fusion.9
  462.6 2.6 convolution_convert_fusion.4
  465.2 9.5 %convert_reduce_fusion.7 = (f32[16,64]{1,0:T(8,128)S(1)}, bf16[16,64,512]{2,1,0:T(8,128)(2,1)}) fusion(bf16[512,16,64]{0,2,1:T(8,128)(2,1)S(1)} %bitcast.204, f32[16,512,512]{1,2,0:T(8,128)} %get-tuple-element.265, f32[16,512]{1,0:T(8,128)S(1)} %copy-done.27), kind=kOutput, calls=%fused_computation.92 | convolution fusion | flops 546831360 | bytes 18911232 | tf_op jit(solution)/shard_map/while/body/eval_jaxpr/hqk,qhe->khe/dot_general | solution.py:111
  474.9 4.2 convolution_convert_fusion.5
  479.1 8.1 %fusion.131 = f32[16,512,512]{1,2,0:T(8,128)} fusion(bf16[512,16,64]{0,2,1:T(8,128)(2,1)S(1)} %bitcast.205, bf16[512,16,64]{0,2,1:T(8,128)(2,1)S(1)} %bitcast.215), kind=kOutput, calls=%fused_computation.184 | convolution fusion | flops 536870912 | bytes 18874368 | tf_op jit(solution)/shard_map/while/body/eval_jaxpr/qhe,khe->hqk/dot_general | solution.py:108
  487.1 24.0 %fusion.78 = bf16[16,64,512]{2,1,0:T(8,128)(2,1)} fusion(bf16[512,16,64]{0,2,1:T(8,128)(2,1)} %bitcast.219, f32[16,512,512]{1,2,0:T(8,128)} %fusion.131, f32[16,512,512]{1,2,0:T(8,128)} %get-tuple-element.265, f32[16,512]{1,0:T(8,128)S(1)} %copy-done.27), kind=kOutput, calls=%fused_computation.129 | convolution fusion | flops 566764032 | bytes 35684352 | tf_op jit(solution)/shard_map/while/body/eval_jaxpr/hqk,qhe->khe/dot_general | solution.py:119
  511.2 23.5 %convert_reduce_fusion.8 = (f32[16,64]{1,0:T(8,128)S(1)}, bf16[16,64,512]{2,1,0:T(8,128)(2,1)}) fusion(bf16[512,16,64]{0,2,1:T(8,128)(2,1)S(1)} %bitcast.217, f32[16,512,512]{1,2,0:T(8,128)} %fusion.131, f32[16,512,512]{1,2,0:T(8,128)} %get-tuple-element.265, f32[16,512]{1,0:T(8,128)S(1)} %copy-done.27), kind=kOutput, calls=%fused_computation.93 | convolution fusion | flops 567811584 | bytes 35688448 | tf_op jit(solution)/shard_map/while/body/eval_jaxpr/hqk,khe->qhe/dot_general | solution.py:116
  534.7 3.4 fusion.133
  540.0 2.1 fusion.60
  542.1 2.0 fusion.59
  545.2 4.2 convolution_convert_fusion.7
  549.4 2.9 convolution_convert_fusion.6
  552.3 160.1 %scatter_grads.1 = (f32[8,128]{1,0:T(8,128)}, f32[32,1024]{1,0:T(8,128)}, f32[32,1024]{1,0:T(8,128)}, f32[32,1024]{1,0:T(8,128)}, f32[32,1024]{1,0:T(8,128)}, /*...) custom-call(f32[2,2,2,2,2,8,128]{6,5,4,3,2,1,0:T(8,128)} %bitcast.24, ...), custom_call_target="tpu_custom_call" | custom-call | tf_op jit(solution)/shard_map/scatter_grads/pallas_call | solution.py:464
  (194 shorter events, 46.4 us)
Async XLA Ops:
  0.7 197.5 %copy-start = (bf16[1,588,1024]{2,1,0:T(8,128)(2,1)S(1)}, bf16[1,588,1024]{2,1,0:T(8,128)(2,1)}, u32[]{:S(2)}) copy-start(bf16[1,588,1024]{2,1,0:T(8,128)(2,1)} %param.30) | copy-start | bytes 3612676
  12.1 168.4 %copy-start.3 = (bf16[1,512,1024]{2,1,0:T(8,128)(2,1)S(1)}, bf16[1,512,1024]{2,1,0:T(8,128)(2,1)}, u32[]{:S(2)}) copy-start(bf16[1,512,1024]{2,1,0:T(8,128)(2,1)} %param.29) | copy-start | bytes 3145732
  13.7 179.1 %copy-start.28 = (f32[512]{0:T(512)}, f32[512]{0:T(512)S(1)}, u32[]{:S(2)}) copy-start(f32[512]{0:T(512)S(1)} %broadcast_multiply_fusion.8) | copy-start | bytes 6148
  15.3 177.4 %copy-start.36 = (f32[512]{0:T(512)}, f32[512]{0:T(512)S(1)}, u32[]{:S(2)}) copy-start(f32[512]{0:T(512)S(1)} %add_rsqrt_fusion.2) | copy-start | bytes 6148
  179.8 13.0 %copy-start.32 = (f32[1024]{0:T(1024)}, f32[1024]{0:T(1024)S(1)}, u32[]{:S(2)}) copy-start(f32[1024]{0:T(1024)S(1)} %mul.234) | copy-start | bytes 12292
  179.8 12.9 %copy-start.40 = (f32[1024]{0:T(1024)}, f32[1024]{0:T(1024)S(1)}, u32[]{:S(2)}) copy-start(f32[1024]{0:T(1024)S(1)} %add.205) | copy-start | bytes 12292
  180.0 58.6 %copy-start.34 = (f32[1024]{0:T(1024)}, f32[1024]{0:T(1024)S(1)}, u32[]{:S(2)}) copy-start(f32[1024]{0:T(1024)S(1)} %mul.241) | copy-start | bytes 12292
  180.1 58.4 %copy-start.42 = (f32[1024]{0:T(1024)}, f32[1024]{0:T(1024)S(1)}, u32[]{:S(2)}) copy-start(f32[1024]{0:T(1024)S(1)} %add.222) | copy-start | bytes 12292
  186.1 42.7 %copy-start.13 = (bf16[512,1024]{0,1:T(8,128)(2,1)}, bf16[512,1024]{0,1:T(8,128)(2,1)S(1)}, u32[]{:S(2)}) copy-start(bf16[512,1024]{0,1:T(8,128)(2,1)S(1)} %copy.77) | copy-start | bytes 3145732
  198.1 13.3 %copy-start.15 = (bf16[512,1024]{0,1:T(8,128)(2,1)}, bf16[512,1024]{0,1:T(8,128)(2,1)S(1)}, u32[]{:S(2)}) copy-start(bf16[512,1024]{0,1:T(8,128)(2,1)S(1)} %copy.79) | copy-start | bytes 3145732
  228.8 7.9 %copy-start.4 = (bf16[1,512,1024]{2,1,0:T(8,128)(2,1)S(1)}, bf16[1,512,1024]{2,1,0:T(8,128)(2,1)}, u32[]{:S(2)}) copy-start(bf16[1,512,1024]{2,1,0:T(8,128)(2,1)} %param.29) | copy-start | bytes 3145732
  228.8 7.9 %copy-start.17 = (bf16[2,2,2,2,2,32,1024]{6,5,4,3,2,1,0:T(8,128)(2,1)S(1)}, bf16[2,2,2,2,2,32,1024]{6,5,4,3,2,1,0:T(8,128)(2,1)}, u32[]{:S(2)}) copy-start(bf16[2,2,2,2,2,32,1024]{6,5,4,3,2,1,0:T(8,128)(2,1)} %get-tuple-element.149) | copy-start | bytes 6291460
  238.1 36.9 %copy-start.1 = (f32[512,1024]{1,0:T(8,128)}, f32[512,1024]{1,0:T(8,128)S(1)}, u32[]{:S(2)}) copy-start(f32[512,1024]{1,0:T(8,128)S(1)} %get-tuple-element.267) | copy-start | bytes 6291460
  265.8 9.3 %copy-start.49 = (bf16[2,2,2,2,2,32,1024]{6,5,4,3,2,1,0:T(8,128)(2,1)S(1)}, bf16[2,2,2,2,2,32,1024]{6,5,4,3,2,1,0:T(8,128)(2,1)}, u32[]{:S(2)}) copy-start(bf16[2,2,2,2,2,32,1024]{6,5,4,3,2,1,0:T(8,128)(2,1)} %get-tuple-element.153) | copy-start | bytes 6291460
  275.1 51.5 %slice-start = ((s8[8388608]{0:T(1024)(128)(4,1)}), s8[4194304]{0:T(1024)(128)(4,1)S(1)}, s32[]{:S(2)}) async-start(s8[8388608]{0:T(1024)(128)(4,1)} %bitcast.246), calls=%async_computation | async-start | bytes 8388608
  276.5 57.2 %copy-start.6 = (f32[512,1024]{1,0:T(8,128)}, f32[512,1024]{1,0:T(8,128)S(1)}, u32[]{:S(2)}) copy-start(f32[512,1024]{1,0:T(8,128)S(1)} %get-tuple-element.271) | copy-start | bytes 6291460
  276.8 27.3 %copy-start.21 = (bf16[1,512,1024]{2,1,0:T(8,128)(2,1)S(1)}, bf16[1,512,1024]{2,1,0:T(8,128)(2,1)}, u32[]{:S(2)}) copy-start(bf16[1,512,1024]{2,1,0:T(8,128)(2,1)} %param.33) | copy-start | bytes 3145732
  276.9 49.8 %slice-start.1 = ((s8[8388608]{0:T(1024)(128)(4,1)}), s8[4194304]{0:T(1024)(128)(4,1)S(1)}, s32[]{:S(2)}) async-start(s8[8388608]{0:T(1024)(128)(4,1)} %bitcast.246), calls=%async_computation.1 | async-start | bytes 8388608
  304.2 13.5 %copy-start.55 = (bf16[512,4096]{1,0:T(8,128)(2,1)}, bf16[512,4096]{1,0:T(8,128)(2,1)S(1)}, u32[]{:S(2)}) copy-start(bf16[512,4096]{1,0:T(8,128)(2,1)S(1)} %get-tuple-element.285) | copy-start | bytes 12582916
  304.2 13.5 %copy-start.44 = (f32[1024]{0:T(1024)S(1)}, f32[1024]{0:T(1024)}, u32[]{:S(2)}) copy-start(f32[1024]{0:T(1024)} %add.240) | copy-start | bytes 12292
  354.7 11.0 %copy-start.19 = (bf16[16,64,588]{2,1,0:T(8,128)(2,1)S(1)}, bf16[16,64,588]{2,1,0:T(8,128)(2,1)}, u32[]{:S(2)}) copy-start(bf16[16,64,588]{2,1,0:T(8,128)(2,1)} %get-tuple-element.282) | copy-start | bytes 3612676
  365.6 3.2 copy-start.56
  368.8 6.9 copy-start.12
  411.7 27.8 %copy-start.2 = (f32[512,1024]{1,0:T(8,128)S(1)}, f32[512,1024]{1,0:T(8,128)}, u32[]{:S(2)}) copy-start(f32[512,1024]{1,0:T(8,128)} %copy-done.1) | copy-start | bytes 6291460
  411.7 27.8 %copy-start.31 = (f32[512]{0:T(512)S(1)}, f32[512]{0:T(512)}, u32[]{:S(2)}) copy-start(f32[512]{0:T(512)} %copy-done.30) | copy-start | bytes 6148
  411.7 27.8 %copy-start.35 = (f32[1024]{0:T(1024)S(1)}, f32[1024]{0:T(1024)}, u32[]{:S(2)}) copy-start(f32[1024]{0:T(1024)} %copy-done.34) | copy-start | bytes 12292
  411.7 27.8 %copy-start.39 = (f32[512]{0:T(512)S(1)}, f32[512]{0:T(512)}, u32[]{:S(2)}) copy-start(f32[512]{0:T(512)} %copy-done.38) | copy-start | bytes 6148
  439.6 4.0 copy-start.8
  444.9 2.9 copy-start.9
  444.9 2.9 copy-start.18
  450.0 3.8 copy-start.20
  450.0 3.8 copy-start.47
  455.6 3.9 copy-start.50
  459.5 3.1 copy-start.10
  459.5 3.1 copy-start.24
  462.6 2.6 copy-start.27
  465.2 9.6 %copy-start.5 = (bf16[1,512,1024]{2,1,0:T(8,128)(2,1)S(1)}, bf16[1,512,1024]{2,1,0:T(8,128)(2,1)}, u32[]{:S(2)}) copy-start(bf16[1,512,1024]{2,1,0:T(8,128)(2,1)} %param.29) | copy-start | bytes 3145732
  465.2 9.6 %copy-start.29 = (f32[512]{0:T(512)S(1)}, f32[512]{0:T(512)}, u32[]{:S(2)}) copy-start(f32[512]{0:T(512)} %copy-done.28) | copy-start | bytes 6148
  465.2 9.6 %copy-start.33 = (f32[1024]{0:T(1024)S(1)}, f32[1024]{0:T(1024)}, u32[]{:S(2)}) copy-start(f32[1024]{0:T(1024)} %copy-done.32) | copy-start | bytes 12292
  465.2 9.6 %copy-start.37 = (f32[512]{0:T(512)S(1)}, f32[512]{0:T(512)}, u32[]{:S(2)}) copy-start(f32[512]{0:T(512)} %copy-done.36) | copy-start | bytes 6148
  465.2 9.6 %copy-start.41 = (f32[1024]{0:T(1024)S(1)}, f32[1024]{0:T(1024)}, u32[]{:S(2)}) copy-start(f32[1024]{0:T(1024)} %copy-done.40) | copy-start | bytes 12292
  474.9 4.2 copy-start.14
  487.1 24.0 %copy-start.16 = (bf16[512,1024]{0,1:T(8,128)(2,1)S(1)}, bf16[512,1024]{0,1:T(8,128)(2,1)}, u32[]{:S(2)}) copy-start(bf16[512,1024]{0,1:T(8,128)(2,1)} %copy-done.15) | copy-start | bytes 3145732
  534.7 3.4 copy-start.46
  534.7 3.4 copy-start.53
  545.2 4.2 copy-start.51
  712.3 15.7 %copy-start.26 = (f32[32,4096]{1,0:T(8,128)S(1)}, f32[32,4096]{1,0:T(8,128)}, u32[]{:S(2)}) copy-start(f32[32,4096]{1,0:T(8,128)} %get-tuple-element.339) | copy-start | bytes 1572868
  712.3 16.5 %copy-start.25 = (f32[128,1024]{1,0:T(8,128)S(1)}, f32[128,1024]{1,0:T(8,128)}, u32[]{:S(2)}) copy-start(f32[128,1024]{1,0:T(8,128)} %get-tuple-element.341) | copy-start | bytes 1572868
  (11 other events, 16.8 us)

commit v2 on v1

--- a/solution.py
+++ b/solution.py
@@ -11,7 +11,6 @@
 
 
 EPSILON = 1e-05
-MASKED = -1000000000.0
 ROOT_HALF = 0.7071067811865476
 INV_ROOT_TWO_PI = 0.3989422804014327
 
@@ -59,107 +58,185 @@
     ) + pre_act * INV_ROOT_TWO_PI * jnp.exp(-0.5 * pre_act * pre_act)
 
 
-def page_mask(length_now, row_count):
-    query_pos = lax.broadcasted_iota(jnp.int32, (row_count, row_count), 0)
-    key_pos = lax.broadcasted_iota(jnp.int32, (row_count, row_count), 1)
-    return (key_pos <= query_pos) & (key_pos < length_now)
-
-
-def split_heads(rows_in):
-    return rows_in.reshape(rows_in.shape[0], HEADS, rows_in.shape[1] // HEADS)
-
-
-def merge_heads(heads_in):
-    return heads_in.reshape(heads_in.shape[0], heads_in.shape[1] * heads_in.shape[2])
-
-
-def scores_of(query_rows, key_rows, mask_now):
-    head_size = query_rows.shape[1] // HEADS
-    raw_scores = jnp.einsum(
-        "qhe,khe->hqk",
-        split_heads(query_rows),
-        split_heads(key_rows),
-        preferred_element_type=jnp.float32,
-    )
-    scaled = raw_scores * head_size ** (-0.5)
-    if mask_now is None:
-        return scaled
-    return jnp.where(mask_now[None], scaled, MASKED)
-
-
-def attend_forward(query_rows, key_rows, value_rows, mask_now):
-    scaled = scores_of(query_rows, key_rows, mask_now)
-    row_top = jnp.max(scaled, axis=-1, keepdims=True)
-    expo_rows = jnp.exp(scaled - row_top)
-    row_total = jnp.sum(expo_rows, axis=-1, keepdims=True)
-    weights_low = (expo_rows / row_total).astype(jnp.bfloat16)
-    mixed = jnp.einsum(
-        "hqk,khe->qhe", weights_low, split_heads(value_rows), preferred_element_type=jnp.float32
-    )
-    return (merge_heads(mixed), row_top + jnp.log(row_total))
-
-
-def attend_backward(query_rows, key_rows, value_rows, mixed_grad, log_total, mask_now):
-    head_size = query_rows.shape[1] // HEADS
-    probs = jnp.exp(scores_of(query_rows, key_rows, mask_now) - log_total)
-    grad_heads = split_heads(mixed_grad)
-    query_heads = split_heads(query_rows)
-    key_heads = split_heads(key_rows)
-    prob_grad = jnp.einsum(
-        "qhe,khe->hqk", grad_heads, split_heads(value_rows), preferred_element_type=jnp.float32
-    )
-    value_grad = jnp.einsum(
-        "hqk,qhe->khe", probs.astype(jnp.bfloat16), grad_heads, preferred_element_type=jnp.float32
-    )
-    row_dot = jnp.sum(probs * prob_grad, axis=-1, keepdims=True)
-    score_grad = (probs * (prob_grad - row_dot) * head_size ** (-0.5)).astype(jnp.bfloat16)
-    query_grad = jnp.einsum(
-        "hqk,khe->qhe", score_grad, key_heads, preferred_element_type=jnp.float32
-    )
-    key_grad = jnp.einsum(
-        "hqk,qhe->khe", score_grad, query_heads, preferred_element_type=jnp.float32
-    )
-    return (merge_heads(query_grad), merge_heads(key_grad), merge_heads(value_grad))
-
-
-def self_forward(query_pages, key_pages, value_pages, lengths_now):
-
-    def one_page(page_item):
-        mask_now = page_mask(page_item[3], page_item[0].shape[0])
-        return attend_forward(page_item[0], page_item[1], page_item[2], mask_now)
-
-    return lax.map(one_page, (query_pages, key_pages, value_pages, lengths_now))
-
-
-def self_backward(query_pages, key_pages, value_pages, grad_pages, total_pages, lengths_now):
-
-    def one_page(page_item):
-        mask_now = page_mask(page_item[5], page_item[0].shape[0])
-        return attend_backward(
-            page_item[0], page_item[1], page_item[2], page_item[3], page_item[4], mask_now
-        )
-
-    return lax.map(
-        one_page, (query_pages, key_pages, value_pages, grad_pages, total_pages, lengths_now)
-    )
-
-
-def cross_forward(query_pages, key_pages, value_pages):
-
-    def one_page(page_item):
-        return attend_forward(page_item[0], page_item[1], page_item[2], None)
-
-    return lax.map(one_page, (query_pages, key_pages, value_pages))
-
-
-def cross_backward(query_pages, key_pages, value_pages, grad_pages, total_pages):
-
-    def one_page(page_item):
-        return attend_backward(
-            page_item[0], page_item[1], page_item[2], page_item[3], page_item[4], None
-        )
-
-    return lax.map(one_page, (query_pages, key_pages, value_pages, grad_pages, total_pages))
+LOG2E = 1.4426950408889634
+LN2 = 0.6931471805599453
+
+
+def dot_nn(a, b):
+    return jnp.dot(a, b, preferred_element_type=jnp.float32)
+
+
+def dot_nt(a, b):
+    return lax.dot_general(a, b, (((1,), (1,)), ((), ())), preferred_element_type=jnp.float32)
+
+
+def dot_tn(a, b):
+    return lax.dot_general(a, b, (((0,), (0,)), ((), ())), preferred_element_type=jnp.float32)
+
+
+def lane_half(x, head, half):
+    lane = lax.broadcasted_iota(jnp.int32, (1, x.shape[1]), 1)
+    keep = (lane < half) if head == 0 else (lane >= half)
+    return jnp.where(keep, x, jnp.zeros_like(x))
+
+
+def causal_spans(rows, chunk):
+    return [(start, chunk, start + chunk) for start in range(0, rows, chunk)]
+
+
+def limit_row(start, width, length):
+    pos = start + lax.broadcasted_iota(jnp.int32, (1, width), 1)
+    return jnp.minimum(pos, length - 1)
+
+
+def forward_pair(load_q, load_k, load_v, write, spans, length, scale):
+    for start, size, keys in spans:
+        q2 = load_q(start, size)
+        k2 = load_k(0, keys)
+        v2 = load_v(0, keys)
+        half = q2.shape[1] // 2
+        vt = v2.T
+        outs, totals = [], []
+        for head in (0, 1):
+            raw = dot_nt(k2, lane_half(q2, head, half))
+            if length is not None:
+                key_pos = lax.broadcasted_iota(jnp.int32, raw.shape, 0)
+                raw = jnp.where(key_pos <= limit_row(start, size, length), raw, -1e30)
+            top = jnp.max(raw, axis=0, keepdims=True)
+            expo = jnp.exp2((raw - top) * (scale * LOG2E))
+            total = jnp.sum(expo, axis=0, keepdims=True)
+            mixed = dot_nn(vt[head * half : (head + 1) * half], expo.astype(jnp.bfloat16))
+            outs.append(mixed / total)
+            totals.append(top * (scale * LOG2E) + jnp.log2(total))
+        write(start, size, jnp.concatenate(outs, axis=0).T.astype(jnp.bfloat16), totals)
+
+
+def fwd_kernel(masked, scale, chunk, *refs):
+    if masked:
+        len_ref, q_ref, k_ref, v_ref, a_ref, t_ref = refs
+        length = len_ref[pl.program_id(0)]
+    else:
+        q_ref, k_ref, v_ref, a_ref, t_ref = refs
+        length = None
+    rows, keys = q_ref.shape[1], k_ref.shape[1]
+    if masked:
+        spans = causal_spans(rows, chunk)
+    else:
+        spans = [(s, chunk, keys) for s in range(0, rows, chunk)]
+
+    def write(start, size, out, totals):
+        a_ref[0, pl.ds(start, size), :] = out
+        for head in (0, 1):
+            t_ref[0, 0, pl.ds(head, 1), pl.ds(start, size)] = totals[head]
+
+    forward_pair(
+        lambda s, n: q_ref[0, pl.ds(s, n), :],
+        lambda s, n: k_ref[0, pl.ds(s, n), :],
+        lambda s, n: v_ref[0, pl.ds(s, n), :],
+        write, spans, length, scale,
+    )
+
+
+def attend_fwd(q, k, v, lengths, heads, chunk=256):
+    pages, rows, width = q.shape
+    keys = k.shape[1]
+    head = width // heads
+    pairs = heads // 2
+    masked = lengths is not None
+    row_spec = pl.BlockSpec((1, rows, 2 * head), lambda p, h: (p, 0, h))
+    key_spec = pl.BlockSpec((1, keys, 2 * head), lambda p, h: (p, 0, h))
+    in_specs = [row_spec, key_spec, key_spec]
+    args = [q, k, v]
+    if masked:
+        in_specs = [pl.BlockSpec(memory_space=pltpu.SMEM)] + in_specs
+        args = [lengths] + args
+    return pl.pallas_call(
+        functools.partial(fwd_kernel, masked, head**-0.5, chunk),
+        grid=(pages, pairs),
+        in_specs=in_specs,
+        out_specs=[row_spec, pl.BlockSpec((1, 1, 2, rows), lambda p, h: (p, h, 0, 0))],
+        out_shape=[
+            jax.ShapeDtypeStruct(q.shape, jnp.bfloat16),
+            jax.ShapeDtypeStruct((pages, pairs, 2, rows), jnp.float32),
+        ],
+        compiler_params=pltpu.CompilerParams(vmem_limit_bytes=48 * 1024 * 1024),
+        name="attend_forward",
+    )(*args)
+
+
+def bwd_kernel(masked, scale, chunk, *refs):
+    if masked:
+        len_ref, q_ref, k_ref, v_ref, g_ref, t_ref, dq_ref, dk_ref, dv_ref, dk_acc, dv_acc = refs
+        length = len_ref[pl.program_id(0)]
+    else:
+        q_ref, k_ref, v_ref, g_ref, t_ref, dq_ref, dk_ref, dv_ref, dk_acc, dv_acc = refs
+        length = None
+    rows, keys_all = q_ref.shape[1], k_ref.shape[1]
+    if masked:
+        spans = causal_spans(rows, chunk)[::-1]
+    else:
+        spans = [(s, chunk, keys_all) for s in range(0, rows, chunk)]
+    half = q_ref.shape[2] // 2
+    for step, (start, size, keys) in enumerate(spans):
+        q2 = q_ref[0, pl.ds(start, size), :]
+        g2 = g_ref[0, pl.ds(start, size), :]
+        k2 = k_ref[0, pl.ds(0, keys), :]
+        v2 = v_ref[0, pl.ds(0, keys), :]
+        kt = k2.T
+        dk, dv, dqt = None, None, []
+        for head in (0, 1):
+            qm = lane_half(q2, head, half)
+            gm = lane_half(g2, head, half)
+            raw = dot_nt(k2, qm)
+            total = t_ref[0, 0, pl.ds(head, 1), pl.ds(start, size)]
+            probs = jnp.exp2(raw * (scale * LOG2E) - total)
+            if length is not None:
+                key_pos = lax.broadcasted_iota(jnp.int32, raw.shape, 0)
+                probs = jnp.where(key_pos <= limit_row(start, size, length), probs, 0.0)
+            grad = dot_nt(v2, gm)
+            part = probs * grad
+            dot_row = jnp.sum(part, axis=0, keepdims=True)
+            score = ((part - probs * dot_row) * scale).astype(jnp.bfloat16)
+            dvh = dot_nn(probs.astype(jnp.bfloat16), gm)
+            dkh = dot_nn(score, qm)
+            dv = dvh if dv is None else dv + dvh
+            dk = dkh if dk is None else dk + dkh
+            dqt.append(dot_nn(kt[head * half : (head + 1) * half], score))
+        dq_ref[0, pl.ds(start, size), :] = jnp.concatenate(dqt, axis=0).T.astype(jnp.bfloat16)
+        if step == 0:
+            dk_acc[pl.ds(0, keys), :] = dk
+            dv_acc[pl.ds(0, keys), :] = dv
+        else:
+            dk_acc[pl.ds(0, keys), :] += dk
+            dv_acc[pl.ds(0, keys), :] += dv
+    dk_ref[0] = dk_acc[...].astype(jnp.bfloat16)
+    dv_ref[0] = dv_acc[...].astype(jnp.bfloat16)
+
+
+def attend_bwd(q, k, v, g, totals, lengths, heads, chunk=256):
+    pages, rows, width = q.shape
+    keys = k.shape[1]
+    head = width // heads
+    pairs = heads // 2
+    masked = lengths is not None
+    row_spec = pl.BlockSpec((1, rows, 2 * head), lambda p, h: (p, 0, h))
+    key_spec = pl.BlockSpec((1, keys, 2 * head), lambda p, h: (p, 0, h))
+    total_spec = pl.BlockSpec((1, 1, 2, rows), lambda p, h: (p, h, 0, 0))
+    in_specs = [row_spec, key_spec, key_spec, row_spec, total_spec]
+    args = [q, k, v, g, totals]
+    if masked:
+        in_specs = [pl.BlockSpec(memory_space=pltpu.SMEM)] + in_specs
+        args = [lengths] + args
+    return pl.pallas_call(
+        functools.partial(bwd_kernel, masked, head**-0.5, chunk),
+        grid=(pages, pairs),
+        in_specs=in_specs,
+        out_specs=[row_spec, key_spec, key_spec],
+        out_shape=[jax.ShapeDtypeStruct(a.shape, jnp.bfloat16) for a in (q, k, v)],
+        scratch_shapes=[pltpu.VMEM((keys, 2 * head), jnp.float32)] * 2,
+        compiler_params=pltpu.CompilerParams(vmem_limit_bytes=48 * 1024 * 1024),
+        name="attend_backward",
+    )(*args)
 
 
 MESH_ID = pl.DeviceIdType.MESH
@@ -643,8 +720,10 @@
     query_pages = query_low.reshape(page_count, page_len, width)
     key_pages = key_low.reshape(page_count, page_len, width)
     value_pages = value_low.reshape(page_count, page_len, width)
-    self_mixed, self_total = self_forward(query_pages, key_pages, value_pages, lengths_now)
-    self_low = self_mixed.reshape(row_count, width).astype(jnp.bfloat16)
+    self_mixed, self_total = attend_fwd(
+        query_pages, key_pages, value_pages, lengths_now, HEADS, 512
+    )
+    self_low = self_mixed.reshape(row_count, width)
     after_self = inputs + product(self_low, out_mat) + out_vec.astype(jnp.float32)
     second_norm, second_unit, second_std = normalize(
         after_self, gain_two.astype(jnp.float32), shift_two.astype(jnp.float32)
@@ -660,8 +739,10 @@
     cquery_pages = cquery_low.reshape(page_count, page_len, width)
     ckey_pages = ckey_low.reshape(page_count, mem_len, width)
     cvalue_pages = cvalue_low.reshape(page_count, mem_len, width)
-    cross_mixed, cross_total = cross_forward(cquery_pages, ckey_pages, cvalue_pages)
-    cross_low = cross_mixed.reshape(row_count, width).astype(jnp.bfloat16)
+    cross_mixed, cross_total = attend_fwd(
+        cquery_pages, ckey_pages, cvalue_pages, None, HEADS, 512
+    )
+    cross_low = cross_mixed.reshape(row_count, width)
     after_cross = after_self + product(cross_low, cout_mat) + cout_vec.astype(jnp.float32)
     third_norm, third_unit, third_std = normalize(
         after_cross, gain_three.astype(jnp.float32), shift_three.astype(jnp.float32)
@@ -688,12 +769,12 @@
     cmix_grad = (
         product_nt(cout_grad, cout_mat).astype(jnp.bfloat16).reshape(page_count, page_len, width)
     )
-    cquery_grad, ckey_grad, cvalue_grad = cross_backward(
-        cquery_pages, ckey_pages, cvalue_pages, cmix_grad, cross_total
-    )
-    cquery_grad = cquery_grad.reshape(row_count, width).astype(jnp.bfloat16)
-    ckey_grad = ckey_grad.reshape(page_count * mem_len, width).astype(jnp.bfloat16)
-    cvalue_grad = cvalue_grad.reshape(page_count * mem_len, width).astype(jnp.bfloat16)
+    cquery_grad, ckey_grad, cvalue_grad = attend_bwd(
+        cquery_pages, ckey_pages, cvalue_pages, cmix_grad, cross_total, None, HEADS, 512
+    )
+    cquery_grad = cquery_grad.reshape(row_count, width)
+    ckey_grad = ckey_grad.reshape(page_count * mem_len, width)
+    cvalue_grad = cvalue_grad.reshape(page_count * mem_len, width)
     grad_cquery_mat = product_tn(second_low, cquery_grad).astype(jnp.bfloat16)
     grad_cquery_vec = jnp.sum(cquery_grad.astype(jnp.float32), axis=0)
     grad_ckey_mat = product_tn(mem_rows, ckey_grad).astype(jnp.bfloat16)
@@ -712,12 +793,12 @@
     smix_grad = (
         product_nt(sout_grad, out_mat).astype(jnp.bfloat16).reshape(page_count, page_len, width)
     )
-    query_grad, key_grad, value_grad = self_backward(
-        query_pages, key_pages, value_pages, smix_grad, self_total, lengths_now
-    )
-    query_grad = query_grad.reshape(row_count, width).astype(jnp.bfloat16)
-    key_grad = key_grad.reshape(row_count, width).astype(jnp.bfloat16)
-    value_grad = value_grad.reshape(row_count, width).astype(jnp.bfloat16)
+    query_grad, key_grad, value_grad = attend_bwd(
+        query_pages, key_pages, value_pages, smix_grad, self_total, lengths_now, HEADS, 256
+    )
+    query_grad = query_grad.reshape(row_count, width)
+    key_grad = key_grad.reshape(row_count, width)
+    value_grad = value_grad.reshape(row_count, width)
     grad_query_mat = product_tn(first_low, query_grad).astype(jnp.bfloat16)
     grad_query_vec = jnp.sum(query_grad.astype(jnp.float32), axis=0)
     grad_key_mat = product_tn(first_low, key_grad).astype(jnp.bfloat16)

time: 734 us -> 592 us (0.81)
  matrix products: 323 us -> 127 us
  Pallas kernels: 322 us -> 385 us
  other arithmetic: 27.7 us -> 11.3 us
    dot_general x12 -> x0, matrix products: 175 us -> none  [the longest x2 51.8 us: attend_backward(): jnp.einsum('hqk,qhe->khe', score_grad, query_heads, preferred_element_typ...]
    pallas_call x0 -> x4, Pallas kernels: none -> 63.3 us  [the longest x2 38.3 us: attend_bwd(): pl.pallas_call(functools.partial(bwd_kernel, masked, head ** (-0.5), chun...]
    reduce_sum x2 -> x4, other arithmetic: 18 us -> 1.94 us  [the longest x1 0.77 us: on_device(): grad_query_vec = jnp.sum(query_grad.astype(jnp.float32), axis=0)]
    convert_element_type x8 -> x0, local copies, waits for them, and re-layouts: 15 us -> none  [the longest x1 2.46 us: on_device(): ckey_low = product(mem_rows, ckey_mat).astype(jnp.bfloat16)]
    dot_general x10, matrix products: 61.8 us -> 48.6 us  [product(): return jnp.dot(left, right, preferred_element_type=jnp.float32)]
    reshape x13, local copies, waits for them, and re-layouts: 0.91 us -> 13.9 us  [spread(): grads[i].reshape(devices, -1)]
    dot_general x10, matrix products: 45.5 us -> 37.3 us  [product_tn(): lax.dot_general(left, right, (((0,), (0,)), ((), ())), preferred_element_...]
    unnamed x132 -> x172, local copies, waits for them, and re-layouts: 24.2 us -> 30.9 us
where the time goes in v2:
time: 592 us; the launch traced here: 587 us
  Pallas kernels  385 us (65%)
  matrix products  127 us (21%)
  local copies, waits for them, and re-layouts  60.1 us (10%)
  other arithmetic  11.3 us (2%)
    pallas_call x1, Pallas kernels, gather_all(): pl.pallas_call(functools.partial(gather_kernel, bits, units, orders, plan...  162 us
    pallas_call x1, Pallas kernels, scatter_all(): pl.pallas_call(functools.partial(scatter_kernel, bits, units, orders, pla...  160 us
    dot_general x10, matrix products, product(): return jnp.dot(left, right, preferred_element_type=jnp.float32)  48.6 us
    dot_general x10, matrix products, product_nt(): lax.dot_general(left, right, (((1,), (1,)), ((), ())), preferred_element_...  40.8 us
    pallas_call x2, Pallas kernels, attend_bwd(): pl.pallas_call(functools.partial(bwd_kernel, masked, head ** (-0.5), chun...  38.3 us
    dot_general x10, matrix products, product_tn(): lax.dot_general(left, right, (((0,), (0,)), ((), ())), preferred_element_...  37.3 us
    unnamed x172, local copies, waits for them, and re-layouts  30.9 us
    pallas_call x2, Pallas kernels, attend_fwd(): pl.pallas_call(functools.partial(fwd_kernel, masked, head ** (-0.5), chun...  25.1 us

profile of v2, /device:TPU:0, one launch (start us, length us, event | category | flops | bytes accessed | tf_op | source)
XLA Modules:
  0.0 586.6 jit_solution(2223159104094296709)
XLA Ops:
  2.1 9.4 %concatenate.7 = bf16[544]{0:T(1024)(128)(2,1)S(1)} concatenate(bf16[32]{0:T(256)(128)(2,1)} %param.34, bf16[32]{0:T(256)(128)(2,1)} %param.35, bf16[32]{0:T(256)(128)(2,1)} %param.37, bf16[32]{0:T(256)(128)(2,1)} %param.40, bf16[32]{0:T(256)(128)(2,1)} %param.42, bf16[32]{0:T(256)(128)(2,1)} %param.43, bf16[32]{0:T(256)(128)(2,1)} %param.44, bf16[32]{0:T(256)(128)(2,1)} %param.46, ...), dimensions={0} | concatenate | bytes 2176 | tf_op jit(solution)/shard_map/concatenate | solution.py:577
  12.1 1.5 convert_reduce_fusion.1
  13.7 1.6 fusion.28
  15.3 161.9 %gather_weights.1 = (f32[2,2,2,2,2,8,128]{6,5,4,3,2,1,0:T(8,128)}, bf16[2,2,2,2,2,32,1024]{6,5,4,3,2,1,0:T(8,128)(2,1)}, bf16[2,2,2,2,2,32,1024]{6,5,4,3,2,1,0:T...) custom-call(f32[8,128]{1,0:T(8,128)} %bitcast_convert_fusion.refs_0_, ...), custom_call_target="tpu_custom_call" | custom-call | tf_op jit(solution)/shard_map/gather_weights/pallas_call | solution.py:397
  179.2 3.1 fusion.39.refs_1_
  185.3 12.2 %attend_forward.2 = (bf16[1,512,1024]{2,1,0:T(8,128)(2,1)S(1)}, f32[1,8,2,512]{3,2,1,0:T(2,128)S(1)}) custom-call(s32[1]{0:T(128)S(6)} %select_n.4.refs_0_, bf16[1,512,1024]{2,1,0:T(8,128)(2,1)S(1)} %fusion.39.refs_1_, bf16[1,512,1024]{2,1,0:T(8,128)(2,1)S(1)} %fusion.36.refs_2_, bf16[1,512,1024]{2,1,0:T(8,128)(2,1)S(1)} %fusion.40.refs_3_), custom_call_target="tpu_custom_call" | custom-call | tf_op jit(solution)/shard_map/attend_forward/pallas_call | solution.py:153
  197.5 1.4 fusion.35.refs_2_
  199.5 1.4 fusion.34.refs_1_
  206.6 12.8 %attend_forward.3 = (bf16[1,512,1024]{2,1,0:T(8,128)(2,1)S(1)}, f32[1,8,2,512]{3,2,1,0:T(2,128)S(1)}) custom-call(bf16[1,512,1024]{2,1,0:T(8,128)(2,1)S(1)} %fusion.41.refs_0_, bf16[1,588,1024]{2,1,0:T(8,128)(2,1)S(1)} %fusion.34.refs_1_, bf16[1,588,1024]{2,1,0:T(8,128)(2,1)S(1)} %fusion.35.refs_2_), custom_call_target="tpu_custom_call" | custom-call | tf_op jit(solution)/shard_map/attend_forward/pallas_call | solution.py:153
  219.5 3.3 fusion.84
  224.0 25.1 %fusion.2 = (bf16[512,4096]{1,0:T(8,128)(2,1)S(1)}, f32[512,4096]{1,0:T(8,128)}) fusion(f32[4096]{0:T(1024)S(1)} %slice_bitcast_fusion, bf16[1024,4096]{1,0:T(8,128)(2,1)S(1)} %bitcast.222, f32[512,1024]{1,0:T(8,128)S(1)} %get-tuple-element.164, f32[1024]{0:T(1024)S(1)} %add.207, f32[1024]{0:T(1024)S(1)} %mul.210, f32[512]{0:T(512)S(1)} %add_rsqrt_fusion, ...), kind=kOutput, calls=%fused_computation.4 | convolution fusion | flops 4436000768 | bytes 23097344 | tf_op jit(solution)/shard_map/dot_general | solution.py:19
  249.2 14.6 %convert_reduce_fusion = (f32[4096]{0:T(1024)}, bf16[512,4096]{1,0:T(8,128)(2,1)}) fusion(f32[512,4096]{1,0:T(8,128)} %get-tuple-element.171, f32[4096]{0:T(1024)S(1)} %slice_bitcast_fusion, bf16[4096,1024]{1,0:T(8,128)(2,1)} %bitcast.226, bf16[1,512,1024]{2,1,0:T(8,128)(2,1)S(1)} %copy-done.28), kind=kOutput, calls=%fused_computation.10 | convolution fusion | flops 4322226176 | bytes 22052864 | tf_op jit(solution)/shard_map/dot_general | solution.py:29
  263.8 8.9 %fusion.42 = bf16[1,512,1024]{2,1,0:T(8,128)(2,1)} fusion(f32[512,1024]{1,0:T(8,128)S(1)} %get-tuple-element.164, bf16[512,4096]{1,0:T(8,128)(2,1)S(1)} %get-tuple-element.170, bf16[4096,1024]{1,0:T(8,128)(2,1)} %bitcast.227, f32[1024]{0:T(1024)S(1)} %add.214), kind=kOutput, calls=%fused_computation.100 | convolution fusion | flops 4296540160 | bytes 15732736 | tf_op jit(solution)/shard_map/dot_general | solution.py:19
  272.7 7.6 %multiply_reduce_fusion = (f32[1024]{0:T(1024)}, f32[512]{0:T(512)S(1)}, f32[512]{0:T(512)S(1)}, f32[1024]{0:T(1024)}, f32[512,1024]{1,0:T(8,128)S(1)}) fusion(f32[512,1024]{1,0:T(8,128)S(1)} %get-tuple-element.164, f32[512]{0:T(512)S(1)} %add_rsqrt_fusion, f32[512]{0:T(512)S(1)} %broadcast_multiply_fusion.6, f32[1024]{0:T(1024)S(1)} %mul.210, ...), kind=kOutput, calls=%fused_computation.55 | convolution fusion | flops 4299682816 | bytes 16797696 | tf_op jit(solution)/shard_map/dot_general | solution.py:29
  280.4 1.6 convert_reduce_fusion.4
  284.5 20.6 %attend_backward.2 = (bf16[1,512,1024]{2,1,0:T(8,128)(2,1)S(1)}, bf16[1,588,1024]{2,1,0:T(8,128)(2,1)S(1)}, bf16[1,588,1024]{2,1,0:T(8,128)(2,1)S(1)}) custom-call(bf16[1,512,1024]{2,1,0:T(8,128)(2,1)S(1)} %fusion.41.refs_0_, bf16[1,588,1024]{2,1,0:T(8,128)(2,1)} %copy-done.2, bf16[1,588,1024]{2,1,0:T(8,128)(2,1)} %copy-done.1, ...), custom_call_target="tpu_custom_call" | custom-call | tf_op jit(solution)/shard_map/attend_backward/pallas_call | solution.py:230
  308.5 1.4 reshape.516
  309.9 5.1 multiply_reduce_fusion.1
  316.3 2.8 convolution_convert_fusion.3
  319.1 2.6 convolution_convert_fusion.2
  321.7 2.3 fusion.38.refs_4_
  324.0 17.7 %attend_backward.3 = (bf16[1,512,1024]{2,1,0:T(8,128)(2,1)S(1)}, bf16[1,512,1024]{2,1,0:T(8,128)(2,1)S(1)}, bf16[1,512,1024]{2,1,0:T(8,128)(2,1)S(1)}) custom-call(s32[1]{0:T(128)S(6)} %select_n.4.refs_0_, bf16[1,512,1024]{2,1,0:T(8,128)(2,1)S(1)} %fusion.39.refs_1_, bf16[1,512,1024]{2,1,0:T(8,128)(2,1)S(1)} %copy-done.5, bf16[1,512,1024]{2,1,0:T(8,128)(2,1)} %copy-done.3, ...), custom_call_target="tpu_custom_call" | custom-call | tf_op jit(solution)/shard_map/attend_backward/pallas_call | solution.py:230
  343.0 1.4 copy-done.65
  346.3 2.4 fusion.27
  348.8 2.0 fusion.26
  350.8 2.6 convolution_convert_fusion.4
  355.7 1.4 reshape.508
  366.6 1.6 concatenate.8
  369.8 3.6 fusion.46
  373.4 1.5 add_bitcast_fusion
  374.9 3.9 copy.56
  378.8 3.5 convolution_convert_fusion.8
  382.3 3.3 convolution_convert_fusion.9
  385.6 2.8 convolution_convert_fusion.5
  388.4 2.9 convolution_convert_fusion.7
  391.3 2.8 convolution_convert_fusion.6
  394.8 7.3 %convolution_convert_fusion.1 = bf16[1024,4096]{1,0:T(8,128)(2,1)} fusion(bf16[512,4096]{1,0:T(8,128)(2,1)S(1)} %copy-done.74, f32[512,1024]{1,0:T(8,128)S(1)} %copy-done.23, f32[1024]{0:T(1024)S(1)} %copy-done.57, f32[1024]{0:T(1024)S(1)} %copy-done.44, f32[512]{0:T(512)S(1)} %copy-done.48, f32[512]{0:T(512)S(1)} %copy-done.34), kind=kOutput, calls=%fused_computation.27 | convolution fusion | flops 4301783040 | bytes 14692352 | tf_op jit(solution)/shard_map/dot_general | solution.py:23
  402.1 6.8 %convolution_convert_fusion = bf16[4096,1024]{1,0:T(8,128)(2,1)} fusion(bf16[512,4096]{1,0:T(8,128)(2,1)S(1)} %copy-done.73, bf16[1,512,1024]{2,1,0:T(8,128)(2,1)S(1)} %copy-done.29), kind=kOutput, calls=%fused_computation.26 | convolution fusion | flops 4299161600 | bytes 13631488 | tf_op jit(solution)/shard_map/dot_general | solution.py:23
  408.9 159.9 %scatter_grads.1 = (f32[8,128]{1,0:T(8,128)}, f32[32,1024]{1,0:T(8,128)}, f32[32,1024]{1,0:T(8,128)}, f32[32,1024]{1,0:T(8,128)}, f32[32,1024]{1,0:T(8,128)}, /*...) custom-call(f32[2,2,2,2,2,8,128]{6,5,4,3,2,1,0:T(8,128)} %bitcast.21, ...), custom_call_target="tpu_custom_call" | custom-call | tf_op jit(solution)/shard_map/scatter_grads/pallas_call | solution.py:541
  570.2 1.8 fusion.82
  572.0 1.6 copy.73
  573.6 1.6 copy.74
  575.1 1.6 copy.75
  576.7 1.6 copy.76
  578.3 1.6 copy.77
  579.8 1.6 copy.78
  581.4 1.6 copy.79
  583.0 1.6 copy.80
  (217 shorter events, 40.5 us)
Async XLA Ops:
  0.7 196.8 %copy-start = (bf16[1,588,1024]{2,1,0:T(8,128)(2,1)S(1)}, bf16[1,588,1024]{2,1,0:T(8,128)(2,1)}, u32[]{:S(2)}) copy-start(bf16[1,588,1024]{2,1,0:T(8,128)(2,1)} %param.30) | copy-start | bytes 3612676
  12.1 167.1 %copy-start.20 = (bf16[1,512,1024]{2,1,0:T(8,128)(2,1)S(1)}, bf16[1,512,1024]{2,1,0:T(8,128)(2,1)}, u32[]{:S(2)}) copy-start(bf16[1,512,1024]{2,1,0:T(8,128)(2,1)} %param.29) | copy-start | bytes 3145732
  13.6 170.0 %copy-start.35 = (f32[512]{0:T(512)}, f32[512]{0:T(512)S(1)}, u32[]{:S(2)}) copy-start(f32[512]{0:T(512)S(1)} %broadcast_multiply_fusion.8) | copy-start | bytes 6148
  15.3 168.4 %copy-start.49 = (f32[512]{0:T(512)}, f32[512]{0:T(512)S(1)}, u32[]{:S(2)}) copy-start(f32[512]{0:T(512)S(1)} %add_rsqrt_fusion.2) | copy-start | bytes 6148
  178.4 5.2 copy-start.40
  178.5 5.2 copy-start.54
  178.6 101.8 %copy-start.43 = (f32[1024]{0:T(1024)}, f32[1024]{0:T(1024)S(1)}, u32[]{:S(2)}) copy-start(f32[1024]{0:T(1024)S(1)} %mul.210) | copy-start | bytes 12292
  178.7 24.6 %copy-start.45 = (f32[1024]{0:T(1024)}, f32[1024]{0:T(1024)S(1)}, u32[]{:S(2)}) copy-start(f32[1024]{0:T(1024)S(1)} %mul.204) | copy-start | bytes 12292
  178.7 44.5 %copy-start.56 = (f32[1024]{0:T(1024)}, f32[1024]{0:T(1024)S(1)}, u32[]{:S(2)}) copy-start(f32[1024]{0:T(1024)S(1)} %add.207) | copy-start | bytes 12292
  178.8 24.5 %copy-start.58 = (f32[1024]{0:T(1024)}, f32[1024]{0:T(1024)S(1)}, u32[]{:S(2)}) copy-start(f32[1024]{0:T(1024)S(1)} %add.193) | copy-start | bytes 12292
  179.2 3.1 copy-start.63
  185.2 13.7 %copy-start.4 = (bf16[1,512,1024]{2,1,0:T(8,128)(2,1)}, bf16[1,512,1024]{2,1,0:T(8,128)(2,1)S(1)}, u32[]{:S(2)}) copy-start(bf16[1,512,1024]{2,1,0:T(8,128)(2,1)S(1)} %fusion.36.refs_2_) | copy-start | bytes 3145732
  185.2 12.3 %copy-start.60 = (bf16[2,2,2,2,2,32,1024]{6,5,4,3,2,1,0:T(8,128)(2,1)S(1)}, bf16[2,2,2,2,2,32,1024]{6,5,4,3,2,1,0:T(8,128)(2,1)}, u32[]{:S(2)}) copy-start(bf16[2,2,2,2,2,32,1024]{6,5,4,3,2,1,0:T(8,128)(2,1)} %get-tuple-element.67) | copy-start | bytes 6291460
  197.5 3.4 copy-start.14
  199.5 7.1 %copy-start.1 = (bf16[1,588,1024]{2,1,0:T(8,128)(2,1)}, bf16[1,588,1024]{2,1,0:T(8,128)(2,1)S(1)}, u32[]{:S(2)}) copy-start(bf16[1,588,1024]{2,1,0:T(8,128)(2,1)S(1)} %fusion.35.refs_2_) | copy-start | bytes 3612676
  201.5 5.1 copy-start.2
  202.9 16.6 %copy-start.26 = (f32[512,1024]{1,0:T(8,128)}, f32[512,1024]{1,0:T(8,128)S(1)}, u32[]{:S(2)}) copy-start(f32[512,1024]{1,0:T(8,128)S(1)} %get-tuple-element.162) | copy-start | bytes 6291460
  219.4 3.4 copy-start.16
  219.4 3.8 slice-start
  219.5 4.6 slice-start.1
  219.5 53.3 %slice-start.2 = ((s8[8388608]{0:T(1024)(128)(4,1)}), s8[4194304]{0:T(1024)(128)(4,1)S(1)}, s32[]{:S(2)}) async-start(s8[8388608]{0:T(1024)(128)(4,1)} %bitcast.223), calls=%async_computation.2 | async-start | bytes 8388608
  222.8 57.5 %copy-start.22 = (f32[512,1024]{1,0:T(8,128)}, f32[512,1024]{1,0:T(8,128)S(1)}, u32[]{:S(2)}) copy-start(f32[512,1024]{1,0:T(8,128)S(1)} %get-tuple-element.164) | copy-start | bytes 6291460
  222.8 57.5 %copy-start.33 = (f32[512]{0:T(512)}, f32[512]{0:T(512)S(1)}, u32[]{:S(2)}) copy-start(f32[512]{0:T(512)S(1)} %broadcast_multiply_fusion.6) | copy-start | bytes 6148
  224.0 56.3 %copy-start.47 = (f32[512]{0:T(512)}, f32[512]{0:T(512)S(1)}, u32[]{:S(2)}) copy-start(f32[512]{0:T(512)S(1)} %add_rsqrt_fusion) | copy-start | bytes 6148
  224.0 25.2 %copy-start.28 = (bf16[1,512,1024]{2,1,0:T(8,128)(2,1)S(1)}, bf16[1,512,1024]{2,1,0:T(8,128)(2,1)}, u32[]{:S(2)}) copy-start(bf16[1,512,1024]{2,1,0:T(8,128)(2,1)} %param.33) | copy-start | bytes 3145732
  224.0 48.7 %slice-start.3 = ((s8[8388608]{0:T(1024)(128)(4,1)}), s8[4194304]{0:T(1024)(128)(4,1)S(1)}, s32[]{:S(2)}) async-start(s8[8388608]{0:T(1024)(128)(4,1)} %bitcast.223), calls=%async_computation.3 | async-start | bytes 8388608
  249.2 14.6 %copy-start.72 = (bf16[512,4096]{1,0:T(8,128)(2,1)}, bf16[512,4096]{1,0:T(8,128)(2,1)S(1)}, u32[]{:S(2)}) copy-start(bf16[512,4096]{1,0:T(8,128)(2,1)S(1)} %get-tuple-element.170) | copy-start | bytes 12582916
  309.9 5.1 copy-start.25
  309.9 5.1 copy-start.27
  309.9 5.1 copy-start.39
  309.9 5.1 copy-start.46
  309.9 5.1 copy-start.53
  324.0 17.7 %copy-start.67 = (bf16[2,2,2,2,2,32,1024]{6,5,4,3,2,1,0:T(8,128)(2,1)S(1)}, bf16[2,2,2,2,2,32,1024]{6,5,4,3,2,1,0:T(8,128)(2,1)}, u32[]{:S(2)}) copy-start(bf16[2,2,2,2,2,32,1024]{6,5,4,3,2,1,0:T(8,128)(2,1)} %get-tuple-element.61) | copy-start | bytes 6291460
  341.7 11.8 %copy-start.6 = (bf16[1,512,1024]{2,1,0:T(8,128)(2,1)}, bf16[1,512,1024]{2,1,0:T(8,128)(2,1)S(1)}, u32[]{:S(2)}) copy-start(bf16[1,512,1024]{2,1,0:T(8,128)(2,1)S(1)} %get-tuple-element.75) | copy-start | bytes 3145732
  341.7 12.5 %copy-start.8 = (bf16[1,512,1024]{2,1,0:T(8,128)(2,1)}, bf16[1,512,1024]{2,1,0:T(8,128)(2,1)S(1)}, u32[]{:S(2)}) copy-start(bf16[1,512,1024]{2,1,0:T(8,128)(2,1)S(1)} %get-tuple-element.77) | copy-start | bytes 3145732
  353.4 13.2 %copy-start.32 = (f32[32,32]{1,0:T(8,128)S(1)}, f32[32,32]{1,0:T(8,128)}, u32[]{:S(2)}) copy-start(f32[32,32]{1,0:T(8,128)} %reshape.516) | copy-start | bytes 12292
  369.8 3.6 copy-start.61
  378.8 3.5 copy-start.13
  382.3 3.3 copy-start.9
  382.3 3.3 copy-start.37
  382.3 3.3 copy-start.42
  382.3 3.3 copy-start.51
  382.3 3.3 copy-start.55
  391.2 3.6 copy-start.74
  394.8 7.3 %copy-start.29 = (bf16[1,512,1024]{2,1,0:T(8,128)(2,1)S(1)}, bf16[1,512,1024]{2,1,0:T(8,128)(2,1)}, u32[]{:S(2)}) copy-start(bf16[1,512,1024]{2,1,0:T(8,128)(2,1)} %param.33) | copy-start | bytes 3145732
  394.8 7.3 %copy-start.73 = (bf16[512,4096]{1,0:T(8,128)(2,1)S(1)}, bf16[512,4096]{1,0:T(8,128)(2,1)}, u32[]{:S(2)}) copy-start(bf16[512,4096]{1,0:T(8,128)(2,1)} %copy-done.72) | copy-start | bytes 12582916
  568.8 15.7 %copy-start.31 = (f32[32,4096]{1,0:T(8,128)S(1)}, f32[32,4096]{1,0:T(8,128)}, u32[]{:S(2)}) copy-start(f32[32,4096]{1,0:T(8,128)} %get-tuple-element.224) | copy-start | bytes 1572868
  568.9 16.5 %copy-start.30 = (f32[128,1024]{1,0:T(8,128)S(1)}, f32[128,1024]{1,0:T(8,128)}, u32[]{:S(2)}) copy-start(f32[128,1024]{1,0:T(8,128)} %get-tuple-element.226) | copy-start | bytes 1572868
  (31 other events, 60.4 us)

commit v3 on v2

--- a/solution.py
+++ b/solution.py
@@ -50,12 +50,6 @@
         jnp.sum(grad_norm * unit_rows, axis=0),
         jnp.sum(grad_norm, axis=0),
     )
-
-
-def gelu_slope(pre_act):
-    return 0.5 * (
-        1.0 + jax.scipy.special.erf(pre_act * ROOT_HALF)
-    ) + pre_act * INV_ROOT_TWO_PI * jnp.exp(-0.5 * pre_act * pre_act)
 
 
 LOG2E = 1.4426950408889634
@@ -244,8 +238,6 @@
 CORE_RATE = 500e3
 LINK_RATE = 96e3
 HOP = 2.5
-VEC_ROWS = 8
-VEC_LANES = 128
 
 
 def bit_table(mesh):
@@ -286,6 +278,7 @@
     ready = [(0.0, unit, 0) for unit in range(len(orders))]
     free = {}
     plan = []
+    arrive = {}
     while ready:
         choices = []
         for when, unit, stage in ready:
@@ -300,12 +293,14 @@
         for link, took in loads.items():
             free[link] = start + took
         plan.append((start, unit, stage))
+        after = start + max(loads.values()) + HOP
+        if add_rate:
+            after += sizes[unit] * scale / add_rate
         if stage + 1 < count:
-            after = start + max(loads.values()) + HOP
-            if add_rate:
-                after += sizes[unit] * scale / add_rate
             ready.append((after, unit, stage + 1))
-    return [(unit, stage) for _, unit, stage in sorted(plan)]
+        else:
+            arrive[unit] = after
+    return sorted(plan), arrive
 
 
 def my_bits(bits):
@@ -333,84 +328,6 @@
     array, rows, cols = unit
     block = blocks[array]
     return (len(range(*rows.indices(block[0]))), len(range(*cols.indices(block[1]))))
-
-
-def gather_kernel(bits, units, orders, plan, n_arrays, *refs):
-    count = len(bits)
-    sources = refs[:n_arrays]
-    targets = refs[n_arrays : 2 * n_arrays]
-    send_sem, recv_sem, own_sem = refs[2 * n_arrays :]
-    mine = my_bits(bits)
-    own = [
-        pltpu.make_async_copy(sources[i], targets[i].at[tuple(mine)], own_sem.at[i])
-        for i in range(n_arrays)
-    ]
-    for copy in own:
-        copy.start()
-    greet(bits, mine)
-
-    def message(unit, stage):
-        array, rows, cols = units[unit]
-        order = orders[unit]
-        where = tuple(slice(None) if b in order[:stage] else mine[b] for b in range(count))
-        place = targets[array].at[where + (rows, cols)]
-        source = sources[array].at[rows, cols] if stage == 0 else place
-        return pltpu.make_async_remote_copy(
-            src_ref=source,
-            dst_ref=place,
-            send_sem=send_sem.at[unit, stage],
-            recv_sem=recv_sem.at[unit, stage],
-            device_id=partner(bits, mine, order[stage]),
-            device_id_type=MESH_ID,
-        )
-
-    settled = set()
-    for unit, stage in plan:
-        array = units[unit][0]
-        if stage > 0:
-            if array not in settled:
-                settled.add(array)
-                own[array].wait()
-            message(unit, stage - 1).wait_recv()
-        message(unit, stage).start()
-    for array in range(n_arrays):
-        if array not in settled:
-            own[array].wait()
-    for unit in range(len(units)):
-        message(unit, count - 1).wait_recv()
-    for unit in range(len(units)):
-        for stage in range(count):
-            message(unit, stage).wait_send()
-
-
-def gather_all(mesh, shards, units, collective_id):
-    bits = bit_table(mesh)
-    routes = route_orders(bits)
-    orders = [routes[u % 2] for u in range(len(units))]
-    shapes = [unit_shape([s.shape for s in shards], unit) for unit in units]
-    sizes = [
-        shape[0] * shape[1] * shards[unit[0]].dtype.itemsize for shape, unit in zip(shapes, units)
-    ]
-    plan = plan_sends(bits, orders, sizes, True, None)
-    n = len(shards)
-    sems = (len(units), len(bits))
-    return pl.pallas_call(
-        functools.partial(gather_kernel, bits, units, orders, plan, n),
-        out_shape=[
-            jax.ShapeDtypeStruct((2,) * len(bits) + s.shape, s.dtype) for s in shards
-        ],
-        in_specs=[pl.BlockSpec(memory_space=pltpu.HBM)] * n,
-        out_specs=[pl.BlockSpec(memory_space=pltpu.HBM)] * n,
-        scratch_shapes=[
-            pltpu.SemaphoreType.DMA(sems),
-            pltpu.SemaphoreType.DMA(sems),
-            pltpu.SemaphoreType.DMA((n,)),
-        ],
-        compiler_params=pltpu.CompilerParams(
-            collective_id=collective_id, has_side_effects=True
-        ),
-        name="gather_weights",
-    )(*shards)
 
 
 def scatter_kernel(bits, units, orders, plan, n_arrays, n_units, *refs):
@@ -500,7 +417,7 @@
             totals[unit], results[array].at[rows, cols], store_sem.at[unit]
         )
 
-    for unit, stage in plan:
+    for _, unit, stage in plan:
         if stage > 0:
             add(unit, stage - 1)
         message(unit, stage).start()
@@ -521,7 +438,7 @@
     shapes = [unit_shape([t.shape[count:] for t in terms], unit) for unit in units]
     kinds = [terms[array].dtype for array, _, _ in units]
     sizes = [s[0] * s[1] * kind.itemsize for s, kind in zip(shapes, kinds)]
-    plan = plan_sends(bits, orders, sizes, False, 1000e3)
+    plan, _ = plan_sends(bits, orders, sizes, False, 1000e3)
     n = len(terms)
     n_units = len(units)
     sems = (n_units, count)
@@ -553,7 +470,391 @@
     )(*terms)
 
 
+ERF_RATE = 0.3275911
+ERF_TERMS = (0.254829592, -0.284496736, 1.421413741, -1.453152027, 1.061405429)
+
+
+def gelu_parts(pre):
+    bell = jnp.exp2(pre * pre * (-0.5 * LOG2E))
+    arm = 1.0 / (1.0 + jnp.abs(pre) * (ERF_RATE * ROOT_HALF))
+    series = ERF_TERMS[4]
+    for term in ERF_TERMS[3::-1]:
+        series = series * arm + term
+    tail = 0.5 * series * arm * bell
+    below = jnp.where(pre >= 0.0, 1.0 - tail, tail)
+    return pre * below, below + pre * bell * INV_ROOT_TWO_PI
+
+
+class Schedule:
+    def __init__(self, plan, issue):
+        self.plan = plan
+        self.issue = issue
+        self.at = 0
+        self.now = 0.0
+
+    def due(self):
+        items = []
+        while self.at < len(self.plan) and self.plan[self.at][0] <= self.now:
+            items.append(self.plan[self.at][1:])
+            self.at += 1
+        return items
+
+    def spend(self, took):
+        self.now += took
+        for unit, stage in self.due():
+            self.issue(unit, stage)
+
+    def until(self, when):
+        self.now = max(self.now, when)
+        for unit, stage in self.due():
+            self.issue(unit, stage)
+
+    def loop(self, count, took, body):
+        buckets = []
+        for _ in range(count):
+            self.now += took
+            buckets.append(self.due())
+
+        def step(i, carry):
+            body(i)
+            for k, items in enumerate(buckets):
+                if items:
+
+                    @pl.when(i == k)
+                    def _(items=items):
+                        for unit, stage in items:
+                            self.issue(unit, stage)
+
+            return carry
+
+        lax.fori_loop(0, count, step, 0)
+
+
+ROWS_STEP = 128
+
+
+N_VECS = 14
+VEC_ROWS = 16
+VEC_LANES = 128
+
+
+def device_index(bits, mine):
+    count = len(bits)
+    return sum(mine[b] * 2 ** (count - 1 - b) for b in range(count))
+
+
+def pack_vectors(loose, pack, spot, size):
+    row = lax.broadcasted_iota(jnp.int32, (size, VEC_LANES), 0)
+    lane = lax.broadcasted_iota(jnp.int32, (size, VEC_LANES), 1)
+    place = (lane == row + size * spot).astype(jnp.float32)
+    pieces = []
+    for ref in loose[:-1]:
+        pieces.append(dot_nn(ref[...].astype(jnp.float32).reshape(1, size), place))
+    pieces.append(loose[-1][...].astype(jnp.float32).reshape(1, VEC_LANES))
+    pieces.append(jnp.zeros((VEC_ROWS - len(pieces), VEC_LANES), jnp.float32))
+    pack[...] = jnp.concatenate(pieces, axis=0).astype(pack.dtype)
+
+
+def forward_kernel(bits, units, orders, plan, arrive, n_arrays, heads, *refs):
+    count = len(bits)
+    (tokens, memory, lengths), refs = refs[:3], refs[3:]
+    loose, refs = refs[:N_VECS], refs[N_VECS:]
+    sources, refs = refs[: n_arrays - 1], refs[n_arrays - 1 :]
+    targets, refs = refs[:n_arrays], refs[n_arrays:]
+    saved_names = ("q", "k", "v", "a", "total", "h1")
+    saved_names += ("cq", "ck", "cv", "ca", "ctotal", "h2", "g", "slope", "out")
+    saved = dict(zip(saved_names, refs[: len(saved_names)]))
+    refs = refs[len(saved_names) :]
+    x, mem, n, q, k, v, a, h, ck, cv, g, slope, tot, ctot = refs[:14]
+    wide, tall, pack, vecs, table, hidden_row = refs[14:-6]
+    send_sem, recv_sem, own_sem, in_sem, w_sem, out_sem = refs[-6:]
+    mine = my_bits(bits)
+    rows, width = x.shape
+    devices = 2**count
+    lanes_each = width // devices
+    pack_vectors(loose, pack, device_index(bits, mine) % (VEC_LANES // lanes_each), lanes_each)
+    sources = (pack,) + tuple(sources)
+    own = [
+        pltpu.make_async_copy(sources[i], targets[i].at[tuple(mine)], own_sem.at[i])
+        for i in range(n_arrays)
+    ]
+    for copy in own:
+        copy.start()
+    load_x = pltpu.make_async_copy(tokens, x, in_sem.at[0])
+    load_mem = pltpu.make_async_copy(memory, mem, in_sem.at[1])
+    load_x.start()
+    load_mem.start()
+    greet(bits, mine)
+
+    def message(unit, stage):
+        array, top, left = units[unit]
+        order = orders[unit]
+        where = tuple(slice(None) if b in order[:stage] else mine[b] for b in range(count))
+        place = targets[array].at[where + (top, left)]
+        source = sources[array].at[top, left] if stage == 0 else place
+        return pltpu.make_async_remote_copy(
+            src_ref=source,
+            dst_ref=place,
+            send_sem=send_sem.at[unit, stage],
+            recv_sem=recv_sem.at[unit, stage],
+            device_id=partner(bits, mine, order[stage]),
+            device_id_type=MESH_ID,
+        )
+
+    settled = set()
+
+    def issue(unit, stage):
+        array = units[unit][0]
+        if stage > 0:
+            if array not in settled:
+                settled.add(array)
+                own[array].wait()
+            message(unit, stage - 1).wait_recv()
+        message(unit, stage).start()
+
+    clock = Schedule(plan, issue)
+    every = (slice(None),) * count
+
+    def fetch(unit, slot, sem):
+        clock.until(arrive[unit])
+        message(unit, count - 1).wait_recv()
+        array, top, left = units[unit]
+        if array not in settled:
+            settled.add(array)
+            own[array].wait()
+        copy = pltpu.make_async_copy(targets[array].at[every + (top, left)], slot, w_sem.at[sem])
+        copy.start()
+        copy.wait()
+
+    def times(lhs, slot, tile, write, took=1.4):
+        depth = lhs.shape[1]
+        tiles = slot.shape[-1] // tile
+
+        def body(j):
+            cols = pl.ds(pl.multiple_of(j * tile, tile), tile)
+            weight = slot[every + (slice(None), cols)].reshape(depth, tile)
+            write(cols, dot_nn(lhs[...], weight))
+
+        clock.loop(tiles, took / tiles, body)
+
+    def norm_into(gain, shift, source):
+        def body(i):
+            part = pl.ds(pl.multiple_of(i * ROWS_STEP, ROWS_STEP), ROWS_STEP)
+            r = source[part, :].astype(jnp.float32)
+            n[part, :] = normalize(r, gain, shift)[0].astype(jnp.bfloat16)
+
+        clock.loop(rows // ROWS_STEP, 0.4, body)
+
+    pending = []
+
+    def save(source, name, index):
+        copy = pltpu.make_async_copy(source, saved[name], out_sem.at[index])
+        copy.start()
+        pending.append(copy)
+        return copy
+
+    def vec(i):
+        return table[pl.ds(i, 1), :]
+
+    clock.until(0.0)
+    fetch(0, vecs, 0)
+    for group in range(width // VEC_LANES):
+        share = VEC_LANES // lanes_each
+        total = None
+        for d in range(group * share, (group + 1) * share):
+            where = tuple((d >> (count - 1 - b)) & 1 for b in range(count))
+            block = vecs[where].astype(jnp.float32)
+            total = block if total is None else total + block
+        table[:, pl.ds(group * VEC_LANES, VEC_LANES)] = total
+    for d in range(devices):
+        where = tuple((d >> (count - 1 - b)) & 1 for b in range(count))
+        block = vecs[where].astype(jnp.float32)
+        hidden_row[pl.ds(0, 1), pl.ds(d * VEC_LANES, VEC_LANES)] = block[13:14]
+    load_x.wait()
+    load_mem.wait()
+    norm_into(vec(0), vec(1), x)
+    length = lengths[0]
+
+    def project(bias, target, extra=0):
+        def write(cols, acc):
+            if bias is not None:
+                acc = acc + table[pl.ds(bias, 1), cols]
+            target[:, cols] = acc.astype(target.dtype)
+
+        return write
+
+    def residual(bias, source):
+        def write(cols, acc):
+            h[:, cols] = source[:, cols].astype(jnp.float32) + acc + table[pl.ds(bias, 1), cols]
+
+        return write
+
+    def attend(q_ref, k_ref, v_ref, tot_ref, masked):
+        keys = k_ref.shape[0]
+        pair = 2 * (width // heads)
+
+        def body(p):
+            lanes = pl.ds(pl.multiple_of(p * pair, pair), pair)
+
+            def write(start, size, out, totals):
+                a[pl.ds(start, size), lanes] = out
+                for head in (0, 1):
+                    tot_ref[p, pl.ds(head, 1), pl.ds(start, size)] = totals[head]
+
+            forward_pair(
+                lambda s, m: q_ref[pl.ds(s, m), lanes],
+                lambda s, m: k_ref[pl.ds(s, m), lanes],
+                lambda s, m: v_ref[pl.ds(s, m), lanes],
+                write,
+                [(0, rows, keys)],
+                length if masked else None,
+                (width // heads) ** -0.5,
+            )
+
+        clock.loop(heads // 2, 1.6, body)
+
+    for unit, target, bias in ((1, q, 2), (2, k, None), (3, v, 3)):
+        fetch(unit, wide, 1)
+        times(n, wide, 256, project(bias, target))
+    save(q, "q", 0)
+    save(k, "k", 1)
+    save(v, "v", 2)
+    attend(q, k, v, tot, True)
+    save(a, "a", 3)
+    save(tot, "total", 4)
+    for unit, target, bias in ((4, ck, None), (5, cv, 8)):
+        fetch(unit, wide, 1)
+        times(mem, wide, 256, project(bias, target), 1.6)
+    save(ck, "ck", 5)
+    save(cv, "cv", 6)
+    fetch(6, wide, 1)
+    times(a, wide, 256, residual(4, x))
+    save(h, "h1", 7)
+    norm_into(vec(5), vec(6), h)
+    fetch(7, wide, 1)
+    pending[0].wait()
+    times(n, wide, 256, project(7, q))
+    save(q, "cq", 8)
+    pending[3].wait()
+    attend(q, ck, cv, ctot, False)
+    save(a, "ca", 9)
+    save(ctot, "ctotal", 10)
+    fetch(8, wide, 1)
+    pending[7].wait()
+    times(a, wide, 256, residual(9, h))
+    save(h, "h2", 11)
+    norm_into(vec(10), vec(11), h)
+    block = wide.shape[-1]
+    blocks = g.shape[1] // block
+    for j in range(blocks):
+        fetch(9 + j, wide, 1)
+        tile = 256
+
+        def body(i, j=j):
+            cols = pl.ds(pl.multiple_of(i * tile, tile), tile)
+            spot = pl.ds(pl.multiple_of(j * block + i * tile, tile), tile)
+            weight = wide[every + (slice(None), cols)].reshape(width, tile)
+            for r in range(0, rows, ROWS_STEP):
+                part = pl.ds(r, ROWS_STEP)
+                pre = dot_nn(n[part, :], weight) + hidden_row[:, spot]
+                low, rate = gelu_parts(pre)
+                g[part, spot] = low.astype(jnp.bfloat16)
+                slope[part, spot] = rate.astype(jnp.bfloat16)
+
+        clock.loop(block // tile, 0.8, body)
+    save(g, "g", 12)
+    save(slope, "slope", 13)
+    for j in range(width // tall.shape[-1]):
+        fetch(9 + blocks + j, tall, 2)
+        cols = pl.ds(j * tall.shape[-1], tall.shape[-1])
+        weight = tall[...].reshape(g.shape[1], tall.shape[-1])
+        acc = dot_nn(g[...], weight)
+        x[:, cols] = (h[:, cols] + acc + table[pl.ds(12, 1), cols]).astype(jnp.bfloat16)
+        clock.spend(1.6)
+    save(x, "out", 14)
+    clock.until(1e9)
+    for i, copy in enumerate(pending):
+        if i not in (0, 3, 7):
+            copy.wait()
+    for unit in range(len(units)):
+        for stage in range(count):
+            message(unit, stage).wait_send()
+
+
+def fused_forward(mesh, tokens, memory, lengths, mats, vecs, heads, collective_id):
+    bits = bit_table(mesh)
+    routes = route_orders(bits)
+    rows, width = tokens.shape
+    keys = memory.shape[0]
+    block = mats[0].shape
+    pack = (VEC_ROWS, VEC_LANES)
+    every = slice(None)
+    units = [(0, every, every)] + [(i, every, every) for i in range(1, 9)]
+    hidden = mats[8].shape[1]
+    for left in range(0, hidden, width):
+        units.append((9, every, slice(left, left + width)))
+    tall_rows = mats[9].shape[0]
+    tall_cols = width * block[0] // tall_rows
+    for left in range(0, width, tall_cols):
+        units.append((10, every, slice(left, left + tall_cols)))
+    blocks = [pack] + [m.shape for m in mats]
+    shapes = [unit_shape(blocks, unit) for unit in units]
+    sizes = [2 * s[0] * s[1] for s in shapes]
+    orders = [routes[u % 2] for u in range(len(units))]
+    plan, arrive = plan_sends(bits, orders, sizes, True, None)
+    n = len(blocks)
+    spots = (2,) * len(bits)
+    low = jnp.bfloat16
+    wide_rows = jax.ShapeDtypeStruct((rows, width), low)
+    wide_keys = jax.ShapeDtypeStruct((keys, width), low)
+    full = jax.ShapeDtypeStruct((rows, width), jnp.float32)
+    totals = jax.ShapeDtypeStruct((heads // 2, 2, rows), jnp.float32)
+    ff = jax.ShapeDtypeStruct((rows, hidden), low)
+    saved = [
+        wide_rows, wide_rows, wide_rows, wide_rows, totals, full,
+        wide_rows, wide_keys, wide_keys, wide_rows, totals, full, ff, ff, wide_rows,
+    ]
+    vm = lambda s: pltpu.VMEM(s.shape, s.dtype)
+    sems = (len(units), len(bits))
+    hbm = pl.BlockSpec(memory_space=pltpu.HBM)
+    got = pl.pallas_call(
+        functools.partial(forward_kernel, bits, units, orders, plan, arrive, n, heads),
+        out_shape=[jax.ShapeDtypeStruct(spots + b, low) for b in blocks] + saved,
+        in_specs=[hbm, hbm, pl.BlockSpec(memory_space=pltpu.SMEM)]
+        + [pl.BlockSpec(memory_space=pltpu.VMEM)] * len(vecs)
+        + [hbm] * len(mats),
+        out_specs=[hbm] * (n + len(saved)),
+        scratch_shapes=[
+            vm(wide_rows), vm(wide_keys), vm(wide_rows), vm(wide_rows), vm(wide_rows),
+            vm(wide_rows), vm(wide_rows), vm(full), vm(wide_keys), vm(wide_keys),
+            vm(ff), vm(ff), vm(totals), vm(totals),
+            pltpu.VMEM(spots + block, low),
+            pltpu.VMEM(spots + (tall_rows, tall_cols), low),
+            pltpu.VMEM(pack, low),
+            pltpu.VMEM(spots + pack, low),
+            pltpu.VMEM((VEC_ROWS, width), jnp.float32),
+            pltpu.VMEM((1, hidden), jnp.float32),
+            pltpu.SemaphoreType.DMA(sems),
+            pltpu.SemaphoreType.DMA(sems),
+            pltpu.SemaphoreType.DMA((n,)),
+            pltpu.SemaphoreType.DMA((2,)),
+            pltpu.SemaphoreType.DMA((3,)),
+            pltpu.SemaphoreType.DMA((len(saved),)),
+        ],
+        compiler_params=pltpu.CompilerParams(
+            collective_id=collective_id,
+            has_side_effects=True,
+            vmem_limit_bytes=60 * 1024 * 1024,
+        ),
+        name="forward_layer",
+    )(tokens, memory, lengths, *vecs, *mats)
+    return got[:n], got[n:]
+
+
 MATS = (2, 4, 5, 7, 11, 13, 14, 16, 20, 22)
+MATS_ORDER = (2, 4, 5, 13, 14, 7, 11, 16, 20, 22)
+GRAD_ROWS = 8
+GRAD_LANES = 128
 VECS = (0, 1, 3, 6, 8, 9, 10, 12, 15, 17, 18, 19, 23, 21)
 
 
@@ -569,27 +870,22 @@
     return units
 
 
-def collect(mesh, *shards):
-    mats = [shards[i] for i in MATS]
-    if not can_route(mesh, mats[0].shape[0]):
-        return tuple(lax.all_gather(s, BOTH, axis=0, tiled=True) for s in shards)
-    per = shards[0].shape[0]
-    packed = jnp.concatenate([shards[i].astype(jnp.float32) for i in VECS])
-    spare = VEC_ROWS * VEC_LANES - packed.shape[0]
-    packed = jnp.pad(packed, (0, spare)).reshape(VEC_ROWS, VEC_LANES)
-    units = split_units([m.shape for m in mats])
-    got = gather_all(mesh, [packed] + mats, units, 0)
-    devices = mesh.shape["dp"] * mesh.shape["fsdp"]
-    table = got[0].reshape(devices, VEC_ROWS * VEC_LANES)
+def collect(*shards):
+    return tuple(lax.all_gather(s, BOTH, axis=0, tiled=True) for s in shards)
+
+
+def unpack_vectors(table, shards):
+    devices = table.size // (VEC_ROWS * VEC_LANES)
+    table = table.reshape(devices, VEC_ROWS, VEC_LANES)
+    size = shards[0].shape[0]
+    share = VEC_LANES // size
+    narrow = table.reshape(devices // share, share, VEC_ROWS, VEC_LANES).astype(jnp.float32)
+    narrow = jnp.sum(narrow, axis=1).transpose(1, 0, 2).reshape(VEC_ROWS, devices * size)
     full = [None] * len(shards)
-    start = 0
-    for i in VECS:
-        size = shards[i].shape[0]
-        full[i] = table[:, start : start + size].reshape(devices * size)
-        start += size
-    for i, value in zip(MATS, got[1:]):
-        full[i] = value.reshape(devices * shards[i].shape[0], shards[i].shape[1])
-    return tuple(full)
+    for row, i in enumerate(VECS[:-1]):
+        full[i] = narrow[row]
+    full[VECS[-1]] = table[:, len(VECS) - 1].reshape(-1)
+    return full
 
 
 def spread(mesh, *grads):
@@ -602,8 +898,8 @@
         )
     spots = (2,) * len(bit_table(mesh))
     table = jnp.concatenate([grads[i].reshape(devices, -1) for i in VECS], axis=1)
-    spare = VEC_ROWS * VEC_LANES - table.shape[1]
-    table = jnp.pad(table, ((0, 0), (0, spare))).reshape(spots + (VEC_ROWS, VEC_LANES))
+    spare = GRAD_ROWS * GRAD_LANES - table.shape[1]
+    table = jnp.pad(table, ((0, 0), (0, spare))).reshape(spots + (GRAD_ROWS, GRAD_LANES))
     terms = [m.reshape(spots + (m.shape[0] // devices, m.shape[1])) for m in mats]
     units = split_units([t.shape[-2:] for t in terms])
     got = scatter_all(mesh, [table] + terms, units, 1)
@@ -657,8 +953,7 @@
     lengths_now = jnp.where(end_flags == 1, 1, page_lengths)
     inputs = tokens.reshape(row_count, width).astype(jnp.float32)
     mem_rows = memory.reshape(page_count * mem_len, width)
-    full_set = collect(
-        mesh,
+    shard_set = (
         self_gain,
         self_shift,
         self_query,
@@ -684,6 +979,25 @@
         feed_out,
         feed_out_bias,
     )
+    if can_route(mesh, self_query.shape[0]):
+        mats = [shard_set[i] for i in MATS_ORDER]
+        got, saved = fused_forward(
+            mesh, tokens[0], memory[0], lengths_now, mats, [shard_set[i] for i in VECS], HEADS, 0
+        )
+        full_set = unpack_vectors(got[0], shard_set)
+        for i, value in zip(MATS_ORDER, got[1:]):
+            full_set[i] = value.reshape(-1, value.shape[-1])
+        (
+            query_low, key_low, value_low, self_low, self_total, after_self,
+            cquery_low, ckey_low, cvalue_low, cross_low, cross_total, after_cross,
+            hidden_low, hidden_rate, layer_out,
+        ) = saved
+        self_total, cross_total = self_total[None], cross_total[None]
+        layer_out = layer_out[None]
+        query_pages, key_pages, value_pages = query_low[None], key_low[None], value_low[None]
+        cquery_pages, ckey_pages, cvalue_pages = cquery_low[None], ckey_low[None], cvalue_low[None]
+    else:
+        full_set = collect(*shard_set)
     (
         gain_one,
         shift_one,
@@ -710,53 +1024,59 @@
         final_mat,
         final_vec,
     ) = full_set
-    first_norm, first_unit, first_std = normalize(
-        inputs, gain_one.astype(jnp.float32), shift_one.astype(jnp.float32)
-    )
+    norm_of = lambda r, g, b: normalize(r, g.astype(jnp.float32), b.astype(jnp.float32))
+    first_norm, first_unit, first_std = norm_of(inputs, gain_one, shift_one)
     first_low = first_norm.astype(jnp.bfloat16)
-    query_low = (product(first_low, query_mat) + query_vec.astype(jnp.float32)).astype(jnp.bfloat16)
-    key_low = product(first_low, key_mat).astype(jnp.bfloat16)
-    value_low = (product(first_low, value_mat) + value_vec.astype(jnp.float32)).astype(jnp.bfloat16)
-    query_pages = query_low.reshape(page_count, page_len, width)
-    key_pages = key_low.reshape(page_count, page_len, width)
-    value_pages = value_low.reshape(page_count, page_len, width)
-    self_mixed, self_total = attend_fwd(
-        query_pages, key_pages, value_pages, lengths_now, HEADS, 512
-    )
-    self_low = self_mixed.reshape(row_count, width)
-    after_self = inputs + product(self_low, out_mat) + out_vec.astype(jnp.float32)
-    second_norm, second_unit, second_std = normalize(
-        after_self, gain_two.astype(jnp.float32), shift_two.astype(jnp.float32)
-    )
+    if not can_route(mesh, self_query.shape[0]):
+        query_low = (product(first_low, query_mat) + query_vec.astype(jnp.float32)).astype(jnp.bfloat16)
+        key_low = product(first_low, key_mat).astype(jnp.bfloat16)
+        value_low = (product(first_low, value_mat) + value_vec.astype(jnp.float32)).astype(jnp.bfloat16)
+        query_pages = query_low.reshape(page_count, page_len, width)
+        key_pages = key_low.reshape(page_count, page_len, width)
+        value_pages = value_low.reshape(page_count, page_len, width)
+        self_mixed, self_total = attend_fwd(
+            query_pages, key_pages, value_pages, lengths_now, HEADS, 512
+        )
+        self_low = self_mixed.reshape(row_count, width)
+        after_self = inputs + product(self_low, out_mat) + out_vec.astype(jnp.float32)
+        second_norm, second_unit, second_std = normalize(
+            after_self, gain_two.astype(jnp.float32), shift_two.astype(jnp.float32)
+        )
+        second_low = second_norm.astype(jnp.bfloat16)
+        cquery_low = (product(second_low, cquery_mat) + cquery_vec.astype(jnp.float32)).astype(
+            jnp.bfloat16
+        )
+        ckey_low = product(mem_rows, ckey_mat).astype(jnp.bfloat16)
+        cvalue_low = (product(mem_rows, cvalue_mat) + cvalue_vec.astype(jnp.float32)).astype(
+            jnp.bfloat16
+        )
+        cquery_pages = cquery_low.reshape(page_count, page_len, width)
+        ckey_pages = ckey_low.reshape(page_count, mem_len, width)
+        cvalue_pages = cvalue_low.reshape(page_count, mem_len, width)
+        cross_mixed, cross_total = attend_fwd(
+            cquery_pages, ckey_pages, cvalue_pages, None, HEADS, 512
+        )
+        cross_low = cross_mixed.reshape(row_count, width)
+        after_cross = after_self + product(cross_low, cout_mat) + cout_vec.astype(jnp.float32)
+        third_norm, third_unit, third_std = normalize(
+            after_cross, gain_three.astype(jnp.float32), shift_three.astype(jnp.float32)
+        )
+        third_low = third_norm.astype(jnp.bfloat16)
+        hidden_pre = product(third_low, hidden_mat) + hidden_vec.astype(jnp.float32)
+        hidden_low, hidden_rate = gelu_parts(hidden_pre)
+        hidden_low = hidden_low.astype(jnp.bfloat16)
+        hidden_rate = hidden_rate.astype(jnp.bfloat16)
+        result = after_cross + product(hidden_low, final_mat) + final_vec.astype(jnp.float32)
+        layer_out = result.astype(jnp.bfloat16).reshape(page_count, page_len, width)
+    second_norm, second_unit, second_std = norm_of(after_self, gain_two, shift_two)
     second_low = second_norm.astype(jnp.bfloat16)
-    cquery_low = (product(second_low, cquery_mat) + cquery_vec.astype(jnp.float32)).astype(
-        jnp.bfloat16
-    )
-    ckey_low = product(mem_rows, ckey_mat).astype(jnp.bfloat16)
-    cvalue_low = (product(mem_rows, cvalue_mat) + cvalue_vec.astype(jnp.float32)).astype(
-        jnp.bfloat16
-    )
-    cquery_pages = cquery_low.reshape(page_count, page_len, width)
-    ckey_pages = ckey_low.reshape(page_count, mem_len, width)
-    cvalue_pages = cvalue_low.reshape(page_count, mem_len, width)
-    cross_mixed, cross_total = attend_fwd(
-        cquery_pages, ckey_pages, cvalue_pages, None, HEADS, 512
-    )
-    cross_low = cross_mixed.reshape(row_count, width)
-    after_cross = after_self + product(cross_low, cout_mat) + cout_vec.astype(jnp.float32)
-    third_norm, third_unit, third_std = normalize(
-        after_cross, gain_three.astype(jnp.float32), shift_three.astype(jnp.float32)
-    )
+    third_norm, third_unit, third_std = norm_of(after_cross, gain_three, shift_three)
     third_low = third_norm.astype(jnp.bfloat16)
-    hidden_pre = product(third_low, hidden_mat) + hidden_vec.astype(jnp.float32)
-    hidden_low = jax.nn.gelu(hidden_pre, approximate=False).astype(jnp.bfloat16)
-    result = after_cross + product(hidden_low, final_mat) + final_vec.astype(jnp.float32)
-    layer_out = result.astype(jnp.bfloat16).reshape(page_count, page_len, width)
     grad_rows = out_grad.reshape(row_count, width).astype(jnp.float32)
     final_grad = out_grad.reshape(row_count, width)
     grad_final_mat = product_tn(hidden_low, final_grad).astype(jnp.bfloat16)
     grad_final_vec = jnp.sum(final_grad.astype(jnp.float32), axis=0)
-    hidden_grad = (product_nt(final_grad, final_mat) * gelu_slope(hidden_pre)).astype(jnp.bfloat16)
+    hidden_grad = (product_nt(final_grad, final_mat) * hidden_rate.astype(jnp.float32)).astype(jnp.bfloat16)
     grad_hidden_mat = product_tn(third_low, hidden_grad).astype(jnp.bfloat16)
     grad_hidden_vec = jnp.sum(hidden_grad.astype(jnp.float32), axis=0)
     third_back, grad_gain_three, grad_shift_three = normalize_back(

time: 592 us -> 497 us (0.84)
  matrix products: 127 us -> 68 us
  local copies, waits for them, and re-layouts: 60.1 us -> 25 us
    dot_general x10 -> x0, matrix products: 48.6 us -> none  [product(): return jnp.dot(left, right, preferred_element_type=jnp.float32)]
    unnamed x172 -> x156, local copies, waits for them, and re-layouts: 30.9 us -> 17.7 us
    dot_general x10, matrix products: 40.8 us -> 28.8 us  [product_nt(): lax.dot_general(left, right, (((1,), (1,)), ((), ())), preferred_element_...]
    reshape x13, local copies, waits for them, and re-layouts: 13.9 us -> 2.75 us  [spread(): grads[i].reshape(devices, -1)]
    concatenate x1 -> x0, local copies, waits for them, and re-layouts: 9.43 us -> none  [collect(): packed = jnp.concatenate([shards[i].astype(jnp.float32) for i in VECS])]
    pallas_call x3 -> x1, Pallas kernels: 187 us -> 180 us  [fused_forward(): pl.pallas_call(functools.partial(forward_kernel, bits, units, orders, pla...]
where the time goes in v3:
time: 497 us; the launch traced here: 489 us
  Pallas kernels  380 us (76%)
  matrix products  68 us (14%)
  local copies, waits for them, and re-layouts  25 us (5%)
  other arithmetic  13.1 us (3%)
    pallas_call x1, Pallas kernels, fused_forward(): pl.pallas_call(functools.partial(forward_kernel, bits, units, orders, pla...  180 us
    pallas_call x1, Pallas kernels, scatter_all(): pl.pallas_call(functools.partial(scatter_kernel, bits, units, orders, pla...  161 us
    dot_general x10, matrix products, product_tn(): lax.dot_general(left, right, (((0,), (0,)), ((), ())), preferred_element_...  39.2 us
    pallas_call x2, Pallas kernels, attend_bwd(): pl.pallas_call(functools.partial(bwd_kernel, masked, head ** (-0.5), chun...  38.2 us
    dot_general x10, matrix products, product_nt(): lax.dot_general(left, right, (((1,), (1,)), ((), ())), preferred_element_...  28.8 us
    unnamed x156, local copies, waits for them, and re-layouts  17.7 us

profile of v3, /device:TPU:0, one launch (start us, length us, event | category | flops | bytes accessed | tf_op | source)
XLA Modules:
  0.0 488.9 jit_solution(17306797235906816524)
XLA Ops:
  2.0 180.1 %forward_layer.1 = (bf16[2,2,2,2,2,16,128]{6,5,4,3,2,1,0:T(8,128)(2,1)}, bf16[2,2,2,2,2,32,1024]{6,5,4,3,2,1,0:T(8,128)(2,1)}, bf16[2,2,2,2,2,32,1024]{6,5,4,3,2...) custom-call(bf16[512,1024]{1,0:T(8,128)(2,1)} %bitcast.144, ...), custom_call_target="tpu_custom_call" | custom-call | tf_op jit(solution)/shard_map/forward_layer/pallas_call | solution.py:820
  182.1 1.9 reduce_sum.248
  185.3 9.7 %convert_reduce_fusion = (f32[4096]{0:T(1024)}, bf16[512,4096]{1,0:T(8,128)(2,1)S(1)}) fusion(bf16[512,4096]{1,0:T(8,128)(2,1)} %get-tuple-element.72, bf16[4096,1024]{1,0:T(8,128)(2,1)} %bitcast.184, bf16[1,512,1024]{2,1,0:T(8,128)(2,1)S(1)} %copy-done.22), kind=kOutput, calls=%fused_computation.2 | convolution fusion | flops 4305448960 | bytes 17842176 | tf_op jit(solution)/shard_map/dot_general | solution.py:29
  195.0 6.2 %multiply_reduce_fusion = (f32[1024]{0:T(1024)S(1)}, f32[512]{0:T(512)S(1)}, f32[512]{0:T(512)S(1)}, f32[1024]{0:T(1024)S(1)}, f32[512,1024]{1,0:T(8,128)}) fusion(f32[512,1024]{1,0:T(8,128)S(1)} %copy-done.10, f32[512]{0:T(512)S(1)} %add_rsqrt_fusion.2, f32[512]{0:T(512)S(1)} %broadcast_multiply_fusion.7, f32[1024]{0:T(1024)S(1)} %bitcast.162, ...), kind=kOutput, calls=%fused_computation.26 | convolution fusion | flops 4299682816 | bytes 16797696 | tf_op jit(solution)/shard_map/dot_general | solution.py:29
  201.2 1.8 reduce_sum.252
  203.1 3.6 convert_reduce_fusion.4
  206.8 1.3 fusion.13.refs_3_
  208.7 20.6 %attend_backward.2 = (bf16[1,512,1024]{2,1,0:T(8,128)(2,1)S(1)}, bf16[1,588,1024]{2,1,0:T(8,128)(2,1)S(1)}, bf16[1,588,1024]{2,1,0:T(8,128)(2,1)S(1)}) custom-call(bf16[1,512,1024]{2,1,0:T(8,128)(2,1)S(1)} %bitcast.141, bf16[1,588,1024]{2,1,0:T(8,128)(2,1)} %bitcast.156, bf16[1,588,1024]{2,1,0:T(8,128)(2,1)} %bitcast.157, ...), custom_call_target="tpu_custom_call" | custom-call | tf_op jit(solution)/shard_map/attend_backward/pallas_call | solution.py:224
  229.3 1.8 multiply_reduce_fusion.1
  231.1 0.7 convert_reduce_fusion.6
  233.0 1.3 copy-done.62
  234.3 2.3 fusion.14.refs_4_
  236.6 17.7 %attend_backward.3 = (bf16[1,512,1024]{2,1,0:T(8,128)(2,1)S(1)}, bf16[1,512,1024]{2,1,0:T(8,128)(2,1)S(1)}, bf16[1,512,1024]{2,1,0:T(8,128)(2,1)S(1)}) custom-call(s32[1]{0:T(128)S(6)} %select_n.4.refs_2_.refs_0_, bf16[1,512,1024]{2,1,0:T(8,128)(2,1)S(1)} %bitcast.139, bf16[1,512,1024]{2,1,0:T(8,128)(2,1)S(1)} %bitcast.140, bf16[1,512,1024]{2,1,0:T(8,128)(2,1)} %bitcast.158, ...), custom_call_target="tpu_custom_call" | custom-call | tf_op jit(solution)/shard_map/attend_backward/pallas_call | solution.py:224
  254.3 1.3 fusion.27
  255.6 1.0 copy-done.60
  256.6 1.3 fusion.24
  258.2 2.1 fusion.11
  260.4 2.0 fusion.10
  262.4 1.5 fusion.18
  264.0 1.5 add_bitcast_fusion
  265.5 3.9 copy.56
  269.5 1.4 convert_reduce_fusion.8
  272.1 0.7 reshape.384
  272.8 0.7 reshape.385
  273.4 0.7 reshape.386
  274.1 0.9 concatenate.3
  275.0 0.7 copy.57
  275.7 4.7 convolution_convert_fusion.7
  280.5 2.9 convolution_convert_fusion.6
  283.3 2.8 convolution_convert_fusion.5
  286.2 2.6 convolution_convert_fusion.4
  288.9 2.8 convolution_convert_fusion.3
  291.7 3.2 convolution_convert_fusion.9
  294.9 3.2 convolution_convert_fusion.8
  298.2 2.6 convolution_convert_fusion.2
  300.8 0.9 copy-done.68
  301.8 7.6 %convolution_convert_fusion.1 = bf16[1024,4096]{1,0:T(8,128)(2,1)} fusion(bf16[512,4096]{1,0:T(8,128)(2,1)S(1)} %copy-done.68, f32[512,1024]{1,0:T(8,128)S(1)} %copy-done.11, f32[1024]{0:T(1024)S(1)} %bitcast.176, f32[512]{0:T(512)S(1)} %copy-done.48, f32[512]{0:T(512)S(1)} %copy-done.38, f32[1024]{0:T(1024)S(1)} %bitcast.164), kind=kOutput, calls=%fused_computation.4 | convolution fusion | flops 4301783040 | bytes 14692352 | tf_op jit(solution)/shard_map/dot_general | solution.py:23
  309.4 6.8 %convolution_convert_fusion = bf16[4096,1024]{1,0:T(8,128)(2,1)} fusion(bf16[512,4096]{1,0:T(8,128)(2,1)S(1)} %copy-done.56, bf16[1,512,1024]{2,1,0:T(8,128)(2,1)S(1)} %copy-done.23), kind=kOutput, calls=%fused_computation.3 | convolution fusion | flops 4299161600 | bytes 13631488 | tf_op jit(solution)/shard_map/dot_general | solution.py:23
  316.2 161.3 %scatter_grads.1 = (f32[8,128]{1,0:T(8,128)}, f32[32,1024]{1,0:T(8,128)}, f32[32,1024]{1,0:T(8,128)}, f32[32,1024]{1,0:T(8,128)}, f32[32,1024]{1,0:T(8,128)}, /*...) custom-call(f32[2,2,2,2,2,8,128]{6,5,4,3,2,1,0:T(8,128)} %bitcast.16, ...), custom_call_target="tpu_custom_call" | custom-call | tf_op jit(solution)/shard_map/scatter_grads/pallas_call | solution.py:458
  477.6 1.8 fusion.52
  479.3 1.3 slice.84
  480.6 1.0 copy.71
  481.6 0.7 copy.72
  482.2 0.7 copy.73
  482.9 0.7 copy.74
  483.5 0.7 copy.75
  486.8 0.8 copy.80
  487.6 0.8 copy.81
  (175 shorter events, 7.6 us)
Async XLA Ops:
  182.1 3.2 copy-start.22
  184.3 18.7 %copy-start.37 = (f32[512]{0:T(512)}, f32[512]{0:T(512)S(1)}, u32[]{:S(2)}) copy-start(f32[512]{0:T(512)S(1)} %broadcast_multiply_fusion.7) | copy-start | bytes 6148
  184.3 10.7 %slice-start = ((s8[8388608]{0:T(1024)(128)(4,1)}), s8[4194304]{0:T(1024)(128)(4,1)S(1)}, s32[]{:S(2)}) async-start(s8[8388608]{0:T(1024)(128)(4,1)} %bitcast.181), calls=%async_computation | async-start | bytes 8388608
  184.6 18.4 %copy-start.47 = (f32[512]{0:T(512)}, f32[512]{0:T(512)S(1)}, u32[]{:S(2)}) copy-start(f32[512]{0:T(512)S(1)} %add_rsqrt_fusion.2) | copy-start | bytes 6148
  185.3 17.7 %copy-start.41 = (f32[1,8,128]{2,0,1:T(1,128)}, f32[1,8,128]{2,0,1:T(1,128)S(1)}, u32[]{:S(2)}) copy-start(f32[1,8,128]{2,0,1:T(1,128)S(1)} %get-tuple-element.162) | copy-start | bytes 12292
  185.3 45.8 %copy-start.43 = (f32[1,8,128]{2,0,1:T(1,128)}, f32[1,8,128]{2,0,1:T(1,128)S(1)}, u32[]{:S(2)}) copy-start(f32[1,8,128]{2,0,1:T(1,128)S(1)} %get-tuple-element.161) | copy-start | bytes 12292
  185.3 75.0 %copy-start.45 = (f32[1,8,128]{2,0,1:T(1,128)}, f32[1,8,128]{2,0,1:T(1,128)S(1)}, u32[]{:S(2)}) copy-start(f32[1,8,128]{2,0,1:T(1,128)S(1)} %get-tuple-element.160) | copy-start | bytes 12292
  185.3 9.7 %slice-start.1 = ((s8[8388608]{0:T(1024)(128)(4,1)}), s8[4194304]{0:T(1024)(128)(4,1)S(1)}, s32[]{:S(2)}) async-start(s8[8388608]{0:T(1024)(128)(4,1)} %bitcast.181), calls=%async_computation.1 | async-start | bytes 8388608
  195.0 6.2 %copy-start.67 = (bf16[512,4096]{1,0:T(8,128)(2,1)}, bf16[512,4096]{1,0:T(8,128)(2,1)S(1)}, u32[]{:S(2)}) copy-start(bf16[512,4096]{1,0:T(8,128)(2,1)S(1)} %get-tuple-element.180) | copy-start | bytes 12582916
  203.0 28.1 %copy-start.39 = (f32[512]{0:T(512)}, f32[512]{0:T(512)S(1)}, u32[]{:S(2)}) copy-start(f32[512]{0:T(512)S(1)} %broadcast_multiply_fusion.4) | copy-start | bytes 6148
  203.1 3.7 copy-start.64
  206.7 24.4 %copy-start.16 = (f32[512,1024]{1,0:T(8,128)}, f32[512,1024]{1,0:T(8,128)S(1)}, u32[]{:S(2)}) copy-start(f32[512,1024]{1,0:T(8,128)S(1)} %get-tuple-element.153) | copy-start | bytes 6291460
  206.7 24.4 %copy-start.49 = (f32[512]{0:T(512)}, f32[512]{0:T(512)S(1)}, u32[]{:S(2)}) copy-start(f32[512]{0:T(512)S(1)} %add_rsqrt_fusion.1) | copy-start | bytes 6148
  208.7 20.6 %copy-start.12 = (f32[512,1024]{1,0:T(8,128)S(1)}, f32[512,1024]{1,0:T(8,128)}, u32[]{:S(2)}) copy-start(f32[512,1024]{1,0:T(8,128)} %get-tuple-element.83) | copy-start | bytes 6291460
  208.7 20.6 %copy-start.63 = (bf16[2,2,2,2,2,32,1024]{6,5,4,3,2,1,0:T(8,128)(2,1)S(1)}, bf16[2,2,2,2,2,32,1024]{6,5,4,3,2,1,0:T(8,128)(2,1)}, u32[]{:S(2)}) copy-start(bf16[2,2,2,2,2,32,1024]{6,5,4,3,2,1,0:T(8,128)(2,1)} %get-tuple-element.82) | copy-start | bytes 6291460
  229.3 33.1 %copy-start.6 = (bf16[1,588,1024]{2,1,0:T(8,128)(2,1)}, bf16[1,588,1024]{2,1,0:T(8,128)(2,1)S(1)}, u32[]{:S(2)}) copy-start(bf16[1,588,1024]{2,1,0:T(8,128)(2,1)S(1)} %get-tuple-element.95) | copy-start | bytes 3612676
  231.9 28.5 %copy-start.18 = (f32[512,1024]{1,0:T(8,128)}, f32[512,1024]{1,0:T(8,128)S(1)}, u32[]{:S(2)}) copy-start(f32[512,1024]{1,0:T(8,128)S(1)} %get-tuple-element.155) | copy-start | bytes 6291460
  232.6 27.8 %copy-start.35 = (f32[512]{0:T(512)}, f32[512]{0:T(512)S(1)}, u32[]{:S(2)}) copy-start(f32[512]{0:T(512)S(1)} %broadcast_multiply_fusion.1) | copy-start | bytes 6148
  233.0 27.4 %copy-start.51 = (f32[512]{0:T(512)}, f32[512]{0:T(512)S(1)}, u32[]{:S(2)}) copy-start(f32[512]{0:T(512)S(1)} %add_rsqrt_fusion) | copy-start | bytes 6148
  236.6 17.7 %copy-start.61 = (bf16[2,2,2,2,2,32,1024]{6,5,4,3,2,1,0:T(8,128)(2,1)S(1)}, bf16[2,2,2,2,2,32,1024]{6,5,4,3,2,1,0:T(8,128)(2,1)}, u32[]{:S(2)}) copy-start(bf16[2,2,2,2,2,32,1024]{6,5,4,3,2,1,0:T(8,128)(2,1)} %get-tuple-element.90) | copy-start | bytes 6291460
  275.7 4.7 copy-start.9
  275.7 4.7 copy-start.15
  275.7 4.7 copy-start.36
  275.7 4.7 copy-start.46
  275.7 4.7 copy-start.52
  275.7 4.7 copy-start.55
  283.3 2.8 copy-start.19
  283.3 2.8 copy-start.66
  286.1 2.7 copy-start.13
  286.1 2.7 copy-start.40
  288.8 2.8 copy-start.7
  288.8 2.8 copy-start.20
  294.9 3.2 copy-start.17
  294.9 3.2 copy-start.65
  298.2 3.6 copy-start.68
  301.8 7.6 %copy-start.23 = (bf16[1,512,1024]{2,1,0:T(8,128)(2,1)S(1)}, bf16[1,512,1024]{2,1,0:T(8,128)(2,1)}, u32[]{:S(2)}) copy-start(bf16[1,512,1024]{2,1,0:T(8,128)(2,1)} %param.33) | copy-start | bytes 3145732
  301.8 7.6 %copy-start.56 = (bf16[512,4096]{1,0:T(8,128)(2,1)S(1)}, bf16[512,4096]{1,0:T(8,128)(2,1)}, u32[]{:S(2)}) copy-start(bf16[512,4096]{1,0:T(8,128)(2,1)} %get-tuple-element.101) | copy-start | bytes 12582916
  316.1 164.4 %copy-start.21 = (bf16[512,1024]{1,0:T(8,128)(2,1)S(1)}, bf16[512,1024]{1,0:T(8,128)(2,1)}, u32[]{:S(2)}) copy-start(bf16[512,1024]{1,0:T(8,128)(2,1)} %get-tuple-element.70) | copy-start | bytes 3145732
  477.5 4.1 copy-start.34
  477.5 4.7 copy-start.33
  477.5 5.4 %copy-start.32 = (f32[32,1024]{1,0:T(8,128)S(1)}, f32[32,1024]{1,0:T(8,128)}, u32[]{:S(2)}) copy-start(f32[32,1024]{1,0:T(8,128)} %get-tuple-element.217) | copy-start | bytes 393220
  477.5 6.0 %copy-start.31 = (f32[32,1024]{1,0:T(8,128)S(1)}, f32[32,1024]{1,0:T(8,128)}, u32[]{:S(2)}) copy-start(f32[32,1024]{1,0:T(8,128)} %get-tuple-element.219) | copy-start | bytes 393220
  477.5 6.7 %copy-start.30 = (f32[32,1024]{1,0:T(8,128)S(1)}, f32[32,1024]{1,0:T(8,128)}, u32[]{:S(2)}) copy-start(f32[32,1024]{1,0:T(8,128)} %get-tuple-element.223) | copy-start | bytes 393220
  477.5 7.3 %copy-start.29 = (f32[32,1024]{1,0:T(8,128)S(1)}, f32[32,1024]{1,0:T(8,128)}, u32[]{:S(2)}) copy-start(f32[32,1024]{1,0:T(8,128)} %get-tuple-element.225) | copy-start | bytes 393220
  477.5 8.0 %copy-start.28 = (f32[32,1024]{1,0:T(8,128)S(1)}, f32[32,1024]{1,0:T(8,128)}, u32[]{:S(2)}) copy-start(f32[32,1024]{1,0:T(8,128)} %get-tuple-element.226) | copy-start | bytes 393220
  477.5 8.6 %copy-start.27 = (f32[32,1024]{1,0:T(8,128)S(1)}, f32[32,1024]{1,0:T(8,128)}, u32[]{:S(2)}) copy-start(f32[32,1024]{1,0:T(8,128)} %get-tuple-element.228) | copy-start | bytes 393220
  480.6 6.2 %copy-start.25 = (f32[32,4096]{1,0:T(8,128)S(1)}, f32[32,4096]{1,0:T(8,128)}, u32[]{:S(2)}) copy-start(f32[32,4096]{1,0:T(8,128)} %get-tuple-element.232) | copy-start | bytes 1572868
  480.6 7.0 %copy-start.24 = (f32[128,1024]{1,0:T(8,128)S(1)}, f32[128,1024]{1,0:T(8,128)}, u32[]{:S(2)}) copy-start(f32[128,1024]{1,0:T(8,128)} %get-tuple-element.234) | copy-start | bytes 1572868
  (23 other events, 50.7 us)

commit v4 on v3

--- a/solution.py
+++ b/solution.py
@@ -47,8 +47,8 @@
     )
     return (
         inner_part * inv_std,
-        jnp.sum(grad_norm * unit_rows, axis=0),
-        jnp.sum(grad_norm, axis=0),
+        jnp.sum(grad_norm * unit_rows, axis=0, keepdims=True),
+        jnp.sum(grad_norm, axis=0, keepdims=True),
     )
 
 
@@ -273,9 +273,9 @@
     return loads
 
 
-def plan_sends(bits, orders, sizes, growing, add_rate):
+def plan_sends(bits, orders, sizes, growing, add_rate, begin=None):
     count = len(bits)
-    ready = [(0.0, unit, 0) for unit in range(len(orders))]
+    ready = [(begin[unit] if begin else 0.0, unit, 0) for unit in range(len(orders))]
     free = {}
     plan = []
     arrive = {}
@@ -330,146 +330,6 @@
     return (len(range(*rows.indices(block[0]))), len(range(*cols.indices(block[1]))))
 
 
-def scatter_kernel(bits, units, orders, plan, n_arrays, n_units, *refs):
-    count = len(bits)
-    sources = refs[:n_arrays]
-    results = refs[n_arrays : 2 * n_arrays]
-    held = refs[2 * n_arrays : 2 * n_arrays + n_units]
-    boxes = refs[2 * n_arrays + n_units : 2 * n_arrays + n_units + n_units * count]
-    totals = refs[2 * n_arrays + n_units + n_units * count : -4]
-    send_sem, recv_sem, load_sem, store_sem = refs[-4:]
-    mine = my_bits(bits)
-
-    def load(unit):
-        array, rows, cols = units[unit]
-        first = orders[unit][0]
-        where = tuple(mine[b] if b == first else slice(None) for b in range(count))
-        return pltpu.make_async_copy(
-            sources[array].at[where + (rows, cols)], held[unit], load_sem.at[unit]
-        )
-
-    for unit in range(n_units):
-        load(unit).start()
-    greet(bits, mine)
-
-    def message(unit, stage):
-        array, rows, cols = units[unit]
-        order = orders[unit]
-        now = order[stage]
-        where = []
-        for b in range(count):
-            if b == now:
-                where.append(1 - mine[b])
-            elif b in order[:stage]:
-                where.append(mine[b])
-            else:
-                where.append(slice(None))
-        if stage == 0:
-            source = sources[array].at[tuple(where) + (rows, cols)]
-        else:
-            source = held[unit].at[tuple(w for b, w in enumerate(where) if b != order[0])]
-        return pltpu.make_async_remote_copy(
-            src_ref=source,
-            dst_ref=boxes[unit * count + stage],
-            send_sem=send_sem.at[unit, stage],
-            recv_sem=recv_sem.at[unit, stage],
-            device_id=partner(bits, mine, now),
-            device_id_type=MESH_ID,
-        )
-
-    def add(unit, stage):
-        order = orders[unit]
-        message(unit, stage).wait_recv()
-        if stage == 0:
-            load(unit).wait()
-        box = boxes[unit * count + stage]
-        open_bits = [b for b in range(count) if b not in order[: stage + 1]]
-        blocks = 2 ** len(open_bits)
-
-        def one(block, carry):
-            where = []
-            spot = []
-            for b in range(count):
-                if b == order[0]:
-                    continue
-                if b in open_bits:
-                    digit = (block // 2 ** (len(open_bits) - 1 - open_bits.index(b))) % 2
-                    where.append(digit)
-                    spot.append(digit)
-                else:
-                    where.append(mine[b])
-            where, spot = tuple(where), tuple(spot)
-            total = held[unit][where].astype(jnp.float32) + box[spot].astype(jnp.float32)
-            if stage == count - 1:
-                totals[unit][...] = total
-            else:
-                held[unit][where] = total.astype(held[unit].dtype)
-            return carry
-
-        if blocks == 1:
-            one(0, 0)
-        else:
-            lax.fori_loop(0, blocks, one, 0)
-
-    def store(unit):
-        array, rows, cols = units[unit]
-        return pltpu.make_async_copy(
-            totals[unit], results[array].at[rows, cols], store_sem.at[unit]
-        )
-
-    for _, unit, stage in plan:
-        if stage > 0:
-            add(unit, stage - 1)
-        message(unit, stage).start()
-    for unit in range(n_units):
-        add(unit, count - 1)
-        store(unit).start()
-    for unit in range(n_units):
-        store(unit).wait()
-        for stage in range(count):
-            message(unit, stage).wait_send()
-
-
-def scatter_all(mesh, terms, units, collective_id):
-    bits = bit_table(mesh)
-    routes = route_orders(bits)
-    count = len(bits)
-    orders = [routes[u % 2][::-1] for u in range(len(units))]
-    shapes = [unit_shape([t.shape[count:] for t in terms], unit) for unit in units]
-    kinds = [terms[array].dtype for array, _, _ in units]
-    sizes = [s[0] * s[1] * kind.itemsize for s, kind in zip(shapes, kinds)]
-    plan, _ = plan_sends(bits, orders, sizes, False, 1000e3)
-    n = len(terms)
-    n_units = len(units)
-    sems = (n_units, count)
-    scratch = [
-        pltpu.VMEM((2,) * (count - 1) + shapes[u], kinds[u]) for u in range(n_units)
-    ]
-    for u in range(n_units):
-        for stage in range(count):
-            scratch.append(pltpu.VMEM((2,) * (count - 1 - stage) + shapes[u], kinds[u]))
-    scratch += [pltpu.VMEM(shapes[u], jnp.float32) for u in range(n_units)]
-    scratch += [
-        pltpu.SemaphoreType.DMA(sems),
-        pltpu.SemaphoreType.DMA(sems),
-        pltpu.SemaphoreType.DMA((n_units,)),
-        pltpu.SemaphoreType.DMA((n_units,)),
-    ]
-    return pl.pallas_call(
-        functools.partial(scatter_kernel, bits, units, orders, plan, n, n_units),
-        out_shape=[jax.ShapeDtypeStruct(t.shape[count:], jnp.float32) for t in terms],
-        in_specs=[pl.BlockSpec(memory_space=pltpu.HBM)] * n,
-        out_specs=[pl.BlockSpec(memory_space=pltpu.HBM)] * n,
-        scratch_shapes=scratch,
-        compiler_params=pltpu.CompilerParams(
-            collective_id=collective_id,
-            has_side_effects=True,
-            vmem_limit_bytes=60 * 1024 * 1024,
-        ),
-        name="scatter_grads",
-    )(*terms)
-
-
 ERF_RATE = 0.3275911
 ERF_TERMS = (0.254829592, -0.284496736, 1.421413741, -1.453152027, 1.061405429)
 
@@ -553,6 +413,23 @@
     pieces.append(loose[-1][...].astype(jnp.float32).reshape(1, VEC_LANES))
     pieces.append(jnp.zeros((VEC_ROWS - len(pieces), VEC_LANES), jnp.float32))
     pack[...] = jnp.concatenate(pieces, axis=0).astype(pack.dtype)
+
+
+def unpack_table(vecs, table, bits, width, hidden_row=None):
+    count = len(bits)
+    devices = 2**count
+    share = devices * VEC_LANES // width
+    spots = [tuple((d >> (count - 1 - b)) & 1 for b in range(count)) for d in range(devices)]
+    for group in range(width // VEC_LANES):
+        total = None
+        for d in range(group * share, (group + 1) * share):
+            block = vecs[spots[d]].astype(jnp.float32)
+            total = block if total is None else total + block
+        table[:, pl.ds(group * VEC_LANES, VEC_LANES)] = total
+    if hidden_row is not None:
+        for d in range(devices):
+            block = vecs[spots[d]].astype(jnp.float32)
+            hidden_row[pl.ds(0, 1), pl.ds(d * VEC_LANES, VEC_LANES)] = block[N_VECS - 1 : N_VECS]
 
 
 def forward_kernel(bits, units, orders, plan, arrive, n_arrays, heads, *refs):
@@ -658,18 +535,7 @@
 
     clock.until(0.0)
     fetch(0, vecs, 0)
-    for group in range(width // VEC_LANES):
-        share = VEC_LANES // lanes_each
-        total = None
-        for d in range(group * share, (group + 1) * share):
-            where = tuple((d >> (count - 1 - b)) & 1 for b in range(count))
-            block = vecs[where].astype(jnp.float32)
-            total = block if total is None else total + block
-        table[:, pl.ds(group * VEC_LANES, VEC_LANES)] = total
-    for d in range(devices):
-        where = tuple((d >> (count - 1 - b)) & 1 for b in range(count))
-        block = vecs[where].astype(jnp.float32)
-        hidden_row[pl.ds(0, 1), pl.ds(d * VEC_LANES, VEC_LANES)] = block[13:14]
+    unpack_table(vecs, table, bits, width, hidden_row)
     load_x.wait()
     load_mem.wait()
     norm_into(vec(0), vec(1), x)
@@ -851,10 +717,649 @@
     return got[:n], got[n:]
 
 
-MATS = (2, 4, 5, 7, 11, 13, 14, 16, 20, 22)
+class Deferred(Schedule):
+    def __init__(self, plan, issue):
+        super().__init__(list(plan), issue)
+        self.made = set()
+
+    def due(self):
+        items, rest, held_back = [], [], set()
+        for item in self.plan:
+            when, unit, stage = item
+            if unit in self.made and unit not in held_back and when <= self.now:
+                items.append((unit, stage))
+            else:
+                held_back.add(unit)
+                rest.append(item)
+        self.plan = rest
+        return items
+
+    def finish(self, unit, last=99):
+        late = [when for when, u, stage in self.plan if u == unit and stage <= last]
+        if late:
+            self.until(max(late))
+
+
+def backward_pair(refs, accs, total_of, spans, length, scale, lanes):
+    q_ref, k_ref, v_ref, g_ref = refs
+    dk_acc, dv_acc = accs
+    keys_all = k_ref.shape[0]
+    half = (dk_acc.shape[1]) // 2
+    for step, (start, size, keys) in enumerate(spans):
+        part_rows = pl.ds(start, size)
+        q2 = q_ref[part_rows, lanes]
+        g2 = g_ref[part_rows, lanes]
+        k2 = k_ref[pl.ds(0, keys), lanes]
+        v2 = v_ref[pl.ds(0, keys), lanes]
+        kt = k2.T
+        dk, dv, dqt = None, None, []
+        for head in (0, 1):
+            qm = lane_half(q2, head, half)
+            gm = lane_half(g2, head, half)
+            raw = dot_nt(k2, qm)
+            probs = jnp.exp2(raw * (scale * LOG2E) - total_of(head, start, size))
+            if length is not None:
+                key_pos = lax.broadcasted_iota(jnp.int32, raw.shape, 0)
+                probs = jnp.where(key_pos <= limit_row(start, size, length), probs, 0.0)
+            grad = dot_nt(v2, gm)
+            part = probs * grad
+            dot_row = jnp.sum(part, axis=0, keepdims=True)
+            score = ((part - probs * dot_row) * scale).astype(jnp.bfloat16)
+            dvh = dot_nn(probs.astype(jnp.bfloat16), gm)
+            dkh = dot_nn(score, qm)
+            dv = dvh if dv is None else dv + dvh
+            dk = dkh if dk is None else dk + dkh
+            dqt.append(dot_nn(kt[head * half : (head + 1) * half], score))
+        q_ref[part_rows, lanes] = jnp.concatenate(dqt, axis=0).T.astype(jnp.bfloat16)
+        if step == 0:
+            dk_acc[pl.ds(0, keys), :] = dk
+            dv_acc[pl.ds(0, keys), :] = dv
+        else:
+            dk_acc[pl.ds(0, keys), :] += dk
+            dv_acc[pl.ds(0, keys), :] += dv
+    every_key = pl.ds(0, keys_all)
+    k_ref[every_key, lanes] = dk_acc[every_key, :].astype(jnp.bfloat16)
+    v_ref[every_key, lanes] = dv_acc[every_key, :].astype(jnp.bfloat16)
+
+
+BACK_INPUTS = ("dz", "tokens", "memory", "lengths")
+BACK_INPUTS += ("q", "k", "v", "a", "total", "h1", "cq", "ck", "cv", "ca", "ctotal", "h2", "g", "rate")
+BACK_INPUTS += ("wvec", "wq", "wk", "wv", "wck", "wcv", "wo", "wcq", "wco", "win", "wout")
+MADE_AT = (5.0, 8.0, 11.0, 14.0, 21.0, 26.0, 31.0, 36.0, 44.0)
+MADE_AT += (70.0, 72.0, 74.0, 88.0, 112.0, 114.0, 116.0, 128.0)
+TALL_UNITS = 4
+WIDE_HELD = 6
+WIDE_BOXES = 3
+TALL_BOXES = 2
+SUM_SLOTS = 4
+
+
+def ring_place(unit, n_wide):
+    if unit < TALL_UNITS:
+        return "tall", unit
+    if unit < TALL_UNITS + n_wide:
+        return "wide", unit - TALL_UNITS
+    return "vec", 0
+
+
+def backward_kernel(bits, orders, plan, outs_of, heads, *refs):
+    count = len(bits)
+    n_units = len(orders)
+    n_wide = n_units - TALL_UNITS - 1
+    given = dict(zip(BACK_INPUTS, refs[: len(BACK_INPUTS)]))
+    refs = refs[len(BACK_INPUTS) :]
+    tokens_grad, memory_grad = refs[:2]
+    results = refs[2:13]
+    refs = refs[13:]
+    bdz, n, acc, dh, hb, wide_a, wide_b, stage_a, stage_b = refs[:9]
+    held_tall, held_wide, box_tall, box_wide = refs[9:13]
+    rest_tall, rest_wide = refs[13 : 13 + count - 1], refs[13 + count - 1 : 13 + 2 * (count - 1)]
+    refs = refs[13 + 2 * (count - 1) :]
+    vec_stage, vec_held = refs[:2]
+    vec_boxes = refs[2 : 2 + count]
+    refs = refs[2 + count :]
+    sum_tall, sum_wide, sum_vec, vgrad, hgrad, table, vecs, tot, dk_acc, dv_acc = refs[:10]
+    send_sem, recv_sem, own_sem, store_sem, load_sem, w_sem, credit = refs[10:]
+    wides, stages = (wide_a, wide_b), (stage_a, stage_b)
+    vgrad[...] = jnp.zeros_like(vgrad)
+    mine = my_bits(bits)
+    core = count - 1
+    rows, width = bdz.shape
+    every = (slice(None),) * count
+    tall_stage = [None]
+
+    loads = {}
+
+    def load(name, source, target):
+        loads[name] = pltpu.make_async_copy(source, target, load_sem.at[len(loads)])
+        loads[name].start()
+
+    load("dz", given["dz"], bdz)
+    load("vecs", given["wvec"], vecs)
+    load("h2", given["h2"], hb)
+    greet(bits, mine)
+
+    def held_of(unit):
+        kind, i = ring_place(unit, n_wide)
+        if kind == "vec":
+            return vec_held
+        return held_tall.at[i] if kind == "tall" else held_wide.at[i % WIDE_HELD]
+
+    def stage_of(unit):
+        kind, i = ring_place(unit, n_wide)
+        if kind == "vec":
+            return vec_stage
+        return tall_stage[i % len(tall_stage)] if kind == "tall" else stages[i % len(stages)]
+
+    def box_of(unit, stage):
+        kind, i = ring_place(unit, n_wide)
+        if kind == "vec":
+            return vec_boxes[stage]
+        if kind == "tall":
+            return box_tall.at[i % TALL_BOXES] if stage == 0 else rest_tall[stage - 1].at[i]
+        return box_wide.at[i % WIDE_BOXES] if stage == 0 else rest_wide[stage - 1].at[i]
+
+    def own_copy(unit):
+        half = stage_of(unit).at[(slice(None),) * core + (mine[core],)]
+        return pltpu.make_async_copy(half, held_of(unit), own_sem.at[unit])
+
+    def message(unit, stage):
+        order = orders[unit]
+        now = order[stage]
+        where = []
+        for b in range(count):
+            if b == now:
+                where.append(1 - mine[b])
+            elif b in order[:stage]:
+                where.append(mine[b])
+            else:
+                where.append(slice(None))
+        if stage == 0:
+            source = stage_of(unit).at[tuple(where)]
+        else:
+            source = held_of(unit).at[tuple(where[:core])]
+        return pltpu.make_async_remote_copy(
+            src_ref=source,
+            dst_ref=box_of(unit, stage),
+            send_sem=send_sem.at[unit, stage],
+            recv_sem=recv_sem.at[unit, stage],
+            device_id=partner(bits, mine, now),
+            device_id_type=MESH_ID,
+        )
+
+    sent = set()
+    copied = set()
+
+    def own_ready(unit):
+        if unit not in copied:
+            copied.add(unit)
+            own_copy(unit).wait()
+
+    def drained(unit, stage):
+        if (unit, stage) not in sent:
+            sent.add((unit, stage))
+            message(unit, stage).wait_send()
+
+    def next_in_ring(unit):
+        kind, i = ring_place(unit, n_wide)
+        if kind == "tall":
+            return i + TALL_BOXES < TALL_UNITS
+        return kind == "wide" and i + WIDE_BOXES < n_wide
+
+    def credit_of(unit):
+        kind, i = ring_place(unit, n_wide)
+        return credit.at[i % TALL_BOXES] if kind == "tall" else credit.at[TALL_BOXES + i % WIDE_BOXES]
+
+    def add(unit, stage, target=None):
+        order = orders[unit]
+        message(unit, stage).wait_recv()
+        if stage == 0:
+            own_ready(unit)
+        held, box = held_of(unit), box_of(unit, stage)
+        open_bits = [b for b in range(count) if b not in order[: stage + 1]]
+        blocks = 2 ** len(open_bits)
+
+        def one(block, carry):
+            where, spot = [], []
+            for b in range(core):
+                if b in open_bits:
+                    digit = (block // 2 ** (len(open_bits) - 1 - open_bits.index(b))) % 2
+                    where.append(digit)
+                    spot.append(digit)
+                else:
+                    where.append(mine[b])
+            where, spot = tuple(where), tuple(spot)
+            if target is not None:
+                total = held[where].astype(jnp.float32) + box[spot].astype(jnp.float32)
+                target[...] = total
+            else:
+                held[where] = held[where] + box[spot]
+            return carry
+
+        if blocks == 1:
+            one(0, 0)
+        else:
+            lax.fori_loop(0, blocks, one, 0)
+        if stage == 0 and next_in_ring(unit):
+            pl.semaphore_signal(
+                credit_of(unit), inc=1, device_id=partner(bits, mine, core), device_id_type=MESH_ID
+            )
+
+    stored = {}
+
+    def sum_of(unit):
+        kind, i = ring_place(unit, n_wide)
+        if kind == "vec":
+            return sum_vec
+        return sum_tall.at[i] if kind == "tall" else sum_wide.at[i % SUM_SLOTS]
+
+    def store(unit):
+        array, top, left = outs_of[unit]
+        return pltpu.make_async_copy(
+            sum_of(unit), results[array].at[top, left], store_sem.at[unit]
+        )
+
+    def end(unit):
+        kind, i = ring_place(unit, n_wide)
+        if kind == "wide":
+            if i % SUM_SLOTS in stored:
+                store(stored[i % SUM_SLOTS]).wait()
+            stored[i % SUM_SLOTS] = unit
+        add(unit, count - 1, sum_of(unit))
+        store(unit).start()
+
+    def issue(unit, stage):
+        if stage == count:
+            end(unit)
+        else:
+            add(unit, stage - 1)
+            message(unit, stage).start()
+
+    clock = Deferred(plan, issue)
+
+    def made(unit):
+        kind, i = ring_place(unit, n_wide)
+        if kind == "wide" and i >= WIDE_HELD:
+            clock.finish(unit - WIDE_HELD)
+            for stage in range(1, count):
+                drained(unit - WIDE_HELD, stage)
+        own_copy(unit).start()
+        ring = TALL_BOXES if kind == "tall" else WIDE_BOXES
+        if kind != "vec" and i >= ring:
+            clock.finish(unit - ring, 1)
+            pl.semaphore_wait(credit_of(unit), 1)
+        message(unit, 0).start()
+        clock.made.add(unit)
+        clock.spend(0.0)
+
+    def stage_free(unit):
+        kind, i = ring_place(unit, n_wide)
+        depth = len(tall_stage) if kind == "tall" else len(stages)
+        if i >= depth:
+            own_ready(unit - depth)
+            drained(unit - depth, 0)
+
+    whole = every + (slice(None), slice(None))
+    hidden = hgrad.shape[1]
+    blocks = hidden // width
+    names = [("win", every + (slice(None), slice(j * width, (j + 1) * width))) for j in range(blocks)]
+    names += [(name, whole) for name in ("wco", "wcq", "wck", "wcv", "wo", "wq", "wk", "wv")]
+    weights = [
+        pltpu.make_async_copy(given[name].at[where], wides[i % 2], w_sem.at[i])
+        for i, (name, where) in enumerate(names)
+    ]
+    weights[0].start()
+    weights[1].start()
+
+    def back_through(i, lhs, write, took=1.4):
+        weights[i].wait()
+        slot = wides[i % 2]
+
+        def body(t):
+            part = slot[t].reshape(width // 2, width)
+            write(pl.ds(pl.multiple_of(t * (width // 2), width // 2), width // 2), dot_nt(lhs(), part))
+
+        clock.loop(2, took / 2, body)
+        if i + 2 < len(weights):
+            weights[i + 2].start()
+
+    def produce(unit, lhs, rhs, took=1.5):
+        stage_free(unit)
+        slot = stage_of(unit)
+        half = width // 2
+
+        def body(t):
+            start = pl.multiple_of(t * half, half)
+            cols = pl.ds(start, half)
+            tile = dot_tn(lhs(), rhs(start, half)).astype(jnp.bfloat16)
+            slot[every + (slice(None), cols)] = tile.reshape(slot.shape[:-1] + (half,))
+
+        clock.loop(2, took / 2, body)
+        made(unit)
+
+    def column_sums(ref, rows_now, target, at):
+        ones = jnp.ones((8, rows_now), jnp.bfloat16)
+        target[pl.ds(at, 1), :] = dot_nn(ones, ref)[0:1]
+
+    loads["vecs"].wait()
+    unpack_table(vecs, table, bits, width)
+
+    def vec(i):
+        return table[pl.ds(i, 1), :]
+
+    def norm_rows(source, gain, shift):
+        def body(i):
+            part = pl.ds(pl.multiple_of(i * ROWS_STEP, ROWS_STEP), ROWS_STEP)
+            r = source[part, :].astype(jnp.float32)
+            n[part, :] = normalize(r, vec(gain), vec(shift))[0].astype(jnp.bfloat16)
+
+        clock.loop(rows // ROWS_STEP, 0.4, body)
+
+    def norm_back(source, gain, base):
+        vgrad[pl.ds(gain, 2), :] = jnp.zeros((2, width), jnp.float32)
+
+        def body(i):
+            part = pl.ds(pl.multiple_of(i * ROWS_STEP, ROWS_STEP), ROWS_STEP)
+            r = source[part, :].astype(jnp.float32)
+            _, unit_rows, inv_std = normalize(r, vec(gain), vec(gain))
+            back, gain_sum, shift_sum = normalize_back(acc[part, :], unit_rows, inv_std, vec(gain))
+            vgrad[pl.ds(gain, 1), :] += gain_sum
+            vgrad[pl.ds(gain + 1, 1), :] += shift_sum
+            total = base(part) + back
+            dh[part, :] = total
+            bdz[part, :] = total.astype(jnp.bfloat16)
+
+        clock.loop(rows // ROWS_STEP, 0.8, body)
+
+    def feed_phase(big, rate, wrow, tall_a):
+        tall_stage[0] = tall_a
+        load("g", given["g"], big)
+
+        def rate_copy(j):
+            cols = pl.ds(j * width, width)
+            return pltpu.make_async_copy(given["rate"].at[:, cols], rate, load_sem.at[20 + j])
+
+        def row_copy(j):
+            return pltpu.make_async_copy(given["wout"].at[j // 2, j % 2], wrow, load_sem.at[24 + j])
+
+        rate_copy(0).start()
+        row_copy(0).start()
+        loads["dz"].wait()
+        loads["g"].wait()
+        tall_cols = tall_a.shape[-1]
+        for j in range(TALL_UNITS):
+            stage_free(j)
+            slot = stage_of(j)
+
+            def body(t, j=j, slot=slot):
+                part = big[:, pl.ds(pl.multiple_of(t * width, width), width)]
+                tile = dot_tn(part, bdz[:, pl.ds(j * tall_cols, tall_cols)]).astype(jnp.bfloat16)
+                slot[t // 2, t % 2] = tile.reshape(slot.shape[2:])
+
+            clock.loop(4, 0.45, body)
+            made(j)
+        column_sums(bdz[...], rows, vgrad, 12)
+        loads["h2"].wait()
+        norm_rows(hb, 10, 11)
+        for j in range(blocks):
+            rate_copy(j).wait()
+            row_copy(j).wait()
+            half = width // 2
+
+            def body(t, j=j):
+                spot = pl.ds(pl.multiple_of(j * width + t * half, half), half)
+                weight = wrow[t].reshape(half, width)
+                slope = rate[:, pl.ds(pl.multiple_of(t * half, half), half)].astype(jnp.float32)
+                big[:, spot] = (dot_nt(bdz[...], weight) * slope).astype(jnp.bfloat16)
+
+            clock.loop(2, 0.8, body)
+            if j + 1 < blocks:
+                rate_copy(j + 1).start()
+                row_copy(j + 1).start()
+            block = pl.ds(j * width, width)
+            hgrad[pl.ds(0, 1), block] = dot_nn(jnp.ones((8, rows), jnp.bfloat16), big[:, block])[0:1]
+            produce(
+                TALL_UNITS + j,
+                lambda: n[...],
+                lambda start, size, j=j: big[:, pl.ds(pl.multiple_of(j * width + start, size), size)],
+            )
+
+            def write(cols, value, j=j):
+                top = pl.ds(0, rows)
+                if j == 0:
+                    acc[top, cols] = value
+                else:
+                    acc[top, cols] += value
+
+            back_through(j, lambda j=j: big[:, pl.ds(j * width, width)], write)
+        norm_back(hb, 10, lambda part: bdz[part, :].astype(jnp.float32))
+        for unit in range(TALL_UNITS):
+            own_ready(unit)
+            drained(unit, 0)
+
+    def attention_phase(bq, bk, bv, bg, mem, ba):
+        load("h1", given["h1"], hb)
+        load("ca", given["ca"], ba)
+        load("cq", given["cq"], bq)
+        load("ck", given["ck"], bk)
+        load("cv", given["cv"], bv)
+        load("ctotal", given["ctotal"], tot)
+        load("memory", given["memory"], mem)
+
+        def into(ref, size=rows):
+            def write(cols, value):
+                ref[pl.ds(0, size), cols] = value.astype(ref.dtype)
+
+            return write
+
+        def attend(keys, masked):
+            pair = 2 * (width // heads)
+            chunk = rows // 2
+            spans = [(s, chunk, s + chunk if masked else keys) for s in range(0, rows, chunk)]
+            key_rows = pl.ds(0, keys)
+            refs_now = (bq, bk.at[key_rows], bv.at[key_rows], bg)
+
+            def body(p):
+                lanes = pl.ds(pl.multiple_of(p * pair, pair), pair)
+                backward_pair(
+                    refs_now,
+                    (dk_acc, dv_acc),
+                    lambda head, start, size: tot[p, pl.ds(head, 1), pl.ds(start, size)],
+                    spans[::-1],
+                    length if masked else None,
+                    (width // heads) ** -0.5,
+                    lanes,
+                )
+
+            clock.loop(heads // 2, 2.5, body)
+
+        def picked(ref, size=rows):
+            return lambda start, width_now: ref[pl.ds(0, size), pl.ds(start, width_now)]
+
+        first = TALL_UNITS + blocks
+        keys = mem.shape[0]
+        length = given["lengths"][0]
+        at = blocks
+        back_through(at, lambda: bdz[...], into(bg))
+        loads["ca"].wait()
+        produce(first, lambda: ba[...], picked(bdz))
+        column_sums(bdz[...], rows, vgrad, 9)
+        for name in ("cq", "ck", "cv", "ctotal"):
+            loads[name].wait()
+        attend(keys, False)
+        load("a", given["a"], ba)
+        load("total", given["total"], tot)
+        loads["h1"].wait()
+        norm_rows(hb, 5, 6)
+        produce(first + 1, lambda: n[...], picked(bq))
+        loads["memory"].wait()
+        produce(first + 2, lambda: mem[...], picked(bk, keys), 1.7)
+        produce(first + 3, lambda: mem[...], picked(bv, keys), 1.7)
+        column_sums(bq[...], rows, vgrad, 7)
+        column_sums(bv[...], keys, vgrad, 8)
+        back_through(at + 1, lambda: bq[...], into(acc))
+        load("q", given["q"], bq)
+        norm_back(hb, 5, lambda part: dh[part, :])
+        back_through(at + 2, lambda: bk[...], into(acc, keys))
+
+        def more(size):
+            def write(cols, value):
+                acc[pl.ds(0, size), cols] += value
+
+            return write
+
+        back_through(at + 3, lambda: bv[...], more(keys))
+        put_memory = pltpu.make_async_copy(acc, memory_grad, load_sem.at[28])
+        put_memory.start()
+        top = pl.ds(0, rows)
+        load("k", given["k"], bk.at[top])
+        load("v", given["v"], bv.at[top])
+        back_through(at + 4, lambda: bdz[...], into(bg))
+        loads["a"].wait()
+        produce(first + 4, lambda: ba[...], picked(bdz))
+        column_sums(bdz[...], rows, vgrad, 4)
+        for name in ("q", "k", "v", "total"):
+            loads[name].wait()
+        load("tokens", given["tokens"], ba)
+        attend(rows, True)
+        loads["tokens"].wait()
+        norm_rows(ba, 0, 1)
+        for i, ref in enumerate((bq, bk, bv)):
+            produce(first + 5 + i, lambda: n[...], picked(ref))
+        column_sums(bq[...], rows, vgrad, 2)
+        column_sums(bv[top, :], rows, vgrad, 3)
+        put_memory.wait()
+        back_through(at + 5, lambda: bq[...], into(acc))
+        back_through(at + 6, lambda: bk[top, :], more(rows))
+        back_through(at + 7, lambda: bv[top, :], more(rows))
+        norm_back(ba, 0, lambda part: dh[part, :])
+
+    ff_dtype = jnp.bfloat16
+    pl.run_scoped(
+        feed_phase,
+        pltpu.VMEM((rows, hidden), ff_dtype),
+        pltpu.VMEM((rows, width), ff_dtype),
+        pltpu.VMEM(given["wout"].shape[2:], ff_dtype),
+        pltpu.VMEM((2,) * count + held_tall.shape[-2:], ff_dtype),
+    )
+    key_rows = given["memory"].shape[0]
+    pl.run_scoped(
+        attention_phase,
+        pltpu.VMEM((rows, width), ff_dtype),
+        pltpu.VMEM((key_rows, width), ff_dtype),
+        pltpu.VMEM((key_rows, width), ff_dtype),
+        pltpu.VMEM((rows, width), ff_dtype),
+        pltpu.VMEM((key_rows, width), ff_dtype),
+        pltpu.VMEM((rows, width), ff_dtype),
+    )
+    put_tokens = pltpu.make_async_copy(dh, tokens_grad, load_sem.at[29])
+    put_tokens.start()
+    devices = 2**count
+    share = devices // (width // VEC_LANES)
+    for d in range(devices):
+        where = tuple((d >> (count - 1 - b)) & 1 for b in range(count))
+        vec_stage[where] = vgrad[:, pl.ds(d // share * VEC_LANES, VEC_LANES)]
+        vec_stage[where + (pl.ds(13, 1),)] = hgrad[:, pl.ds(d * VEC_LANES, VEC_LANES)]
+    made(n_units - 1)
+    clock.until(1e9)
+    put_tokens.wait()
+    waiting = set(stored.values()) | set(range(TALL_UNITS)) | {n_units - 1}
+    for unit in range(n_units):
+        if unit in waiting:
+            store(unit).wait()
+        for stage in range(count):
+            drained(unit, stage)
+
+
+def fused_backward(mesh, dz, tokens, memory, lengths, saved, gathered, heads, collective_id):
+    bits = bit_table(mesh)
+    count = len(bits)
+    routes = route_orders(bits)
+    rows, width = tokens.shape
+    keys = memory.shape[0]
+    shards = [w.shape[count:] for w in gathered[1:]]
+    wide_block = shards[0]
+    tall_rows = shards[9][0]
+    hidden = shards[8][1]
+    tall_cols = width * wide_block[0] // tall_rows
+    tall_block = (tall_rows, tall_cols)
+    pack = (VEC_ROWS, VEC_LANES)
+    every = slice(None)
+    outs_of = [(9, every, slice(c, c + tall_cols)) for c in range(0, width, tall_cols)]
+    outs_of += [(8, every, slice(c, c + width)) for c in range(0, hidden, width)]
+    outs_of += [(i, every, every) for i in (7, 6, 3, 4, 5, 0, 1, 2, 10)]
+    n_units = len(outs_of)
+    n_wide = n_units - TALL_UNITS - 1
+    low = jnp.bfloat16
+    sizes = [2 * wide_block[0] * wide_block[1]] * (n_units - 1) + [4 * pack[0] * pack[1]]
+    orders = [routes[u % 2][::-1] for u in range(n_units)]
+    sends, finish = plan_sends(bits, orders, sizes, False, 1000e3, MADE_AT)
+    plan = [item for item in sends if item[2] > 0]
+    plan = sorted(plan + [(when, unit, count) for unit, when in finish.items()])
+    blocks = shards + [pack]
+    scratch = [
+        pltpu.VMEM((rows, width), low),
+        pltpu.VMEM((rows, width), low),
+        pltpu.VMEM((keys, width), jnp.float32),
+        pltpu.VMEM((rows, width), jnp.float32),
+        pltpu.VMEM((rows, width), jnp.float32),
+    ]
+    spots = (2,) * count
+    scratch += [pltpu.VMEM(spots + wide_block, low)] * 4
+    scratch += [
+        pltpu.VMEM((TALL_UNITS,) + spots[1:] + tall_block, low),
+        pltpu.VMEM((WIDE_HELD,) + spots[1:] + wide_block, low),
+        pltpu.VMEM((TALL_BOXES,) + spots[1:] + tall_block, low),
+        pltpu.VMEM((WIDE_BOXES,) + spots[1:] + wide_block, low),
+    ]
+    for number, block in ((TALL_UNITS, tall_block), (n_wide, wide_block)):
+        for stage in range(1, count):
+            scratch.append(pltpu.VMEM((number,) + (2,) * (count - 1 - stage) + block, low))
+    scratch += [pltpu.VMEM(spots + pack, jnp.float32), pltpu.VMEM(spots[1:] + pack, jnp.float32)]
+    for stage in range(count):
+        scratch.append(pltpu.VMEM((2,) * (count - 1 - stage) + pack, jnp.float32))
+    pair = 2 * (width // heads)
+    scratch += [
+        pltpu.VMEM((TALL_UNITS,) + tall_block, jnp.float32),
+        pltpu.VMEM((SUM_SLOTS,) + wide_block, jnp.float32),
+        pltpu.VMEM(pack, jnp.float32),
+        pltpu.VMEM((VEC_ROWS, width), jnp.float32),
+        pltpu.VMEM((1, hidden), jnp.float32),
+        pltpu.VMEM((VEC_ROWS, width), jnp.float32),
+        pltpu.VMEM(spots + pack, low),
+        pltpu.VMEM((heads // 2, 2, rows), jnp.float32),
+        pltpu.VMEM((keys, pair), jnp.float32),
+        pltpu.VMEM((keys, pair), jnp.float32),
+        pltpu.SemaphoreType.DMA((n_units, count)),
+        pltpu.SemaphoreType.DMA((n_units, count)),
+        pltpu.SemaphoreType.DMA((n_units,)),
+        pltpu.SemaphoreType.DMA((n_units,)),
+        pltpu.SemaphoreType.DMA((30,)),
+        pltpu.SemaphoreType.DMA((12,)),
+        pltpu.SemaphoreType.REGULAR((TALL_BOXES + WIDE_BOXES,)),
+    ]
+    hbm = pl.BlockSpec(memory_space=pltpu.HBM)
+    return pl.pallas_call(
+        functools.partial(backward_kernel, bits, orders, plan, outs_of, heads),
+        out_shape=[
+            jax.ShapeDtypeStruct((rows, width), jnp.float32),
+            jax.ShapeDtypeStruct((keys, width), jnp.float32),
+        ]
+        + [jax.ShapeDtypeStruct(b, jnp.float32) for b in blocks],
+        in_specs=[hbm, hbm, hbm, pl.BlockSpec(memory_space=pltpu.SMEM)]
+        + [hbm] * (len(BACK_INPUTS) - 4),
+        out_specs=[hbm] * (2 + len(blocks)),
+        scratch_shapes=scratch,
+        compiler_params=pltpu.CompilerParams(
+            collective_id=collective_id,
+            has_side_effects=True,
+            vmem_limit_bytes=62 * 1024 * 1024,
+        ),
+        name="backward_layer",
+    )(dz, tokens, memory, lengths, *saved, *gathered)
+
+
 MATS_ORDER = (2, 4, 5, 13, 14, 7, 11, 16, 20, 22)
-GRAD_ROWS = 8
-GRAD_LANES = 128
 VECS = (0, 1, 3, 6, 8, 9, 10, 12, 15, 17, 18, 19, 23, 21)
 
 
@@ -874,45 +1379,22 @@
     return tuple(lax.all_gather(s, BOTH, axis=0, tiled=True) for s in shards)
 
 
-def unpack_vectors(table, shards):
-    devices = table.size // (VEC_ROWS * VEC_LANES)
-    table = table.reshape(devices, VEC_ROWS, VEC_LANES)
+def spread(*grads):
+    return tuple(
+        lax.psum_scatter(g.astype(jnp.float32), BOTH, scatter_dimension=0, tiled=True)
+        for g in grads
+    )
+
+
+def own_vectors(block, position, shards):
     size = shards[0].shape[0]
-    share = VEC_LANES // size
-    narrow = table.reshape(devices // share, share, VEC_ROWS, VEC_LANES).astype(jnp.float32)
-    narrow = jnp.sum(narrow, axis=1).transpose(1, 0, 2).reshape(VEC_ROWS, devices * size)
-    full = [None] * len(shards)
+    spot = position % (VEC_LANES // size)
+    mine = lax.dynamic_slice(block, (0, spot * size), (VEC_ROWS, size))
+    owned = [None] * len(shards)
     for row, i in enumerate(VECS[:-1]):
-        full[i] = narrow[row]
-    full[VECS[-1]] = table[:, len(VECS) - 1].reshape(-1)
-    return full
-
-
-def spread(mesh, *grads):
-    devices = mesh.shape["dp"] * mesh.shape["fsdp"]
-    mats = [grads[i] for i in MATS]
-    if not can_route(mesh, mats[0].shape[0] // devices):
-        return tuple(
-            lax.psum_scatter(g.astype(jnp.float32), BOTH, scatter_dimension=0, tiled=True)
-            for g in grads
-        )
-    spots = (2,) * len(bit_table(mesh))
-    table = jnp.concatenate([grads[i].reshape(devices, -1) for i in VECS], axis=1)
-    spare = GRAD_ROWS * GRAD_LANES - table.shape[1]
-    table = jnp.pad(table, ((0, 0), (0, spare))).reshape(spots + (GRAD_ROWS, GRAD_LANES))
-    terms = [m.reshape(spots + (m.shape[0] // devices, m.shape[1])) for m in mats]
-    units = split_units([t.shape[-2:] for t in terms])
-    got = scatter_all(mesh, [table] + terms, units, 1)
-    flat = got[0].reshape(-1)
-    owned = [None] * len(grads)
-    start = 0
-    for i in VECS:
-        size = grads[i].shape[0] // devices
-        owned[i] = flat[start : start + size]
-        start += size
-    for i, value in zip(MATS, got[1:]):
-        owned[i] = value
-    return tuple(owned)
+        owned[i] = mine[row]
+    owned[VECS[-1]] = block[len(VECS) - 1]
+    return owned
 
 
 def on_device(
@@ -981,23 +1463,19 @@
     )
     if can_route(mesh, self_query.shape[0]):
         mats = [shard_set[i] for i in MATS_ORDER]
-        got, saved = fused_forward(
-            mesh, tokens[0], memory[0], lengths_now, mats, [shard_set[i] for i in VECS], HEADS, 0
+        vecs = [shard_set[i] for i in VECS]
+        gathered, saved = fused_forward(
+            mesh, tokens[0], memory[0], lengths_now, mats, vecs, HEADS, 0
         )
-        full_set = unpack_vectors(got[0], shard_set)
-        for i, value in zip(MATS_ORDER, got[1:]):
-            full_set[i] = value.reshape(-1, value.shape[-1])
-        (
-            query_low, key_low, value_low, self_low, self_total, after_self,
-            cquery_low, ckey_low, cvalue_low, cross_low, cross_total, after_cross,
-            hidden_low, hidden_rate, layer_out,
-        ) = saved
-        self_total, cross_total = self_total[None], cross_total[None]
-        layer_out = layer_out[None]
-        query_pages, key_pages, value_pages = query_low[None], key_low[None], value_low[None]
-        cquery_pages, ckey_pages, cvalue_pages = cquery_low[None], ckey_low[None], cvalue_low[None]
-    else:
-        full_set = collect(*shard_set)
+        got = fused_backward(
+            mesh, out_grad[0], tokens[0], memory[0], lengths_now, saved[:-1], gathered, HEADS, 1
+        )
+        position = lax.axis_index("dp") * mesh.shape["fsdp"] + lax.axis_index("fsdp")
+        owned = own_vectors(got[-1], position, shard_set)
+        for i, value in zip(MATS_ORDER, got[2:-1]):
+            owned[i] = value
+        return (saved[-1][None], got[0][None], got[1][None]) + tuple(owned)
+    full_set = collect(*shard_set)
     (
         gain_one,
         shift_one,
@@ -1027,47 +1505,46 @@
     norm_of = lambda r, g, b: normalize(r, g.astype(jnp.float32), b.astype(jnp.float32))
     first_norm, first_unit, first_std = norm_of(inputs, gain_one, shift_one)
     first_low = first_norm.astype(jnp.bfloat16)
-    if not can_route(mesh, self_query.shape[0]):
-        query_low = (product(first_low, query_mat) + query_vec.astype(jnp.float32)).astype(jnp.bfloat16)
-        key_low = product(first_low, key_mat).astype(jnp.bfloat16)
-        value_low = (product(first_low, value_mat) + value_vec.astype(jnp.float32)).astype(jnp.bfloat16)
-        query_pages = query_low.reshape(page_count, page_len, width)
-        key_pages = key_low.reshape(page_count, page_len, width)
-        value_pages = value_low.reshape(page_count, page_len, width)
-        self_mixed, self_total = attend_fwd(
-            query_pages, key_pages, value_pages, lengths_now, HEADS, 512
-        )
-        self_low = self_mixed.reshape(row_count, width)
-        after_self = inputs + product(self_low, out_mat) + out_vec.astype(jnp.float32)
-        second_norm, second_unit, second_std = normalize(
-            after_self, gain_two.astype(jnp.float32), shift_two.astype(jnp.float32)
-        )
-        second_low = second_norm.astype(jnp.bfloat16)
-        cquery_low = (product(second_low, cquery_mat) + cquery_vec.astype(jnp.float32)).astype(
-            jnp.bfloat16
-        )
-        ckey_low = product(mem_rows, ckey_mat).astype(jnp.bfloat16)
-        cvalue_low = (product(mem_rows, cvalue_mat) + cvalue_vec.astype(jnp.float32)).astype(
-            jnp.bfloat16
-        )
-        cquery_pages = cquery_low.reshape(page_count, page_len, width)
-        ckey_pages = ckey_low.reshape(page_count, mem_len, width)
-        cvalue_pages = cvalue_low.reshape(page_count, mem_len, width)
-        cross_mixed, cross_total = attend_fwd(
-            cquery_pages, ckey_pages, cvalue_pages, None, HEADS, 512
-        )
-        cross_low = cross_mixed.reshape(row_count, width)
-        after_cross = after_self + product(cross_low, cout_mat) + cout_vec.astype(jnp.float32)
-        third_norm, third_unit, third_std = normalize(
-            after_cross, gain_three.astype(jnp.float32), shift_three.astype(jnp.float32)
-        )
-        third_low = third_norm.astype(jnp.bfloat16)
-        hidden_pre = product(third_low, hidden_mat) + hidden_vec.astype(jnp.float32)
-        hidden_low, hidden_rate = gelu_parts(hidden_pre)
-        hidden_low = hidden_low.astype(jnp.bfloat16)
-        hidden_rate = hidden_rate.astype(jnp.bfloat16)
-        result = after_cross + product(hidden_low, final_mat) + final_vec.astype(jnp.float32)
-        layer_out = result.astype(jnp.bfloat16).reshape(page_count, page_len, width)
+    query_low = (product(first_low, query_mat) + query_vec.astype(jnp.float32)).astype(jnp.bfloat16)
+    key_low = product(first_low, key_mat).astype(jnp.bfloat16)
+    value_low = (product(first_low, value_mat) + value_vec.astype(jnp.float32)).astype(jnp.bfloat16)
+    query_pages = query_low.reshape(page_count, page_len, width)
+    key_pages = key_low.reshape(page_count, page_len, width)
+    value_pages = value_low.reshape(page_count, page_len, width)
+    self_mixed, self_total = attend_fwd(
+        query_pages, key_pages, value_pages, lengths_now, HEADS, 512
+    )
+    self_low = self_mixed.reshape(row_count, width)
+    after_self = inputs + product(self_low, out_mat) + out_vec.astype(jnp.float32)
+    second_norm, second_unit, second_std = normalize(
+        after_self, gain_two.astype(jnp.float32), shift_two.astype(jnp.float32)
+    )
+    second_low = second_norm.astype(jnp.bfloat16)
+    cquery_low = (product(second_low, cquery_mat) + cquery_vec.astype(jnp.float32)).astype(
+        jnp.bfloat16
+    )
+    ckey_low = product(mem_rows, ckey_mat).astype(jnp.bfloat16)
+    cvalue_low = (product(mem_rows, cvalue_mat) + cvalue_vec.astype(jnp.float32)).astype(
+        jnp.bfloat16
+    )
+    cquery_pages = cquery_low.reshape(page_count, page_len, width)
+    ckey_pages = ckey_low.reshape(page_count, mem_len, width)
+    cvalue_pages = cvalue_low.reshape(page_count, mem_len, width)
+    cross_mixed, cross_total = attend_fwd(
+        cquery_pages, ckey_pages, cvalue_pages, None, HEADS, 512
+    )
+    cross_low = cross_mixed.reshape(row_count, width)
+    after_cross = after_self + product(cross_low, cout_mat) + cout_vec.astype(jnp.float32)
+    third_norm, third_unit, third_std = normalize(
+        after_cross, gain_three.astype(jnp.float32), shift_three.astype(jnp.float32)
+    )
+    third_low = third_norm.astype(jnp.bfloat16)
+    hidden_pre = product(third_low, hidden_mat) + hidden_vec.astype(jnp.float32)
+    hidden_low, hidden_rate = gelu_parts(hidden_pre)
+    hidden_low = hidden_low.astype(jnp.bfloat16)
+    hidden_rate = hidden_rate.astype(jnp.bfloat16)
+    result = after_cross + product(hidden_low, final_mat) + final_vec.astype(jnp.float32)
+    layer_out = result.astype(jnp.bfloat16).reshape(page_count, page_len, width)
     second_norm, second_unit, second_std = norm_of(after_self, gain_two, shift_two)
     second_low = second_norm.astype(jnp.bfloat16)
     third_norm, third_unit, third_std = norm_of(after_cross, gain_three, shift_three)
@@ -1134,9 +1611,8 @@
     )
     tokens_grad = (self_grad_total + first_back).reshape(page_count, page_len, width)
     owned = spread(
-        mesh,
-        grad_gain_one,
-        grad_shift_one,
+        grad_gain_one[0],
+        grad_shift_one[0],
         grad_query_mat,
         grad_query_vec,
         grad_key_mat,
@@ -1144,8 +1620,8 @@
         grad_value_vec,
         grad_out_mat,
         grad_out_vec,
-        grad_gain_two,
-        grad_shift_two,
+        grad_gain_two[0],
+        grad_shift_two[0],
         grad_cquery_mat,
         grad_cquery_vec,
         grad_ckey_mat,
@@ -1153,8 +1629,8 @@
         grad_cvalue_vec,
         grad_cout_mat,
         grad_cout_vec,
-        grad_gain_three,
-        grad_shift_three,
+        grad_gain_three[0],
+        grad_shift_three[0],
         grad_hidden_mat,
         grad_hidden_vec,
         grad_final_mat,

time: 497 us -> 399 us (0.80)
  matrix products: 68 us -> 0 us
  other arithmetic: 13.1 us -> 0 us
  local copies, waits for them, and re-layouts: 25 us -> 16 us
  Pallas kernels: 380 us -> 374 us
    dot_general x20 -> x0, matrix products: 68 us -> none  [the longest x10 39.2 us: product_tn(): lax.dot_general(left, right, (((0,), (0,)), ((), ())), preferred_element_...]
    reduce_sum x12 -> x0, other arithmetic: 11 us -> none  [the longest x3 3.9 us: normalize(): centered = rows_in - jnp.mean(rows_in, axis=-1, keepdims=True)]
    pallas_call x3 -> x1, Pallas kernels: 200 us -> 193 us  [fused_backward(): pl.pallas_call(functools.partial(backward_kernel, bits, orders, plan, out...]
    unnamed x156 -> x39, local copies, waits for them, and re-layouts: 17.7 us -> 14.8 us
where the time goes in v4:
time: 399 us; the launch traced here: 392 us
  Pallas kernels  374 us (94%)
  local copies, waits for them, and re-layouts  16 us (4%)
    pallas_call x1, Pallas kernels, fused_backward(): pl.pallas_call(functools.partial(backward_kernel, bits, orders, plan, out...  193 us
    pallas_call x1, Pallas kernels, fused_forward(): pl.pallas_call(functools.partial(forward_kernel, bits, units, orders, pla...  180 us
    unnamed x39, local copies, waits for them, and re-layouts  14.8 us

profile of v4, /device:TPU:0, one launch (start us, length us, event | category | flops | bytes accessed | tf_op | source)
XLA Modules:
  0.0 392.0 jit_solution(16216015263755492864)
XLA Ops:
  2.0 180.1 %forward_layer.1 = (bf16[2,2,2,2,2,16,128]{6,5,4,3,2,1,0:T(8,128)(2,1)}, bf16[2,2,2,2,2,32,1024]{6,5,4,3,2,1,0:T(8,128)(2,1)}, bf16[2,2,2,2,2,32,1024]{6,5,4,3,2...) custom-call(bf16[512,1024]{1,0:T(8,128)(2,1)} %bitcast.36, ...), custom_call_target="tpu_custom_call" | custom-call | tf_op jit(solution)/shard_map/forward_layer/pallas_call | solution.py:686
  182.0 193.5 %backward_layer.1 = (f32[512,1024]{1,0:T(8,128)}, f32[588,1024]{1,0:T(8,128)}, f32[32,1024]{1,0:T(8,128)}, f32[32,1024]{1,0:T(8,128)}, f32[32,1024]{1,0:T(8,128)...) custom-call(bf16[512,1024]{1,0:T(8,128)(2,1)} %bitcast.40, ...), custom_call_target="tpu_custom_call" | custom-call | tf_op jit(solution)/shard_map/backward_layer/pallas_call | solution.py:1342
  375.5 0.0 copy-start.12
  375.5 0.0 copy-start.1
  375.5 5.7 %copy.56 = f32[1,588,1024]{2,0,1:T(1,128)} copy(f32[1,588,1024]{2,1,0:T(8,128)} %bitcast.38) | data formatting | bytes 4816896
  381.2 0.0 copy-start
  381.2 0.0 copy-done.12
  381.2 0.6 dynamic-slice_bitcast_fusion
  381.9 0.5 slice_bitcast_fusion
  382.4 0.0 copy-done.1
  382.4 1.0 copy.71
  383.3 0.0 copy-done
  383.3 0.0 copy-start.11
  383.3 0.0 copy-start.10
  383.3 0.0 copy-start.9
  383.4 0.0 copy-start.8
  383.4 0.0 copy-start.7
  383.4 0.0 copy-start.6
  383.4 0.0 copy-start.5
  383.4 0.0 copy-start.4
  383.4 1.3 copy.72
  384.7 0.0 copy-done.11
  384.7 0.0 copy-start.3
  384.7 0.0 copy-start.2
  384.7 0.7 copy.73
  385.4 0.0 copy-done.10
  385.4 0.7 copy.74
  386.0 0.0 copy-done.9
  386.0 0.7 copy.75
  386.7 0.0 copy-done.8
  386.7 0.7 copy.76
  387.4 0.0 copy-done.7
  387.4 0.7 copy.77
  388.0 0.0 copy-done.6
  388.0 0.7 copy.78
  388.7 0.0 copy-done.5
  388.7 0.7 copy.79
  389.3 0.0 copy-done.4
  389.3 0.7 copy.80
  390.0 0.0 copy-done.3
  390.0 0.8 copy.81
  390.8 0.0 copy-done.2
  390.8 0.8 copy.82
Async XLA Ops:
  375.5 5.7 %copy-start.12 = (f32[16,128]{1,0:T(8,128)S(1)}, f32[16,128]{1,0:T(8,128)}, u32[]{:S(2)}) copy-start(f32[16,128]{1,0:T(8,128)} %get-tuple-element.94) | copy-start | bytes 24580
  375.5 6.8 %copy-start.1 = (bf16[512,1024]{1,0:T(8,128)(2,1)S(1)}, bf16[512,1024]{1,0:T(8,128)(2,1)}, u32[]{:S(2)}) copy-start(bf16[512,1024]{1,0:T(8,128)(2,1)} %get-tuple-element.66) | copy-start | bytes 3145732
  381.2 2.1 copy-start
  383.3 1.4 copy-start.11
  383.3 2.0 copy-start.10
  383.3 2.7 copy-start.9
  383.4 3.4 copy-start.8
  383.4 4.0 %copy-start.7 = (f32[32,1024]{1,0:T(8,128)S(1)}, f32[32,1024]{1,0:T(8,128)}, u32[]{:S(2)}) copy-start(f32[32,1024]{1,0:T(8,128)} %get-tuple-element.186) | copy-start | bytes 393220
  383.4 4.7 %copy-start.6 = (f32[32,1024]{1,0:T(8,128)S(1)}, f32[32,1024]{1,0:T(8,128)}, u32[]{:S(2)}) copy-start(f32[32,1024]{1,0:T(8,128)} %get-tuple-element.188) | copy-start | bytes 393220
  383.4 5.3 %copy-start.5 = (f32[32,1024]{1,0:T(8,128)S(1)}, f32[32,1024]{1,0:T(8,128)}, u32[]{:S(2)}) copy-start(f32[32,1024]{1,0:T(8,128)} %get-tuple-element.189) | copy-start | bytes 393220
  383.4 5.9 %copy-start.4 = (f32[32,1024]{1,0:T(8,128)S(1)}, f32[32,1024]{1,0:T(8,128)}, u32[]{:S(2)}) copy-start(f32[32,1024]{1,0:T(8,128)} %get-tuple-element.191) | copy-start | bytes 393220
  384.7 5.3 %copy-start.3 = (f32[32,4096]{1,0:T(8,128)S(1)}, f32[32,4096]{1,0:T(8,128)}, u32[]{:S(2)}) copy-start(f32[32,4096]{1,0:T(8,128)} %get-tuple-element.195) | copy-start | bytes 1572868
  384.7 6.1 %copy-start.2 = (f32[128,1024]{1,0:T(8,128)S(1)}, f32[128,1024]{1,0:T(8,128)}, u32[]{:S(2)}) copy-start(f32[128,1024]{1,0:T(8,128)} %get-tuple-element.197) | copy-start | bytes 1572868
